TPU v7x, 128 devices: a whole 4x4x4 slice. The times are simulated.
128 devices in a mesh: src: 8 (over z, core), rcv: 16 (over y, x).
Axes of the slice: x: 4, y: 4, z: 4, core: 2. Of those that a mesh axis runs over, the one named last changes fastest.
Arguments:
- data: bfloat16 [2, 16384, 16384], P(None, 'src', 'rcv'), may hold values from -15 to 15
- observed: int32 [256, 256], P('src', 'rcv'), may hold values 0 or 1
- band_width: int32 [1], replicated, may hold values from 24 to 48
- left_factor: float32 [32, 8, 64, 256], P(None, 'src'), may hold values from -1.5 to 1.5
- right_factor: float32 [6, 16, 64, 256], P(None, 'rcv'), may hold values from -1.5 to 1.5
Outputs:
- left_out: float32 [32, 8, 64, 256], P(None, 'src')
- right_out: float32 [6, 16, 64, 256], P(None, 'rcv')
All inputs are finite; a program needn't handle non-finite values. No bound on the sum of `observed` on one device may be relied on, other than what follows from the above.
Results may differ from a plain program's by a relative error of at most 0.0044.
The roundings to bfloat16 on the way count: a program that leaves them out, or rounds other values in their place, can miss the bound.
Values may be sent and summed in bfloat16 or wider, within the bound.
No kernel may reach another device: no remote copies, remote signals or barrier semaphores. Data moves between devices by JAX's collectives and lax.ppermute only.
A program may use at most 128 MiB of HBM per device.

v0:
```python
import jax
import jax.numpy as jnp
from jax import lax
from jax.sharding import PartitionSpec as P

ITERS = 2


epsilon = 1e-06


def stacked(factor):
    half_width = factor.shape[1] // 2
    turned = jnp.concatenate([-factor[:, half_width:], factor[:, :half_width]], axis=1)
    return jnp.concatenate([factor, turned], axis=0)


def times_t(first, second):
    return lax.dot_general(
        first, second, (((1,), (1,)), ((), ())), preferred_element_type=jnp.float32
    )


def combine(products):
    count = products.shape[0] // 2
    half_width = products.shape[1] // 2
    upper_part = products[:count]
    lower_part = products[count:]
    return jnp.concatenate(
        [
            upper_part[:, :half_width] + lower_part[:, half_width:],
            upper_part[:, half_width:] - lower_part[:, :half_width],
        ],
        axis=1,
    )


def left_sums(own_rows, curvature):
    numerator, denominator = lax.psum(
        (jnp.sum(own_rows * own_rows), jnp.sum(curvature * curvature)), ("src", "rcv")
    )
    return numerator / (denominator + epsilon)


def right_sums(own_rows, curvature):
    numerator, denominator = lax.psum(
        (jnp.sum(own_rows * own_rows), jnp.sum(curvature * curvature)), ("src", "rcv")
    )
    return numerator / (denominator + epsilon)


def per_device(data, observed, band_width, left_factor, right_factor):
    src_index = lax.axis_index("src")
    rcv_index = lax.axis_index("rcv")
    src_count = lax.axis_size("src")
    rcv_count = lax.axis_size("rcv")
    src_blocks, rcv_blocks = observed.shape
    block_edge = data.shape[1] // src_blocks
    offset_slots = right_factor.shape[0]
    factor_width = left_factor.shape[3]
    per_peer = rcv_blocks // rcv_count
    half_slots = offset_slots // 2
    source_rows = src_index * src_blocks + jnp.arange(src_blocks, dtype=jnp.int32)
    destinations = jnp.arange(rcv_count, dtype=jnp.int32)
    group_ids = jnp.arange(per_peer, dtype=jnp.int32)
    wanted = (
        destinations[None, :, None] + source_rows[:, None, None]
    ) % rcv_count + rcv_count * group_ids[None, None, :]
    selector = (
        jnp.arange(rcv_blocks, dtype=jnp.int32)[None, None, None, :] == wanted[..., None]
    ).astype(jnp.bfloat16)
    blocked = data.reshape(2, src_blocks, block_edge, rcv_blocks, block_edge)
    outgoing = jnp.einsum(
        "ripjq,idgj->drigpq", blocked, selector, preferred_element_type=jnp.float32
    ).astype(jnp.bfloat16)
    out_flags = jnp.einsum(
        "ij,idgj->dig", observed.astype(jnp.bfloat16), selector, preferred_element_type=jnp.float32
    )
    out_flags = out_flags.astype(jnp.bfloat16).reshape(rcv_count, 1, src_blocks, per_peer, 1, 1)
    arrived, arrived_flags = (
        lax.all_to_all(outgoing, "rcv", split_axis=0, concat_axis=0, tiled=True),
        lax.all_to_all(out_flags, "rcv", split_axis=0, concat_axis=0, tiled=True),
    )
    slot_ids = jnp.arange(offset_slots, dtype=jnp.int32)
    source_key = (
        slot_ids[None, :] - half_slots + (rcv_index + source_rows[:, None]) // rcv_count
    ) % (rcv_count * per_peer)
    source_keys = jnp.arange(rcv_count, dtype=jnp.int32)[:, None] * per_peer + group_ids[None, :]
    chooser = (source_keys[None, None, :, :] == source_key[:, :, None, None]).astype(jnp.bfloat16)
    sheared = jnp.einsum(
        "brigpq,itbg->riptq", arrived, chooser, preferred_element_type=jnp.float32
    ).astype(jnp.bfloat16)
    shear_flags = jnp.einsum(
        "big,itbg->it",
        arrived_flags.reshape(rcv_count, src_blocks, per_peer),
        chooser,
        preferred_element_type=jnp.float32,
    ).astype(jnp.bfloat16)
    per_dest = src_blocks // src_count
    offsets = rcv_count * slot_ids + rcv_index - offset_slots * rcv_count // 2
    shifts = offsets // 2
    targets = jnp.arange(src_count, dtype=jnp.int32)
    row_pick = (targets[:, None] - shifts[None, :]) % src_count
    selector_two = (
        jnp.arange(src_count, dtype=jnp.int32)[None, None, :] == row_pick[:, :, None]
    ).astype(jnp.bfloat16)
    split_rows = sheared.reshape(2, per_dest, src_count, block_edge, offset_slots, block_edge)
    outgoing_two = jnp.einsum(
        "ruvptq,etv->eruptq", split_rows, selector_two, preferred_element_type=jnp.float32
    ).astype(jnp.bfloat16)
    flags_two = jnp.einsum(
        "uvt,etv->eut",
        shear_flags.reshape(per_dest, src_count, offset_slots),
        selector_two,
        preferred_element_type=jnp.float32,
    )
    flags_two = flags_two.astype(jnp.bfloat16).reshape(src_count, 1, per_dest, 1, offset_slots, 1)
    arrived_two, arrived_flags_two = (
        lax.all_to_all(outgoing_two, "src", split_axis=0, concat_axis=0, tiled=True),
        lax.all_to_all(flags_two, "src", split_axis=0, concat_axis=0, tiled=True),
    )
    midpoint_ids = jnp.arange(src_blocks, dtype=jnp.int32)
    mid_key = (midpoint_ids[:, None] + (src_index - shifts[None, :]) // src_count) % src_blocks
    mid_keys = (
        jnp.arange(src_count, dtype=jnp.int32)[:, None] * per_dest
        + jnp.arange(per_dest, dtype=jnp.int32)[None, :]
    )
    chooser_two = (mid_keys[None, None, :, :] == mid_key[:, :, None, None]).astype(jnp.bfloat16)
    tile_rows = src_blocks * block_edge
    tile_cols = offset_slots * block_edge
    target = jnp.einsum(
        "aruptq,mtau->mprtq", arrived_two, chooser_two, preferred_element_type=jnp.float32
    )
    target = target.reshape(tile_rows, 2 * tile_cols)
    weight = jnp.einsum(
        "aut,mtau->mt",
        arrived_flags_two.reshape(src_count, per_dest, offset_slots),
        chooser_two,
        preferred_element_type=jnp.float32,
    )
    weight = weight * (jnp.abs(offsets) <= band_width[0]).astype(jnp.float32)[None, :]

    def masked(field):
        shaped = (
            field.reshape(src_blocks, block_edge, 2, offset_slots, block_edge)
            * weight[:, None, None, :, None]
        )
        return shaped.reshape(tile_rows, 2 * tile_cols)

    left_full = left_factor.reshape(tile_rows, factor_width)
    right_full = right_factor.reshape(tile_cols, factor_width)
    left_b = left_full.astype(jnp.bfloat16)
    right_b = right_full.astype(jnp.bfloat16)
    residual = masked(times_t(left_b, stacked(right_b)) - target)
    left_count = tile_rows // rcv_count
    right_count = tile_cols // src_count
    for iteration in range(ITERS):
        residual_b = residual.astype(jnp.bfloat16)
        stacked_right = stacked(right_b)
        gradient = lax.psum(
            jnp.dot(residual_b, stacked_right, preferred_element_type=jnp.float32), "rcv"
        )
        own_rows = lax.dynamic_slice_in_dim(gradient, rcv_index * left_count, left_count, 0)
        curvature = masked(times_t(gradient.astype(jnp.bfloat16), stacked_right))
        step_size = left_sums(own_rows, curvature)
        left_full = left_full - step_size * gradient
        left_b = left_full.astype(jnp.bfloat16)
        residual = residual - step_size * curvature
        residual_b = residual.astype(jnp.bfloat16)
        products = lax.dot_general(
            residual_b, left_b, (((0,), (0,)), ((), ())), preferred_element_type=jnp.float32
        )
        gradient_r = lax.psum(combine(products), "src")
        own_rows = lax.dynamic_slice_in_dim(gradient_r, src_index * right_count, right_count, 0)
        curvature = masked(times_t(left_b, stacked(gradient_r.astype(jnp.bfloat16))))
        step_size = right_sums(own_rows, curvature)
        right_full = right_full - step_size * gradient_r
        right_b = right_full.astype(jnp.bfloat16)
        residual = residual - step_size * curvature
    return (left_full.reshape(left_factor.shape), right_full.reshape(right_factor.shape))


def solution(mesh):
    return jax.shard_map(
        per_device,
        mesh=mesh,
        in_specs=(
            P(None, "src", "rcv"),
            P("src", "rcv"),
            P(),
            P(None, "src", None, None),
            P(None, "rcv", None, None),
        ),
        out_specs=(P(None, "src", None, None), P(None, "rcv", None, None)),
        check_vma=False,
    )
```

profile of v0, /device:TPU:1, one launch (start us, length us, event | category | flops | bytes accessed | tf_op | source)
XLA Modules:
  0.0 1015.3 jit_solution(1019897243227720866)
XLA Ops:
  9.0 7.6 all-to-all-start.2
  16.6 22.1 %reshape.360 = bf16[2,32,64,16,64]{4,3,2,1,0:T(8,128)(2,1)} reshape(bf16[2,2048,1024]{2,1,0:T(8,128)(2,1)} %param.5) | data formatting | bytes 16777216 | tf_op jit(solution)/shard_map/reshape | solution.py:72
  38.7 11.5 %convert_bitcast_fusion = bf16[16,2,32,1,64,64]{5,0,4,1,2,3:T(8,128)(2,1)} fusion(bf16[2,32,64,16,64]{4,3,2,1,0:T(8,128)(2,1)} %reshape.360, s32[32,16]{1,0:T(8,128)S(1)} %add_select_fusion), kind=kOutput, calls=%fused_computation.5 | convolution fusion | flops 138420224 | bytes 16779264 | tf_op jit(solution)/shard_map/ripjq,idgj->drigpq/dot_general | solution.py:73
  50.2 15.1 %copy.128 = bf16[16,2,32,1,64,64]{5,4,1,2,3,0:T(8,128)(2,1)} copy(bf16[16,2,32,1,64,64]{5,0,4,1,2,3:T(8,128)(2,1)} %convert_bitcast_fusion) | data formatting | bytes 16777216 | tf_op jit(solution)/shard_map/convert_element_type | solution.py:75
  65.3 19.6 %reshape.382 = bf16[16,2,131072]{2,1,0:T(2,128)(2,1)} reshape(bf16[16,1,32,2,64,64]{5,4,3,2,1,0:T(8,128)(2,1)} %bitcast.116) | data formatting | bytes 16777216
  85.0 6.7 all-to-all-start
  93.3 120.0 %all-to-all-done = bf16[16,2,131072]{2,1,0:T(2,128)(2,1)} async-done(((bf16[16,2,131072]{2,1,0:T(2,128)(2,1)}), bf16[16,2,131072]{2,1,0:T(2,128)(2,1)}, u32[]{:S(2)}, u32[]{:S(2)}) %all-to-all-start) | async-done | bytes 8388640 | tf_op jit(solution)/shard_map/all_to_all | solution.py:81
  213.3 7.7 all-to-all-start.3
  221.0 19.4 %reshape.383 = bf16[16,1,32,2,64,64]{5,4,3,2,1,0:T(8,128)(2,1)} reshape(bf16[16,2,131072]{2,1,0:T(2,128)(2,1)} %all-to-all-done) | data formatting | bytes 16777216
  240.4 18.5 %fusion.7 = bf16[32,6,2,64,64]{4,1,3,2,0:T(8,128)(2,1)} fusion(bf16[16,2,32,1,64,64]{5,4,1,2,3,0:T(8,128)(2,1)} %bitcast.115, s32[32,6]{1,0:T(8,128)S(1)} %copy.63), kind=kOutput, calls=%fused_computation.6 | convolution fusion | flops 51907584 | bytes 11535104 | tf_op jit(solution)/shard_map/brigpq,itbg->riptq/dot_general | solution.py:90
  259.0 10.6 %convert_bitcast_fusion.1 = bf16[8,2,4,64,6,64]{5,0,2,3,1,4:T(8,128)(2,1)S(1)} fusion(bf16[2,4,8,64,6,64]{5,4,3,0,2,1:T(8,128)(2,1)} %bitcast.117, s32[8,6]{0,1:T(8,128)S(1)} %add_select_fusion.3), kind=kOutput, calls=%fused_computation.20 | convolution fusion | flops 26739072 | bytes 6291648 | tf_op jit(solution)/shard_map/ruvptq,etv->eruptq/dot_general | solution.py:108
  269.5 6.3 copy.129
  275.8 9.1 reshape.384
  284.9 4.8 all-to-all-start.1
  292.2 6.2 mul.154
  298.5 12.2 %mul.155 = f32[2048,768]{0,1:T(8,128)} reshape(f32[32,64,2,6,64]{1,0,4,3,2:T(8,128)} %mul.154) | data formatting | bytes 12582912 | tf_op jit(solution)/shard_map/mul | solution.py:145
  310.6 16.7 %all-to-all-done.1 = bf16[8,2,98304]{2,1,0:T(2,128)(2,1)} async-done(((bf16[8,2,98304]{2,1,0:T(2,128)(2,1)}), bf16[8,2,98304]{2,1,0:T(2,128)(2,1)}, u32[]{:S(2)}, u32[]{:S(2)}) %all-to-all-start.1) | async-done | bytes 3145760 | tf_op jit(solution)/shard_map/all_to_all | solution.py:119
  327.4 8.8 reshape.385
  336.2 11.2 %fusion.15 = f32[32,64,2,6,64]{4,0,1,2,3:T(8,128)} fusion(bf16[8,2,4,64,6,64]{5,2,3,1,4,0:T(4,128)(2,1)} %bitcast.118, s32[32,6]{0,1:T(8,128)S(1)} %add_select_fusion.4, s32[8,4]{0,1:T(4,128)S(1)} %iota_add_fusion), kind=kOutput, calls=%fused_computation.21 | convolution fusion | flops 100669440 | bytes 9438080 | tf_op jit(solution)/shard_map/aruptq,mtau->mprtq/dot_general | solution.py:131
  347.4 14.2 %copy.70 = f32[32,64,2,6,64]{1,0,4,3,2:T(8,128)} copy(f32[32,64,2,6,64]{4,0,1,2,3:T(8,128)} %fusion.15) | data formatting | bytes 12582912 | tf_op jit(solution)/shard_map/aruptq,mtau->mprtq/transpose | solution.py:131
  361.5 11.8 %reshape.363 = f32[2048,768]{0,1:T(8,128)} reshape(f32[32,64,2,6,64]{1,0,4,3,2:T(8,128)} %copy.70) | data formatting | bytes 12582912 | tf_op jit(solution)/shard_map/reshape | solution.py:134
  373.3 5.6 fusion.10
  379.0 2.7 copy-done
  381.6 2.4 fusion.26
  384.1 87.7 %all-reduce.9.cloned.1.call-done = f32[2048,256]{1,0:T(8,128)} async-done(((f32[2048,256]{1,0:T(8,128)}), f32[2048,256]{1,0:T(8,128)}) %all-reduce.9.cloned.1.call-update) | async-done | bytes 2097168 | tf_op jit(solution)/shard_map/psum | solution.py:160
  471.7 8.6 multiply_reduce_fusion.3
  480.9 65.8 %all-reduce.3 = (f32[]{:T(128)}, f32[]{:T(128)}) all-reduce(f32[]{:T(128)} %multiply_reduce_fusion.7, f32[]{:T(128)} %get-tuple-element.32), channel_id=1, replica_groups=mesh['src'=8,'rcv'=16] {'src','rcv'}, use_global_device_ids=true, to_apply=%region_2.3 | all-reduce | flops 2 | bytes 16 | tf_op jit(solution)/shard_map/psum | solution.py:39
  548.0 1.9 fusion.31
  549.9 5.8 fusion.24
  556.8 54.9 %all-reduce.11.cloned.1.call-done = f32[384,256]{0,1:T(8,128)} async-done(((f32[384,256]{0,1:T(8,128)}), f32[384,256]{0,1:T(8,128)}) %all-reduce.11.cloned.1.call-update) | async-done | bytes 393232 | tf_op jit(solution)/shard_map/psum | solution.py:173
  611.7 1.0 convert_element_type.113
  612.8 7.1 multiply_reduce_fusion.2
  620.6 67.1 %all-reduce.2 = (f32[]{:T(128)}, f32[]{:T(128)}) all-reduce(f32[]{:T(128)} %multiply_reduce_fusion.6, f32[]{:T(128)} %get-tuple-element.34), channel_id=1, replica_groups=mesh['src'=8,'rcv'=16] {'src','rcv'}, use_global_device_ids=true, to_apply=%region_7.8 | all-reduce | flops 2 | bytes 16 | tf_op jit(solution)/shard_map/psum | solution.py:46
  689.8 8.6 multiply_subtract_fusion
  698.4 2.7 copy-done.1
  701.0 3.4 fusion.22
  704.5 85.6 %all-reduce.13.cloned.1.call-done = f32[2048,256]{1,0:T(8,128)} async-done(((f32[2048,256]{1,0:T(8,128)}), f32[2048,256]{1,0:T(8,128)}) %all-reduce.13.cloned.1.call-update) | async-done | bytes 2097168 | tf_op jit(solution)/shard_map/psum | solution.py:160
  790.2 7.8 multiply_reduce_fusion.1
  798.0 1.5 multiply_reduce_fusion.5
  799.5 65.8 %all-reduce.1 = (f32[]{:T(128)}, f32[]{:T(128)}) all-reduce(f32[]{:T(128)} %multiply_reduce_fusion.5, f32[]{:T(128)} %get-tuple-element.36), channel_id=1, replica_groups=mesh['src'=8,'rcv'=16] {'src','rcv'}, use_global_device_ids=true, to_apply=%region_12.13 | all-reduce | flops 2 | bytes 16 | tf_op jit(solution)/shard_map/psum | solution.py:39
  866.7 2.8 multiply_subtract_fusion.3
  869.5 1.8 copy-done.4
  871.3 4.1 fusion.20
  876.3 55.2 %all-reduce.15.cloned.1.call-done = f32[384,256]{0,1:T(8,128)} async-done(((f32[384,256]{0,1:T(8,128)}), f32[384,256]{0,1:T(8,128)}) %all-reduce.15.cloned.1.call-update) | async-done | bytes 393232 | tf_op jit(solution)/shard_map/psum | solution.py:173
  931.5 1.1 convert_element_type.119
  932.6 5.9 multiply_reduce_fusion
  939.2 67.1 %all-reduce = (f32[]{:T(128)}, f32[]{:T(128)}) all-reduce(f32[]{:T(128)} %multiply_reduce_fusion.4, f32[]{:T(128)} %multiply_reduce_fusion), channel_id=1, replica_groups=mesh['src'=8,'rcv'=16] {'src','rcv'}, use_global_device_ids=true, to_apply=%region_17.18 | all-reduce | flops 2 | bytes 16 | tf_op jit(solution)/shard_map/psum | solution.py:46
  1007.6 0.9 copy.78
  (78 shorter events, 10.3 us)
Async XLA Ops:
  9.0 76.0 %all-to-all-start.2 = ((bf16[16,1,32,1,1,1]{2,5,4,3,1,0:T(2,128)(2,1)}), bf16[16,1,32,1,1,1]{2,5,4,3,1,0:T(2,128)(2,1)S(1)}, u32[]{:S(2)}, u32[]{:S(2)}) async-start(bf16[16,1,32,1,1,1]{2,5,4,3,1,0:T(2,128)(2,1)} %copy.71), calls=%async_computation.2 | async-start | bytes 16384 | tf_op jit(solution)/shard_map/all_to_all | solution.py:82
  85.0 128.3 %all-to-all-start = ((bf16[16,2,131072]{2,1,0:T(2,128)(2,1)}), bf16[16,2,131072]{2,1,0:T(2,128)(2,1)}, u32[]{:S(2)}, u32[]{:S(2)}) async-start(bf16[16,2,131072]{2,1,0:T(2,128)(2,1)} %reshape.382), calls=%async_computation | async-start | bytes 16777216 | tf_op jit(solution)/shard_map/all_to_all | solution.py:81
  213.3 71.6 %all-to-all-start.3 = ((bf16[8,1,4,1,6,1]{4,2,5,3,1,0:T(4,128)(2,1)}), bf16[8,1,4,1,6,1]{4,2,5,3,1,0:T(4,128)(2,1)S(1)}, u32[]{:S(2)}, u32[]{:S(2)}) async-start(bf16[8,1,4,1,6,1]{4,2,5,3,1,0:T(4,128)(2,1)} %copy.72), calls=%async_computation.3 | async-start | bytes 16384 | tf_op jit(solution)/shard_map/all_to_all | solution.py:120
  275.8 15.2 %copy-start.12 = (f32[6,1,64,256]{3,2,1,0:T(8,128)S(1)}, f32[6,1,64,256]{3,2,1,0:T(8,128)}, u32[]{:S(2)}) copy-start(f32[6,1,64,256]{3,2,1,0:T(8,128)} %param.9) | copy-start | bytes 1179652
  275.8 15.2 %copy-start.6 = (f32[32,1,64,256]{3,2,1,0:T(8,128)S(1)}, f32[32,1,64,256]{3,2,1,0:T(8,128)}, u32[]{:S(2)}) copy-start(f32[32,1,64,256]{3,2,1,0:T(8,128)} %param.8) | copy-start | bytes 6291460
  284.9 42.5 %all-to-all-start.1 = ((bf16[8,2,98304]{2,1,0:T(2,128)(2,1)}), bf16[8,2,98304]{2,1,0:T(2,128)(2,1)}, u32[]{:S(2)}, u32[]{:S(2)}) async-start(bf16[8,2,98304]{2,1,0:T(2,128)(2,1)} %reshape.384), calls=%async_computation.1 | async-start | bytes 6291456 | tf_op jit(solution)/shard_map/all_to_all | solution.py:119
  289.7 182.0 %all-reduce.9.cloned.1.call-start = ((), (), s32[]{:S(2)}) async-start(), calls=%async_computation.4 | async-start | bytes 4194304 | tf_op jit(solution)/shard_map/psum | solution.py:160
  379.0 2.7 copy-start
  384.0 227.7 %all-reduce.11.cloned.1.call-start = ((), (), s32[]{:S(2)}) async-start(), calls=%async_computation.5 | async-start | bytes 786432 | tf_op jit(solution)/shard_map/psum | solution.py:173
  471.7 8.6 copy-start.2
  549.9 6.7 copy-start.13
  556.5 233.6 %all-reduce.13.cloned.1.call-start = ((), (), s32[]{:S(2)}) async-start(), calls=%async_computation.6 | async-start | bytes 4194304 | tf_op jit(solution)/shard_map/psum | solution.py:160
  556.8 132.2 %copy-start.8 = (f32[384,256]{0,1:T(8,128)}, f32[384,256]{0,1:T(8,128)S(1)}, u32[]{:S(2)}) copy-start(f32[384,256]{0,1:T(8,128)S(1)} %copy.75) | copy-start | bytes 1179652
  612.8 7.1 copy-start.7
  689.0 0.7 copy-start.10
  698.4 2.7 copy-start.1
  704.5 162.2 %copy-start.3 = (f32[2048,256]{1,0:T(8,128)S(1)}, f32[2048,256]{1,0:T(8,128)}, u32[]{:S(2)}) copy-start(f32[2048,256]{1,0:T(8,128)} %all-reduce.9.cloned.1.call-done) | copy-start | bytes 6291460
  704.5 227.0 %all-reduce.15.cloned.1.call-start = ((), (), s32[]{:S(2)}) async-start(), calls=%async_computation.7 | async-start | bytes 786432 | tf_op jit(solution)/shard_map/psum | solution.py:173
  866.6 4.6 copy-start.4
  869.5 6.0 copy-start.5
  875.4 132.1 %copy-start.9 = (f32[384,256]{0,1:T(8,128)S(1)}, f32[384,256]{0,1:T(8,128)}, u32[]{:S(2)}) copy-start(f32[384,256]{0,1:T(8,128)} %copy-done.8) | copy-start | bytes 1179652
  931.5 7.0 copy-start.11
Sparse Core Ops, SparseCore 0:
  384.1 87.5 all-reduce.8
  556.7 54.9 all-reduce.10
  704.6 85.5 all-reduce.12
  876.4 54.9 all-reduce.14
where the time goes:
time: 1020 us
  waiting for transfers between devices  420 us (41%)
  blocking collectives  266 us (26%)
  local copies, waits for them, and re-layouts  155 us (15%)
  matrix products  103 us (10%)
  starting transfers between devices  26.9 us (3%)
  other arithmetic  24.4 us (2%)
  between operations  20.2 us (2%)
    psum x2, waiting for transfers between devices, per_device(): lax.psum(jnp.dot(residual_b, stacked_right, preferred_element_type=jnp.fl...  173 us
    psum x2, blocking collectives, right_sums(): lax.psum((jnp.sum(own_rows * own_rows), jnp.sum(curvature * curvature)),...  134 us
    psum x2, blocking collectives, left_sums(): lax.psum((jnp.sum(own_rows * own_rows), jnp.sum(curvature * curvature)),...  132 us
    all_to_all x1, waiting for transfers between devices, per_device(): lax.all_to_all(outgoing, 'rcv', split_axis=0, concat_axis=0, tiled=True)  120 us
    psum x2, waiting for transfers between devices, per_device(): gradient_r = lax.psum(combine(products), 'src')  110 us
    unnamed x34, local copies, waits for them, and re-layouts  64.3 us
    dot_general x5, matrix products, times_t(): lax.dot_general(first, second, (((1,), (1,)), ((), ())), preferred_elemen...  35 us
    reshape x1, local copies, waits for them, and re-layouts, per_device(): blocked = data.reshape(2, src_blocks, block_edge, rcv_blocks, block_edge)  22.1 us
  transfers between devices with their start and end apart: 8, of which 6 were waited for; matrix products, arithmetic and copies ran while one was open for 15% of the time, Pallas kernels for 0%

commit v1 on v0

v1 whole, which is shorter than its diff:
```python
import jax
import jax.numpy as jnp
from jax import lax
from jax.experimental import pallas as pl
from jax.experimental.pallas import tpu as pltpu
from jax.sharding import PartitionSpec as P

ITERS = 2
EPSILON = 1e-06
ABSENT = 1024.0
LIMIT = 512.0
VMEM = 56 * 1024 * 1024
CHUNKS = 4
f32 = jnp.float32
bf16 = jnp.bfloat16


def params():
    return pltpu.CompilerParams(vmem_limit_bytes=VMEM)


def whole(shape, **kw):
    return pl.BlockSpec(shape, lambda *_: (0,) * len(shape), **kw)


def nt(a, b):
    return lax.dot_general(a, b, (((1,), (1,)), ((), ())), preferred_element_type=f32)


def nn(a, b):
    return lax.dot_general(a, b, (((1,), (0,)), ((), ())), preferred_element_type=f32)


def tn(a, b):
    return lax.dot_general(a, b, (((0,), (0,)), ((), ())), preferred_element_type=f32)


def store_stacked(factor, out_ref, edge):
    half = factor.shape[1] // 2
    rounded = factor.astype(bf16)
    turned = jnp.concatenate([-rounded[:, half:], rounded[:, :half]], axis=1)
    for t in range(factor.shape[0] // edge):
        rows = slice(t * edge, (t + 1) * edge)
        out_ref[2 * t * edge : (2 * t + 1) * edge, :] = rounded[rows]
        out_ref[(2 * t + 1) * edge : (2 * t + 2) * edge, :] = turned[rows]


def step_of(sums):
    lane = lax.broadcasted_iota(jnp.int32, sums.shape, 1)
    numerator = jnp.sum(jnp.where(lane == 0, sums, 0.0), keepdims=True)
    denominator = jnp.sum(jnp.where(lane == 1, sums, 0.0), keepdims=True)
    return numerator / (denominator + EPSILON)


def weight_rows(w, edge):
    blocks, columns = w.shape
    return jnp.broadcast_to(w[:, None, :], (blocks, edge, columns)).reshape(
        blocks * edge, columns
    )


def pack_kernel(flags_ref, data_ref, out_ref, *, n_src, n_rcv):
    sigma = pl.program_id(0)
    _, groups, _, edge, width = data_ref.shape
    pairs = width // (2 * edge)
    low = lax.broadcasted_iota(jnp.int32, (edge, 2 * edge), 1) < edge
    for u in range(groups):
        for pair in range(pairs):
            re = data_ref[0, u, 0, :, pair * 2 * edge : (pair + 1) * 2 * edge]
            im = data_ref[1, u, 0, :, pair * 2 * edge : (pair + 1) * 2 * edge]
            first = jnp.concatenate([re[:, :edge], im[:, :edge]], axis=1)
            second = jnp.concatenate([re[:, edge:], im[:, edge:]], axis=1)
            for side, block in ((0, first), (1, second)):
                column = 2 * pair + side
                seen = flags_ref[sigma + n_src * u, column] != 0
                rcv = lax.rem(column - sigma - n_src * u + 4 * n_rcv, n_rcv)
                src = lax.rem(sigma + rcv // 2, n_src)
                out_ref[src * n_rcv + rcv, u] = jnp.where(
                    seen, block, jnp.full_like(block, ABSENT)
                )


def first_kernel(meta_ref, blocks_ref, left_ref, right_ref, res_ref, w_ref, grad_ref,
                 stack_ref, acc_ref, *, n_src, n_rcv, slots, edge, per_src, per_rcv):
    chunk = pl.program_id(0)

    @pl.when(chunk == 0)
    def _():
        store_stacked(right_ref[...], stack_ref, edge)

    src = meta_ref[0]
    rcv = meta_ref[1]
    band = meta_ref[2]
    total = n_src * per_src
    mids = left_ref.shape[0] // edge
    groups = per_src // n_src
    sigma = lax.rem(src - rcv // 2 + n_src, n_src)
    kappa = (sigma + rcv // 2 - src) // n_src
    stack = stack_ref[...]
    acc_ref[...] = nt(left_ref[...].astype(bf16), stack)
    for mm in range(mids):
        mid = chunk * mids + mm
        for t in range(slots):
            offset = n_rcv * t + rcv - n_rcv * slots // 2
            inside = jnp.abs(offset) <= band
            v = lax.rem(mid - t + slots // 2 - kappa + 2 * per_src, per_src)
            receiver = lax.rem(sigma + n_src * v + offset + total, total)
            index = ((v // groups) * n_rcv + receiver // per_rcv) * groups + lax.rem(v, groups)
            values = blocks_ref[index].astype(f32)
            keep = jnp.logical_and(values < LIMIT, inside)
            rows = slice(mm * edge, (mm + 1) * edge)
            cols = slice(t * 2 * edge, (t + 1) * 2 * edge)
            res_ref[rows, cols] = jnp.where(keep, acc_ref[rows, cols] - values, 0.0)
            w_ref[mm : mm + 1, cols] = jnp.where(keep[0:1, :], 1.0, 0.0)
    grad_ref[...] = nn(res_ref[...].astype(bf16), stack)


def spread_kernel(parts_ref, out_ref):
    total = jnp.sum(parts_ref[...], axis=0)
    out_ref[...] = jnp.broadcast_to(total[None], out_ref.shape)


def sums_out(numerator, denominator, shape):
    lane = lax.broadcasted_iota(jnp.int32, shape, 1)
    return jnp.where(lane == 0, numerator, jnp.where(lane == 1, denominator, 0.0))


def left_curve_kernel(grad_ref, right_ref, w_ref, out_ref, stack_ref, num_ref, den_ref,
                      *, edge, copies):
    chunk = pl.program_id(0)

    @pl.when(chunk == 0)
    def _():
        store_stacked(right_ref[...], stack_ref, edge)
        num_ref[...] = jnp.zeros_like(num_ref)
        den_ref[...] = jnp.zeros_like(den_ref)

    grad = grad_ref[...]
    curve = nt(grad.astype(bf16), stack_ref[...])
    squares = (curve * curve).reshape(-1, edge, curve.shape[1])
    den_ref[...] += jnp.sum(squares, axis=1) * w_ref[...]
    num_ref[...] += jnp.sum((grad * grad).reshape(-1, 8, grad.shape[1]), axis=0)

    @pl.when(chunk == pl.num_programs(0) - 1)
    def _():
        numerator = jnp.sum(num_ref[...], keepdims=True) * (1.0 / copies)
        denominator = jnp.sum(den_ref[...], keepdims=True)
        out_ref[...] = sums_out(numerator, denominator, out_ref.shape)


def left_update_kernel(sums_ref, grad_ref, left_ref, res_ref, right_ref, w_ref,
                       left_out_ref, *rest, edge, slots, keep_res):
    if keep_res:
        res_out_ref, out_ref, stack_ref, prod_ref = rest
    else:
        out_ref, stack_ref, prod_ref = rest
    chunk = pl.program_id(0)

    @pl.when(chunk == 0)
    def _():
        store_stacked(right_ref[...], stack_ref, edge)
        prod_ref[...] = jnp.zeros_like(prod_ref)

    step = step_of(sums_ref[...])
    grad = grad_ref[...]
    curve = nt(grad.astype(bf16), stack_ref[...])
    left = left_ref[...] - step * grad
    left_out_ref[...] = left
    residual = res_ref[...] - curve * weight_rows(step * w_ref[...], edge)
    if keep_res:
        res_out_ref[...] = residual
    prod_ref[...] += tn(left.astype(bf16), residual.astype(bf16))

    @pl.when(chunk == pl.num_programs(0) - 1)
    def _():
        products = prod_ref[...].T
        half = products.shape[1] // 2
        for t in range(slots):
            upper = products[2 * t * edge : (2 * t + 1) * edge]
            lower = products[(2 * t + 1) * edge : (2 * t + 2) * edge]
            out_ref[t * edge : (t + 1) * edge, :half] = upper[:, :half] + lower[:, half:]
            out_ref[t * edge : (t + 1) * edge, half:] = upper[:, half:] - lower[:, :half]


def right_curve_kernel(grad_ref, left_ref, w_ref, out_ref, stack_ref, den_ref, *, edge, copies):
    chunk = pl.program_id(0)

    @pl.when(chunk == 0)
    def _():
        store_stacked(grad_ref[...], stack_ref, edge)
        den_ref[...] = jnp.zeros_like(den_ref)

    curve = nt(left_ref[...].astype(bf16), stack_ref[...])
    squares = (curve * curve).reshape(-1, edge, curve.shape[1])
    den_ref[...] += jnp.sum(squares, axis=1) * w_ref[...]

    @pl.when(chunk == pl.num_programs(0) - 1)
    def _():
        grad = grad_ref[...]
        numerator = jnp.sum(grad * grad, keepdims=True) * (1.0 / copies)
        denominator = jnp.sum(den_ref[...], keepdims=True)
        out_ref[...] = sums_out(numerator, denominator, out_ref.shape)


def right_update_kernel(sums_ref, grad_r_ref, right_ref, left_ref, res_ref, w_ref,
                        right_out_ref, res_out_ref, grad_ref, stack_ref, turn_ref, *, edge):
    step = step_of(sums_ref[...])

    @pl.when(pl.program_id(0) == 0)
    def _():
        right = right_ref[...] - step * grad_r_ref[...]
        right_out_ref[...] = right
        store_stacked(right, stack_ref, edge)
        store_stacked(grad_r_ref[...], turn_ref, edge)

    curve = nt(left_ref[...].astype(bf16), turn_ref[...])
    residual = res_ref[...] - curve * weight_rows(step * w_ref[...], edge)
    res_out_ref[...] = residual
    grad_ref[...] = nn(residual.astype(bf16), stack_ref[...])


def right_last_kernel(sums_ref, grad_r_ref, right_ref, right_out_ref):
    right_out_ref[...] = right_ref[...] - step_of(sums_ref[...]) * grad_r_ref[...]


def per_device(data, observed, band_width, left_factor, right_factor):
    n_src = lax.axis_size("src")
    n_rcv = lax.axis_size("rcv")
    devices = n_src * n_rcv
    per_src, per_rcv = observed.shape
    edge = data.shape[1] // per_src
    groups = per_src // n_src
    slots = right_factor.shape[0]
    rank2 = left_factor.shape[3]
    rows = per_src * edge
    cols = slots * edge
    step_rows = rows // CHUNKS
    mids = per_src // CHUNKS
    both = ("src", "rcv")

    meta = jnp.concatenate([
        lax.axis_index("src").reshape(1).astype(jnp.int32),
        lax.axis_index("rcv").reshape(1).astype(jnp.int32),
        band_width.astype(jnp.int32),
    ])

    packed = pl.pallas_call(
        lambda *refs: pack_kernel(*refs, n_src=n_src, n_rcv=n_rcv),
        out_shape=jax.ShapeDtypeStruct((devices, groups, edge, 2 * edge), bf16),
        grid_spec=pltpu.PrefetchScalarGridSpec(
            num_scalar_prefetch=1,
            grid=(n_src,),
            in_specs=[
                pl.BlockSpec(
                    (2, groups, 1, edge, data.shape[2]), lambda s, _: (0, 0, s, 0, 0)
                )
            ],
            out_specs=whole((devices, groups, edge, 2 * edge)),
        ),
        compiler_params=params(),
        name="pack",
    )(observed, data.reshape(2, groups, n_src, edge, data.shape[2]))
    arrived = lax.all_to_all(packed, both, split_axis=0, concat_axis=0, tiled=True)
    arrived = arrived.reshape(devices * groups, edge, 2 * edge)

    left = left_factor.reshape(rows, rank2)
    right = right_factor.reshape(cols, rank2)

    def by_chunk(width):
        return pl.BlockSpec((step_rows, width), lambda c, *_: (c, 0))

    w_spec = pl.BlockSpec((mids, 2 * cols), lambda c, *_: (c, 0))
    res_shape = jax.ShapeDtypeStruct((rows, 2 * cols), f32)
    left_shape = jax.ShapeDtypeStruct((rows, rank2), f32)
    right_shape = jax.ShapeDtypeStruct((cols, rank2), f32)
    sums_shape = jax.ShapeDtypeStruct((devices, 128), f32)
    stack_scratch = pltpu.VMEM((2 * cols, rank2), bf16)

    res, weight, parts = pl.pallas_call(
        lambda *refs: first_kernel(
            *refs, n_src=n_src, n_rcv=n_rcv, slots=slots, edge=edge,
            per_src=per_src, per_rcv=per_rcv,
        ),
        out_shape=(res_shape, jax.ShapeDtypeStruct((per_src, 2 * cols), f32), left_shape),
        grid_spec=pltpu.PrefetchScalarGridSpec(
            num_scalar_prefetch=1,
            grid=(CHUNKS,),
            in_specs=[
                whole(arrived.shape, pipeline_mode=pl.Buffered(1)),
                by_chunk(rank2),
                whole((cols, rank2)),
            ],
            out_specs=(by_chunk(2 * cols), w_spec, by_chunk(rank2)),
            scratch_shapes=[stack_scratch, pltpu.VMEM((step_rows, 2 * cols), f32)],
        ),
        compiler_params=params(),
        name="first_gradient",
    )(meta, arrived, left, right)

    def spread(parts, axis, count):
        split = parts.reshape(count, parts.shape[0] // count, rank2)
        landed = lax.all_to_all(split, axis, split_axis=0, concat_axis=0, tiled=True)
        copies = pl.pallas_call(
            spread_kernel,
            out_shape=jax.ShapeDtypeStruct(split.shape, f32),
            compiler_params=params(),
            name="sum_parts",
        )(landed)
        full = lax.all_to_all(copies, axis, split_axis=0, concat_axis=0, tiled=True)
        return full.reshape(parts.shape)

    def shared(sums):
        return lax.all_to_all(sums, both, split_axis=0, concat_axis=0, tiled=True)

    for iteration in range(ITERS):
        last = iteration == ITERS - 1
        grad = spread(parts, "rcv", n_rcv)
        sums = pl.pallas_call(
            lambda *refs: left_curve_kernel(*refs, edge=edge, copies=n_rcv),
            out_shape=sums_shape,
            grid=(CHUNKS,),
            in_specs=[by_chunk(rank2), whole((cols, rank2)), w_spec],
            out_specs=whole((devices, 128)),
            scratch_shapes=[
                stack_scratch,
                pltpu.VMEM((8, rank2), f32),
                pltpu.VMEM((mids, 2 * cols), f32),
            ],
            compiler_params=params(),
            name="left_curve",
        )(grad, right, weight)
        sums = shared(sums)
        outs = pl.pallas_call(
            lambda *refs: left_update_kernel(*refs, edge=edge, slots=slots, keep_res=not last),
            out_shape=(left_shape,) + ((res_shape,) if not last else ()) + (right_shape,),
            grid=(CHUNKS,),
            in_specs=[
                whole((devices, 128)), by_chunk(rank2), by_chunk(rank2), by_chunk(2 * cols),
                whole((cols, rank2)), w_spec,
            ],
            out_specs=(by_chunk(rank2),) + ((by_chunk(2 * cols),) if not last else ())
            + (whole((cols, rank2)),),
            scratch_shapes=[stack_scratch, pltpu.VMEM((rank2, 2 * cols), f32)],
            compiler_params=params(),
            name="left_update",
        )(sums, grad, left, res, right, weight)
        if last:
            left, parts_r = outs
        else:
            left, res, parts_r = outs
        grad_r = spread(parts_r, "src", n_src)
        sums = pl.pallas_call(
            lambda *refs: right_curve_kernel(*refs, edge=edge, copies=n_src),
            out_shape=sums_shape,
            grid=(CHUNKS,),
            in_specs=[whole((cols, rank2)), by_chunk(rank2), w_spec],
            out_specs=whole((devices, 128)),
            scratch_shapes=[stack_scratch, pltpu.VMEM((mids, 2 * cols), f32)],
            compiler_params=params(),
            name="right_curve",
        )(grad_r, left, weight)
        sums = shared(sums)
        if last:
            right = pl.pallas_call(
                right_last_kernel,
                out_shape=right_shape,
                compiler_params=params(),
                name="right_last",
            )(sums, grad_r, right)
        else:
            right, res, parts = pl.pallas_call(
                lambda *refs: right_update_kernel(*refs, edge=edge),
                out_shape=(right_shape, res_shape, left_shape),
                grid=(CHUNKS,),
                in_specs=[
                    whole((devices, 128)), whole((cols, rank2)), whole((cols, rank2)),
                    by_chunk(rank2), by_chunk(2 * cols), w_spec,
                ],
                out_specs=(whole((cols, rank2)), by_chunk(2 * cols), by_chunk(rank2)),
                scratch_shapes=[stack_scratch, stack_scratch],
                compiler_params=params(),
                name="right_update",
            )(sums, grad_r, right, left, res, weight)
    return left.reshape(left_factor.shape), right.reshape(right_factor.shape)


def solution(mesh):
    return jax.shard_map(
        per_device,
        mesh=mesh,
        in_specs=(
            P(None, "src", "rcv"),
            P("src", "rcv"),
            P(),
            P(None, "src", None, None),
            P(None, "rcv", None, None),
        ),
        out_specs=(P(None, "src", None, None), P(None, "rcv", None, None)),
        check_vma=False,
    )
```

time: 1020 us -> 441 us (0.43)
  waiting for transfers between devices: 420 us -> 97.9 us
  local copies, waits for them, and re-layouts: 155 us -> 1.38 us
  matrix products: 103 us -> 0 us
  Pallas kernels: 0 us -> 77.2 us
  other arithmetic: 24.4 us -> 0.67 us
  between operations: 20.2 us -> 1.31 us
  blocking collectives: 266 us -> 249 us
  starting transfers between devices: 26.9 us -> 12 us
    psum x4 -> x0, waiting for transfers between devices: 283 us -> none  [the longest x2 173 us: per_device(): lax.psum(jnp.dot(residual_b, stacked_right, preferred_element_type=jnp.fl...]
    psum x4 -> x0, blocking collectives: 266 us -> none  [the longest x2 134 us: right_sums(): lax.psum((jnp.sum(own_rows * own_rows), jnp.sum(curvature * curvature)),...]
    all_to_all x0 -> x12, blocking collectives: none -> 249 us  [the longest x4 97.1 us: spread(): lax.all_to_all(split, axis, split_axis=0, concat_axis=0, tiled=True)]
    dot_general x15 -> x0, matrix products: 103 us -> none  [the longest x5 35 us: times_t(): lax.dot_general(first, second, (((1,), (1,)), ((), ())), preferred_elemen...]
    pallas_call x0 -> x14, Pallas kernels: none -> 77.2 us  [the longest x2 17 us: per_device(): pl.pallas_call(lambda *refs: left_update_kernel(*refs, edge=edge, slots=s...]
    unnamed x34 -> x1, local copies, waits for them, and re-layouts: 64.3 us -> 1.38 us
    all_to_all x4 -> x1, waiting for transfers between devices: 137 us -> 97.9 us  [per_device(): lax.all_to_all(packed, both, split_axis=0, concat_axis=0, tiled=True)]
    reshape x7 -> x0, local copies, waits for them, and re-layouts: 35.6 us -> none  [the longest x1 22.1 us: per_device(): blocked = data.reshape(2, src_blocks, block_edge, rcv_blocks, block_edge)]
  transfers between devices with their start and end apart: 8 -> 1, of which waited for: 6 -> 1; matrix products, arithmetic and copies ran while one was open for 15% -> 0% of each run, Pallas kernels for 0% -> 0%
where the time goes in v1:
time: 441 us; the launch traced here: 439 us
  blocking collectives  249 us (56%)
  waiting for transfers between devices  97.9 us (22%)
  Pallas kernels  77.2 us (18%)
  starting transfers between devices  12 us (3%)
    all_to_all x1, waiting for transfers between devices, per_device(): lax.all_to_all(packed, both, split_axis=0, concat_axis=0, tiled=True)  97.9 us
    all_to_all x4, blocking collectives, spread(): lax.all_to_all(split, axis, split_axis=0, concat_axis=0, tiled=True)  97.1 us
    all_to_all x4, blocking collectives, spread(): full = lax.all_to_all(copies, axis, split_axis=0, concat_axis=0, tiled=True)  90.2 us
    all_to_all x4, blocking collectives, shared(): return lax.all_to_all(sums, both, split_axis=0, concat_axis=0, tiled=True)  61.6 us
    pallas_call x2, Pallas kernels, per_device(): pl.pallas_call(lambda *refs: left_update_kernel(*refs, edge=edge, slots=s...  17 us
    pallas_call x1, Pallas kernels, per_device(): pl.pallas_call(lambda *refs: pack_kernel(*refs, n_src=n_src, n_rcv=n_rcv)...  12 us
    all_to_all x1, starting transfers between devices, per_device(): lax.all_to_all(packed, both, split_axis=0, concat_axis=0, tiled=True)  12 us
    pallas_call x4, Pallas kernels, spread(): pl.pallas_call(spread_kernel, out_shape=jax.ShapeDtypeStruct(split.shape,...  9.85 us
  transfers between devices with their start and end apart: 1, of which 1 were waited for; matrix products, arithmetic and copies ran while one was open for 0% of the time, Pallas kernels for 0%

profile of v1, /device:TPU:1, one launch (start us, length us, event | category | flops | bytes accessed | tf_op | source)
XLA Modules:
  0.0 439.2 jit_solution(5454906672718936186)
XLA Ops:
  0.6 1.4 copy.10.refs_0_
  2.0 12.0 %pack.1 = bf16[128,4,64,128]{3,2,1,0:T(8,128)(2,1)} custom-call(s32[32,16]{1,0:T(8,128)} %copy.10.refs_0_, bf16[2,4,8,64,1024]{4,3,2,1,0:T(8,128)(2,1)} %bitcast.40), custom_call_target="tpu_custom_call" | custom-call | tf_op jit(solution)/shard_map/pack/pallas_call | solution.py:247
  14.0 12.0 %all-to-all-start = ((bf16[128,4,64,128]{3,2,1,0:T(8,128)(2,1)}), bf16[128,4,64,128]{3,2,1,0:T(8,128)(2,1)}, u32[]{:S(2)}, u32[]{:S(2)}) async-start(bf16[128,4,64,128]{3,2,1,0:T(8,128)(2,1)} %pack.1), calls=%async_computation | async-start | bytes 16777216 | tf_op jit(solution)/shard_map/all_to_all | solution.py:263
  26.6 0.7 pad_add_fusion.refs_0_
  27.3 97.9 %all-to-all-done = bf16[128,4,64,128]{3,2,1,0:T(8,128)(2,1)} async-done(((bf16[128,4,64,128]{3,2,1,0:T(8,128)(2,1)}), bf16[128,4,64,128]{3,2,1,0:T(8,128)(2,1)}, u32[]{:S(2)}, u32[]{:S(2)}) %all-to-all-start) | async-done | bytes 8388640 | tf_op jit(solution)/shard_map/all_to_all | solution.py:263
  125.2 9.6 %first_gradient.1 = (f32[2048,768]{1,0:T(8,128)}, f32[32,768]{1,0:T(8,128)}, f32[2048,256]{1,0:T(8,128)}) custom-call(s32[3]{0:T(128)} %pad_add_fusion.refs_0_, bf16[512,64,128]{2,1,0:T(8,128)(2,1)} %bitcast.3.refs_1_, f32[2048,256]{1,0:T(8,128)} %bitcast.41, f32[384,256]{1,0:T(8,128)} %bitcast.43), custom_call_target="tpu_custom_call" | custom-call | tf_op jit(solution)/shard_map/first_gradient/pallas_call | solution.py:279
  134.8 39.0 %all_to_all.89.parts_ref = f32[16,128,256]{2,1,0:T(8,128)} all-to-all(f32[16,128,256]{2,1,0:T(8,128)} %bitcast.53), channel_id=1, replica_groups=mesh['src'=8,'rcv'=16] {'rcv'}, dimensions={0} | all-to-all | bytes 4194304 | tf_op jit(solution)/shard_map/all_to_all | solution.py:302
  173.8 3.1 sum_parts.4
  176.9 32.8 %all_to_all.90 = f32[16,128,256]{2,1,0:T(8,128)} all-to-all(f32[16,128,256]{2,1,0:T(8,128)} %sum_parts.4), channel_id=1, replica_groups=mesh['src'=8,'rcv'=16] {'rcv'}, dimensions={0} | all-to-all | bytes 4194304 | tf_op jit(solution)/shard_map/all_to_all | solution.py:309
  209.7 4.4 left_curve.2
  214.1 14.5 %all_to_all.91 = f32[128,1,128]{2,1,0:T(1,128)} all-to-all(f32[128,1,128]{2,1,0:T(1,128)} %bitcast.62), channel_id=1, replica_groups=mesh['src'=8,'rcv'=16] {'src','rcv'}, dimensions={0} | all-to-all | bytes 131072 | tf_op jit(solution)/shard_map/all_to_all | solution.py:313
  228.5 9.3 %left_update.2 = (f32[2048,256]{1,0:T(8,128)}, f32[2048,768]{1,0:T(8,128)}, f32[384,256]{1,0:T(8,128)}) custom-call(f32[128,128]{1,0:T(8,128)} %bitcast.57, f32[2048,256]{1,0:T(8,128)} %bitcast.37, f32[2048,256]{1,0:T(8,128)} %bitcast.42, f32[2048,768]{1,0:T(8,128)} %get-tuple-element.15.refs_3_, f32[384,256]{1,0:T(8,128)} %bitcast.45, ...), custom_call_target="tpu_custom_call" | custom-call | tf_op jit(solution)/shard_map/left_update/pallas_call | solution.py:333
  237.9 13.2 %all_to_all.92.parts_ref = f32[8,48,256]{2,1,0:T(8,128)} all-to-all(f32[8,48,256]{2,1,0:T(8,128)} %bitcast.55), channel_id=1, replica_groups=mesh['src'=8,'rcv'=16] {'src'}, dimensions={0} | all-to-all | bytes 786432 | tf_op jit(solution)/shard_map/all_to_all | solution.py:302
  251.0 1.8 sum_parts.5
  252.8 13.0 %all_to_all.93 = f32[8,48,256]{2,1,0:T(8,128)} all-to-all(f32[8,48,256]{2,1,0:T(8,128)} %sum_parts.5), channel_id=1, replica_groups=mesh['src'=8,'rcv'=16] {'src'}, dimensions={0} | all-to-all | bytes 786432 | tf_op jit(solution)/shard_map/all_to_all | solution.py:309
  265.8 4.4 %right_curve.2 = f32[128,128]{1,0:T(8,128)} custom-call(f32[384,256]{1,0:T(8,128)} %bitcast.47, f32[2048,256]{1,0:T(8,128)} %get-tuple-element.17.refs_1_.refs_3_.refs_2_, f32[32,768]{1,0:T(8,128)} %get-tuple-element.14.refs_2_.refs_5_), custom_call_target="tpu_custom_call" | custom-call | tf_op jit(solution)/shard_map/right_curve/pallas_call | solution.py:352
  270.2 15.0 %all_to_all.94 = f32[128,1,128]{2,1,0:T(1,128)} all-to-all(f32[128,1,128]{2,1,0:T(1,128)} %bitcast.63), channel_id=1, replica_groups=mesh['src'=8,'rcv'=16] {'src','rcv'}, dimensions={0} | all-to-all | bytes 131072 | tf_op jit(solution)/shard_map/all_to_all | solution.py:313
  285.3 9.1 %right_update.1 = (f32[384,256]{1,0:T(8,128)}, f32[2048,768]{1,0:T(8,128)}, f32[2048,256]{1,0:T(8,128)}) custom-call(f32[128,128]{1,0:T(8,128)} %bitcast.58, f32[384,256]{1,0:T(8,128)} %bitcast.48, f32[384,256]{1,0:T(8,128)} %bitcast.46, f32[2048,256]{1,0:T(8,128)} %get-tuple-element.17.refs_1_.refs_3_.refs_2_, f32[2048,768]{1,0:T(8,128)} %get-tuple-element.18.refs_4_, ...), custom_call_target="tpu_custom_call" | custom-call | tf_op jit(solution)/shard_map/right_update/pallas_call | solution.py:371
  294.3 31.8 %all_to_all.95.parts_ref = f32[16,128,256]{2,1,0:T(8,128)} all-to-all(f32[16,128,256]{2,1,0:T(8,128)} %bitcast.52), channel_id=1, replica_groups=mesh['src'=8,'rcv'=16] {'rcv'}, dimensions={0} | all-to-all | bytes 4194304 | tf_op jit(solution)/shard_map/all_to_all | solution.py:302
  326.1 3.1 sum_parts.6
  329.2 31.4 %all_to_all.96 = f32[16,128,256]{2,1,0:T(8,128)} all-to-all(f32[16,128,256]{2,1,0:T(8,128)} %sum_parts.6), channel_id=1, replica_groups=mesh['src'=8,'rcv'=16] {'rcv'}, dimensions={0} | all-to-all | bytes 4194304 | tf_op jit(solution)/shard_map/all_to_all | solution.py:309
  360.6 4.4 left_curve.3
  365.0 17.1 %all_to_all.97 = f32[128,1,128]{2,1,0:T(1,128)} all-to-all(f32[128,1,128]{2,1,0:T(1,128)} %bitcast.64), channel_id=1, replica_groups=mesh['src'=8,'rcv'=16] {'src','rcv'}, dimensions={0} | all-to-all | bytes 131072 | tf_op jit(solution)/shard_map/all_to_all | solution.py:313
  382.0 7.7 %left_update.3 = (f32[2048,256]{1,0:T(8,128)}, f32[384,256]{1,0:T(8,128)}) custom-call(f32[128,128]{1,0:T(8,128)} %bitcast.59, f32[2048,256]{1,0:T(8,128)} %bitcast.39, f32[2048,256]{1,0:T(8,128)} %get-tuple-element.17.refs_1_.refs_3_.refs_2_, f32[2048,768]{1,0:T(8,128)} %get-tuple-element.21.refs_3_, ...), custom_call_target="tpu_custom_call" | custom-call | tf_op jit(solution)/shard_map/left_update/pallas_call | solution.py:333
  389.7 13.2 %all_to_all.98.parts_ref = f32[8,48,256]{2,1,0:T(8,128)} all-to-all(f32[8,48,256]{2,1,0:T(8,128)} %bitcast.56), channel_id=1, replica_groups=mesh['src'=8,'rcv'=16] {'src'}, dimensions={0} | all-to-all | bytes 786432 | tf_op jit(solution)/shard_map/all_to_all | solution.py:302
  402.9 1.8 sum_parts.7
  404.6 13.0 %all_to_all.99 = f32[8,48,256]{2,1,0:T(8,128)} all-to-all(f32[8,48,256]{2,1,0:T(8,128)} %sum_parts.7), channel_id=1, replica_groups=mesh['src'=8,'rcv'=16] {'src'}, dimensions={0} | all-to-all | bytes 786432 | tf_op jit(solution)/shard_map/all_to_all | solution.py:309
  417.7 4.4 %right_curve.3 = f32[128,128]{1,0:T(8,128)} custom-call(f32[384,256]{1,0:T(8,128)} %bitcast.49, f32[2048,256]{1,0:T(8,128)} %get-tuple-element.22.refs_1_, f32[32,768]{1,0:T(8,128)} %get-tuple-element.14.refs_2_.refs_5_), custom_call_target="tpu_custom_call" | custom-call | tf_op jit(solution)/shard_map/right_curve/pallas_call | solution.py:352
  422.1 15.0 %all_to_all.100 = f32[128,1,128]{2,1,0:T(1,128)} all-to-all(f32[128,1,128]{2,1,0:T(1,128)} %bitcast.61), channel_id=1, replica_groups=mesh['src'=8,'rcv'=16] {'src','rcv'}, dimensions={0} | all-to-all | bytes 131072 | tf_op jit(solution)/shard_map/all_to_all | solution.py:313
  437.1 2.1 right_last.1
Async XLA Ops:
  14.0 111.1 %all-to-all-start = ((bf16[128,4,64,128]{3,2,1,0:T(8,128)(2,1)}), bf16[128,4,64,128]{3,2,1,0:T(8,128)(2,1)}, u32[]{:S(2)}, u32[]{:S(2)}) async-start(bf16[128,4,64,128]{3,2,1,0:T(8,128)(2,1)} %pack.1), calls=%async_computation | async-start | bytes 16777216 | tf_op jit(solution)/shard_map/all_to_all | solution.py:263

commit v2 on v1

--- a/solution.py
+++ b/solution.py
@@ -59,11 +59,30 @@
     )
 
 
-def pack_kernel(flags_ref, data_ref, out_ref, *, n_src, n_rcv):
+def pack_kernel(flags_ref, meta_ref, data_ref, out_ref, buf_ref, sem_ref, *, n_src, n_rcv):
     sigma = pl.program_id(0)
+    steps = pl.num_programs(0)
     _, groups, _, edge, width = data_ref.shape
     pairs = width // (2 * edge)
-    low = lax.broadcasted_iota(jnp.int32, (edge, 2 * edge), 1) < edge
+    n_pair = n_rcv // 2
+    place = lax.rem(sigma, 2)
+
+    def copies(step):
+        held = lax.rem(step, 2)
+        return [
+            pltpu.make_async_copy(
+                buf_ref.at[held, q],
+                out_ref.at[lax.rem(step + q, n_src) * n_pair + q],
+                sem_ref.at[held, q],
+            )
+            for q in range(n_pair)
+        ]
+
+    @pl.when(sigma >= 2)
+    def _():
+        for copy in copies(sigma - 2):
+            copy.wait()
+
     for u in range(groups):
         for pair in range(pairs):
             re = data_ref[0, u, 0, :, pair * 2 * edge : (pair + 1) * 2 * edge]
@@ -72,12 +91,25 @@
             second = jnp.concatenate([re[:, edge:], im[:, edge:]], axis=1)
             for side, block in ((0, first), (1, second)):
                 column = 2 * pair + side
-                seen = flags_ref[sigma + n_src * u, column] != 0
-                rcv = lax.rem(column - sigma - n_src * u + 4 * n_rcv, n_rcv)
-                src = lax.rem(sigma + rcv // 2, n_src)
-                out_ref[src * n_rcv + rcv, u] = jnp.where(
+                source = sigma + n_src * u
+                seen = flags_ref[source, column] != 0
+                diff = lax.rem(column - source + 4 * n_rcv, n_rcv)
+                q = diff // 2
+                turns = (source + diff) // n_rcv + (sigma + q) // n_src
+                beta = lax.rem(u + turns + meta_ref[1], 2)
+                near = lax.rem(sigma + diff, n_rcv) < n_rcv // 2
+                slot = 2 * lax.rem(diff, 2) + jnp.where(near, u // 2, u % 2)
+                buf_ref[place, q, beta * groups + slot] = jnp.where(
                     seen, block, jnp.full_like(block, ABSENT)
                 )
+
+    for copy in copies(sigma):
+        copy.start()
+
+    @pl.when(sigma == steps - 1)
+    def _():
+        for copy in copies(sigma - 1) + copies(sigma):
+            copy.wait()
 
 
 def first_kernel(meta_ref, blocks_ref, left_ref, right_ref, res_ref, w_ref, grad_ref,
@@ -89,29 +121,35 @@
         store_stacked(right_ref[...], stack_ref, edge)
 
     src = meta_ref[0]
-    rcv = meta_ref[1]
-    band = meta_ref[2]
+    pair = meta_ref[2]
+    beta = meta_ref[3]
+    band = meta_ref[4]
     total = n_src * per_src
-    mids = left_ref.shape[0] // edge
+    mids = left_ref.shape[0]
+    rank2 = left_ref.shape[3]
     groups = per_src // n_src
-    sigma = lax.rem(src - rcv // 2 + n_src, n_src)
-    kappa = (sigma + rcv // 2 - src) // n_src
+    half = n_rcv // 2
     stack = stack_ref[...]
-    acc_ref[...] = nt(left_ref[...].astype(bf16), stack)
+    acc_ref[...] = nt(left_ref[...].reshape(mids * edge, rank2).astype(bf16), stack)
     for mm in range(mids):
-        mid = chunk * mids + mm
-        for t in range(slots):
-            offset = n_rcv * t + rcv - n_rcv * slots // 2
+        mid = src + n_src * (2 * (chunk * mids + mm) + beta)
+        for column in range(2 * slots):
+            tau, t = column // slots, column % slots
+            residue = 2 * pair + tau
+            offset = n_rcv * t + residue - half * slots
             inside = jnp.abs(offset) <= band
-            v = lax.rem(mid - t + slots // 2 - kappa + 2 * per_src, per_src)
-            receiver = lax.rem(sigma + n_src * v + offset + total, total)
-            index = ((v // groups) * n_rcv + receiver // per_rcv) * groups + lax.rem(v, groups)
+            source = lax.rem(mid - pair - half * t + half * slots // 2 + total, total)
+            receiver = lax.rem(source + offset + total, total)
+            u = lax.rem(source, per_src) // n_src
+            near = lax.rem(lax.rem(source, n_src) + residue, n_rcv) < half
+            slot = 2 * tau + jnp.where(near, u // 2, lax.rem(u, 2))
+            index = ((source // per_src) * n_rcv + receiver // per_rcv) * groups + slot
             values = blocks_ref[index].astype(f32)
             keep = jnp.logical_and(values < LIMIT, inside)
             rows = slice(mm * edge, (mm + 1) * edge)
-            cols = slice(t * 2 * edge, (t + 1) * 2 * edge)
+            cols = slice(column * 2 * edge, (column + 1) * 2 * edge)
             res_ref[rows, cols] = jnp.where(keep, acc_ref[rows, cols] - values, 0.0)
-            w_ref[mm : mm + 1, cols] = jnp.where(keep[0:1, :], 1.0, 0.0)
+            w_ref[0, mm : mm + 1, cols] = jnp.where(keep[0:1, :], 1.0, 0.0)
     grad_ref[...] = nn(res_ref[...].astype(bf16), stack)
 
 
@@ -138,7 +176,7 @@
     grad = grad_ref[...]
     curve = nt(grad.astype(bf16), stack_ref[...])
     squares = (curve * curve).reshape(-1, edge, curve.shape[1])
-    den_ref[...] += jnp.sum(squares, axis=1) * w_ref[...]
+    den_ref[...] += jnp.sum(squares, axis=1) * w_ref[0]
     num_ref[...] += jnp.sum((grad * grad).reshape(-1, 8, grad.shape[1]), axis=0)
 
     @pl.when(chunk == pl.num_programs(0) - 1)
@@ -148,7 +186,7 @@
         out_ref[...] = sums_out(numerator, denominator, out_ref.shape)
 
 
-def left_update_kernel(sums_ref, grad_ref, left_ref, res_ref, right_ref, w_ref,
+def left_update_kernel(meta_ref, sums_ref, grad_ref, left_ref, res_ref, right_ref, w_ref,
                        left_out_ref, *rest, edge, slots, keep_res):
     if keep_res:
         res_out_ref, out_ref, stack_ref, prod_ref = rest
@@ -164,9 +202,9 @@
     step = step_of(sums_ref[...])
     grad = grad_ref[...]
     curve = nt(grad.astype(bf16), stack_ref[...])
-    left = left_ref[...] - step * grad
+    left = left_ref[...].reshape(grad.shape) - step * grad
     left_out_ref[...] = left
-    residual = res_ref[...] - curve * weight_rows(step * w_ref[...], edge)
+    residual = res_ref[...] - curve * weight_rows(step * w_ref[0], edge)
     if keep_res:
         res_out_ref[...] = residual
     prod_ref[...] += tn(left.astype(bf16), residual.astype(bf16))
@@ -192,7 +230,7 @@
 
     curve = nt(left_ref[...].astype(bf16), stack_ref[...])
     squares = (curve * curve).reshape(-1, edge, curve.shape[1])
-    den_ref[...] += jnp.sum(squares, axis=1) * w_ref[...]
+    den_ref[...] += jnp.sum(squares, axis=1) * w_ref[0]
 
     @pl.when(chunk == pl.num_programs(0) - 1)
     def _():
@@ -214,62 +252,73 @@
         store_stacked(grad_r_ref[...], turn_ref, edge)
 
     curve = nt(left_ref[...].astype(bf16), turn_ref[...])
-    residual = res_ref[...] - curve * weight_rows(step * w_ref[...], edge)
+    residual = res_ref[...] - curve * weight_rows(step * w_ref[0], edge)
     res_out_ref[...] = residual
     grad_ref[...] = nn(residual.astype(bf16), stack_ref[...])
 
 
-def right_last_kernel(sums_ref, grad_r_ref, right_ref, right_out_ref):
+def right_last_kernel(meta_ref, sums_ref, grad_r_ref, right_ref, right_out_ref):
     right_out_ref[...] = right_ref[...] - step_of(sums_ref[...]) * grad_r_ref[...]
 
 
 def per_device(data, observed, band_width, left_factor, right_factor):
     n_src = lax.axis_size("src")
-    n_rcv = lax.axis_size("rcv")
+    n_pair = lax.axis_size("pair")
+    n_rcv = 2 * n_pair
     devices = n_src * n_rcv
     per_src, per_rcv = observed.shape
     edge = data.shape[1] // per_src
     groups = per_src // n_src
     slots = right_factor.shape[0]
     rank2 = left_factor.shape[3]
-    rows = per_src * edge
-    cols = slots * edge
+    half_mids = per_src // 2
+    rows = half_mids * edge
+    own_cols = slots * edge
+    cols = 2 * own_cols
     step_rows = rows // CHUNKS
-    mids = per_src // CHUNKS
-    both = ("src", "rcv")
-
-    meta = jnp.concatenate([
-        lax.axis_index("src").reshape(1).astype(jnp.int32),
-        lax.axis_index("rcv").reshape(1).astype(jnp.int32),
-        band_width.astype(jnp.int32),
-    ])
+    mids = half_mids // CHUNKS
+    everyone = ("src", "pair", "beta")
+    swap = [(0, 1), (1, 0)]
+
+    src = lax.axis_index("src")
+    pair = lax.axis_index("pair")
+    beta = lax.axis_index("beta")
+    meta = jnp.stack([src, 2 * pair + beta, pair, beta, band_width[0]]).astype(jnp.int32)
 
     packed = pl.pallas_call(
         lambda *refs: pack_kernel(*refs, n_src=n_src, n_rcv=n_rcv),
-        out_shape=jax.ShapeDtypeStruct((devices, groups, edge, 2 * edge), bf16),
+        out_shape=jax.ShapeDtypeStruct((n_src * n_pair, 2 * groups, edge, 2 * edge), bf16),
         grid_spec=pltpu.PrefetchScalarGridSpec(
-            num_scalar_prefetch=1,
+            num_scalar_prefetch=2,
             grid=(n_src,),
             in_specs=[
-                pl.BlockSpec(
-                    (2, groups, 1, edge, data.shape[2]), lambda s, _: (0, 0, s, 0, 0)
-                )
+                pl.BlockSpec((2, groups, 1, edge, data.shape[2]), lambda s, *_: (0, 0, s, 0, 0))
             ],
-            out_specs=whole((devices, groups, edge, 2 * edge)),
+            out_specs=pl.BlockSpec(memory_space=pl.ANY),
+            scratch_shapes=[
+                pltpu.VMEM((2, n_pair, 2 * groups, edge, 2 * edge), bf16),
+                pltpu.SemaphoreType.DMA((2, n_pair)),
+            ],
         ),
         compiler_params=params(),
         name="pack",
-    )(observed, data.reshape(2, groups, n_src, edge, data.shape[2]))
-    arrived = lax.all_to_all(packed, both, split_axis=0, concat_axis=0, tiled=True)
+    )(observed, meta, data.reshape(2, groups, n_src, edge, data.shape[2]))
+    packed = packed.reshape(devices, groups, edge, 2 * edge)
+    arrived = lax.all_to_all(packed, everyone, split_axis=0, concat_axis=0, tiled=True)
     arrived = arrived.reshape(devices * groups, edge, 2 * edge)
 
-    left = left_factor.reshape(rows, rank2)
-    right = right_factor.reshape(cols, rank2)
+    left = left_factor.reshape(half_mids, 2, edge, rank2)
+    own_right = right_factor.reshape(own_cols, rank2)
+    other_right = lax.ppermute(own_right, "beta", swap)
+    right = jnp.concatenate([
+        jnp.where(beta == 0, own_right, other_right),
+        jnp.where(beta == 0, other_right, own_right),
+    ])
 
     def by_chunk(width):
         return pl.BlockSpec((step_rows, width), lambda c, *_: (c, 0))
 
-    w_spec = pl.BlockSpec((mids, 2 * cols), lambda c, *_: (c, 0))
+    w_spec = pl.BlockSpec((1, mids, 2 * cols), lambda c, *_: (c, 0, 0))
     res_shape = jax.ShapeDtypeStruct((rows, 2 * cols), f32)
     left_shape = jax.ShapeDtypeStruct((rows, rank2), f32)
     right_shape = jax.ShapeDtypeStruct((cols, rank2), f32)
@@ -281,13 +330,15 @@
             *refs, n_src=n_src, n_rcv=n_rcv, slots=slots, edge=edge,
             per_src=per_src, per_rcv=per_rcv,
         ),
-        out_shape=(res_shape, jax.ShapeDtypeStruct((per_src, 2 * cols), f32), left_shape),
+        out_shape=(
+            res_shape, jax.ShapeDtypeStruct((CHUNKS, mids, 2 * cols), f32), left_shape
+        ),
         grid_spec=pltpu.PrefetchScalarGridSpec(
             num_scalar_prefetch=1,
             grid=(CHUNKS,),
             in_specs=[
                 whole(arrived.shape, pipeline_mode=pl.Buffered(1)),
-                by_chunk(rank2),
+                pl.BlockSpec((mids, 1, edge, rank2), lambda c, meta_ref: (c, meta_ref[3], 0, 0)),
                 whole((cols, rank2)),
             ],
             out_specs=(by_chunk(2 * cols), w_spec, by_chunk(rank2)),
@@ -310,13 +361,13 @@
         return full.reshape(parts.shape)
 
     def shared(sums):
-        return lax.all_to_all(sums, both, split_axis=0, concat_axis=0, tiled=True)
+        return lax.all_to_all(sums, everyone, split_axis=0, concat_axis=0, tiled=True)
 
     for iteration in range(ITERS):
         last = iteration == ITERS - 1
-        grad = spread(parts, "rcv", n_rcv)
+        grad = spread(parts, "pair", n_pair)
         sums = pl.pallas_call(
-            lambda *refs: left_curve_kernel(*refs, edge=edge, copies=n_rcv),
+            lambda *refs: left_curve_kernel(*refs, edge=edge, copies=n_pair),
             out_shape=sums_shape,
             grid=(CHUNKS,),
             in_specs=[by_chunk(rank2), whole((cols, rank2)), w_spec],
@@ -330,27 +381,35 @@
             name="left_curve",
         )(grad, right, weight)
         sums = shared(sums)
+        own_left = (
+            pl.BlockSpec((mids, 1, edge, rank2), lambda c, meta_ref: (c, meta_ref[3], 0, 0))
+            if iteration == 0 else by_chunk(rank2)
+        )
         outs = pl.pallas_call(
-            lambda *refs: left_update_kernel(*refs, edge=edge, slots=slots, keep_res=not last),
+            lambda *refs: left_update_kernel(*refs, edge=edge, slots=2 * slots, keep_res=not last),
             out_shape=(left_shape,) + ((res_shape,) if not last else ()) + (right_shape,),
-            grid=(CHUNKS,),
-            in_specs=[
-                whole((devices, 128)), by_chunk(rank2), by_chunk(rank2), by_chunk(2 * cols),
-                whole((cols, rank2)), w_spec,
-            ],
-            out_specs=(by_chunk(rank2),) + ((by_chunk(2 * cols),) if not last else ())
-            + (whole((cols, rank2)),),
-            scratch_shapes=[stack_scratch, pltpu.VMEM((rank2, 2 * cols), f32)],
+            grid_spec=pltpu.PrefetchScalarGridSpec(
+                num_scalar_prefetch=1,
+                grid=(CHUNKS,),
+                in_specs=[
+                    whole((devices, 128)), by_chunk(rank2), own_left, by_chunk(2 * cols),
+                    whole((cols, rank2)), w_spec,
+                ],
+                out_specs=(by_chunk(rank2),) + ((by_chunk(2 * cols),) if not last else ())
+                + (whole((cols, rank2)),),
+                scratch_shapes=[stack_scratch, pltpu.VMEM((rank2, 2 * cols), f32)],
+            ),
             compiler_params=params(),
             name="left_update",
-        )(sums, grad, left, res, right, weight)
+        )(meta, sums, grad, left, res, right, weight)
         if last:
             left, parts_r = outs
+            other_left = lax.ppermute(left, "beta", swap)
         else:
             left, res, parts_r = outs
-        grad_r = spread(parts_r, "src", n_src)
+        grad_r = spread(parts_r, ("src", "beta"), 2 * n_src)
         sums = pl.pallas_call(
-            lambda *refs: right_curve_kernel(*refs, edge=edge, copies=n_src),
+            lambda *refs: right_curve_kernel(*refs, edge=edge, copies=2 * n_src),
             out_shape=sums_shape,
             grid=(CHUNKS,),
             in_specs=[whole((cols, rank2)), by_chunk(rank2), w_spec],
@@ -361,12 +420,19 @@
         )(grad_r, left, weight)
         sums = shared(sums)
         if last:
+            own = pl.BlockSpec((own_cols, rank2), lambda c, meta_ref: (meta_ref[3], 0))
             right = pl.pallas_call(
                 right_last_kernel,
-                out_shape=right_shape,
+                out_shape=jax.ShapeDtypeStruct((own_cols, rank2), f32),
+                grid_spec=pltpu.PrefetchScalarGridSpec(
+                    num_scalar_prefetch=1,
+                    grid=(1,),
+                    in_specs=[whole((devices, 128)), own, own],
+                    out_specs=whole((own_cols, rank2)),
+                ),
                 compiler_params=params(),
                 name="right_last",
-            )(sums, grad_r, right)
+            )(meta, sums, grad_r, right)
         else:
             right, res, parts = pl.pallas_call(
                 lambda *refs: right_update_kernel(*refs, edge=edge),
@@ -381,20 +447,29 @@
                 compiler_params=params(),
                 name="right_update",
             )(sums, grad_r, right, left, res, weight)
+    own_left = left.reshape(half_mids, 1, edge, rank2)
+    other_left = other_left.reshape(half_mids, 1, edge, rank2)
+    parity = lax.broadcasted_iota(jnp.int32, (half_mids, 2, edge, rank2), 1)
+    left = jnp.where(parity == beta, own_left, other_left)
     return left.reshape(left_factor.shape), right.reshape(right_factor.shape)
 
 
 def solution(mesh):
+    n_src, n_rcv = mesh.shape["src"], mesh.shape["rcv"]
+    split = jax.sharding.Mesh(
+        mesh.devices.reshape(n_src, n_rcv // 2, 2), ("src", "pair", "beta")
+    )
+    rcv = ("pair", "beta")
     return jax.shard_map(
         per_device,
-        mesh=mesh,
+        mesh=split,
         in_specs=(
-            P(None, "src", "rcv"),
-            P("src", "rcv"),
+            P(None, "src", rcv),
+            P("src", rcv),
             P(),
             P(None, "src", None, None),
-            P(None, "rcv", None, None),
+            P(None, rcv, None, None),
         ),
-        out_specs=(P(None, "src", None, None), P(None, "rcv", None, None)),
+        out_specs=(P(None, "src", None, None), P(None, rcv, None, None)),
         check_vma=False,
     )

time: 441 us -> 436 us (0.989)
  blocking collectives: 249 us -> 172 us
  waiting for transfers between devices: 97.9 us -> 143 us
  starting transfers between devices: 12 us -> 28.3 us
    ppermute x0 -> x2, waiting for transfers between devices: none -> 102 us  [the longest x1 102 us: per_device(): other_right = lax.ppermute(own_right, 'beta', swap)]
    all_to_all x1 -> x4, waiting for transfers between devices: 97.9 us -> 41.2 us  [the longest x1 22.6 us: spread(): full = lax.all_to_all(copies, axis, split_axis=0, concat_axis=0, tiled=True)]
    all_to_all x4 -> x3, blocking collectives: 90.2 us -> 55.6 us  [spread(): full = lax.all_to_all(copies, axis, split_axis=0, concat_axis=0, tiled=True)]
    all_to_all x4 -> x3, blocking collectives: 97.1 us -> 63.2 us  [spread(): lax.all_to_all(split, axis, split_axis=0, concat_axis=0, tiled=True)]
    all_to_all x1 -> x4, starting transfers between devices: 12 us -> 25.5 us  [the longest x1 12 us: per_device(): lax.all_to_all(packed, everyone, split_axis=0, concat_axis=0, tiled=True)]
    all_to_all x4 -> x3, blocking collectives: 61.6 us -> 53.5 us  [shared(): lax.all_to_all(sums, everyone, split_axis=0, concat_axis=0, tiled=True)]
  transfers between devices with their start and end apart: 1 -> 6, of which waited for: 1 -> 4; matrix products, arithmetic and copies ran while one was open for 0% -> 1% of each run, Pallas kernels for 0% -> 2%
where the time goes in v2:
time: 436 us; the launch traced here: 434 us
  blocking collectives  172 us (39%)
  waiting for transfers between devices  143 us (33%)
  Pallas kernels  81.1 us (19%)
  starting transfers between devices  28.3 us (6%)
  local copies, waits for them, and re-layouts  5.08 us (1%)
    ppermute x1, waiting for transfers between devices, per_device(): other_right = lax.ppermute(own_right, 'beta', swap)  102 us
    all_to_all x3, blocking collectives, spread(): lax.all_to_all(split, axis, split_axis=0, concat_axis=0, tiled=True)  63.2 us
    all_to_all x3, blocking collectives, spread(): full = lax.all_to_all(copies, axis, split_axis=0, concat_axis=0, tiled=True)  55.6 us
    all_to_all x3, blocking collectives, shared(): lax.all_to_all(sums, everyone, split_axis=0, concat_axis=0, tiled=True)  53.5 us
    all_to_all x1, waiting for transfers between devices, spread(): full = lax.all_to_all(copies, axis, split_axis=0, concat_axis=0, tiled=True)  22.6 us
    pallas_call x2, Pallas kernels, per_device(): pl.pallas_call(lambda *refs: left_update_kernel(*refs, edge=edge, slots=2...  17.5 us
    pallas_call x1, Pallas kernels, per_device(): pl.pallas_call(lambda *refs: pack_kernel(*refs, n_src=n_src, n_rcv=n_rcv)...  14.8 us
    all_to_all x1, starting transfers between devices, per_device(): lax.all_to_all(packed, everyone, split_axis=0, concat_axis=0, tiled=True)  12 us
  transfers between devices with their start and end apart: 6, of which 4 were waited for; matrix products, arithmetic and copies ran while one was open for 1% of the time, Pallas kernels for 2%

profile of v2, /device:TPU:1, one launch (start us, length us, event | category | flops | bytes accessed | tf_op | source)
XLA Modules:
  0.0 434.0 jit_solution(1362602742888681091)
XLA Ops:
  1.3 1.4 copy.11.refs_0_
  2.7 0.7 stack.19.refs_1_.refs_0_.meta_ref
  3.3 14.8 %pack.1 = bf16[64,8,64,128]{3,2,1,0:T(8,128)(2,1)} custom-call(s32[32,16]{1,0:T(8,128)} %copy.11.refs_0_, s32[5]{0:T(128)} %stack.19.refs_1_.refs_0_.meta_ref, bf16[2,4,8,64,1024]{4,3,2,1,0:T(8,128)(2,1)} %bitcast.49), custom_call_target="tpu_custom_call" | custom-call | tf_op jit(solution)/shard_map/pack/pallas_call | solution.py:288
  18.1 0.0 copy-start.3
  18.1 12.0 %all-to-all-start = ((bf16[128,4,64,128]{3,2,1,0:T(8,128)(2,1)}), bf16[128,4,64,128]{3,2,1,0:T(8,128)(2,1)}, u32[]{:S(2)}, u32[]{:S(2)}) async-start(bf16[128,4,64,128]{3,2,1,0:T(8,128)(2,1)} %bitcast.42), calls=%async_computation | async-start | bytes 16777216 | tf_op jit(solution)/shard_map/all_to_all | solution.py:307
  30.1 1.5 collective-permute-start
  31.6 102.0 %collective-permute-done = f32[384,256]{1,0:T(8,128)S(1)} collective-permute-done((f32[384,256]{1,0:T(8,128)S(1)}, f32[384,256]{1,0:T(8,128)S(1)}, u32[]{:S(2)}, u32[]{:S(2)}) %collective-permute-start) | collective-permute-done | bytes 393248 | tf_op jit(solution)/shard_map/ppermute | solution.py:312
  133.6 0.1 broadcast_select_fusion.2
  133.7 0.9 pad_maximum_fusion.refs_3_.refs_1_.refs_5_.refs_2_
  134.6 0.0 all-to-all-done
  134.6 10.6 %first_gradient.1 = (f32[1024,1536]{1,0:T(8,128)}, f32[4,4,1536]{2,1,0:T(4,128)}, f32[1024,256]{1,0:T(8,128)}) custom-call(s32[5]{0:T(128)} %stack.19.refs_1_.refs_0_.meta_ref, bf16[512,64,128]{2,1,0:T(8,128)(2,1)} %bitcast.6.refs_1_, f32[16,2,64,256]{3,2,1,0:T(8,128)} %bitcast.50, f32[768,256]{1,0:T(8,128)} %pad_maximum_fusion.refs_3_.refs_1_.refs_5_.refs_2_), custom_call_target="tpu_custom_call" | custom-call | tf_op jit(solution)/shard_map/first_gradient/pallas_call | solution.py:328
  145.2 24.8 %all_to_all.89.parts_ref = f32[8,128,256]{2,1,0:T(8,128)} all-to-all(f32[8,128,256]{2,1,0:T(8,128)} %bitcast.59), channel_id=1, replica_groups=mesh['src'=8,'pair'=8,'beta'=2] {'pair'}, dimensions={0} | all-to-all | bytes 2097152 | tf_op jit(solution)/shard_map/all_to_all | solution.py:353
  170.0 2.3 sum_parts.4
  172.3 19.1 %all_to_all.90 = f32[8,128,256]{2,1,0:T(8,128)} all-to-all(f32[8,128,256]{2,1,0:T(8,128)} %sum_parts.4), channel_id=1, replica_groups=mesh['src'=8,'pair'=8,'beta'=2] {'pair'}, dimensions={0} | all-to-all | bytes 2097152 | tf_op jit(solution)/shard_map/all_to_all | solution.py:360
  191.4 4.3 left_curve.2
  195.7 21.4 %all_to_all.91 = f32[128,1,128]{2,1,0:T(1,128)} all-to-all(f32[128,1,128]{2,1,0:T(1,128)} %bitcast.69), channel_id=1, replica_groups=mesh['src'=8,'pair'=8,'beta'=2] {'src','pair','beta'}, dimensions={0} | all-to-all | bytes 131072 | tf_op jit(solution)/shard_map/all_to_all | solution.py:364
  217.1 9.5 %left_update.2 = (f32[1024,256]{1,0:T(8,128)}, f32[1024,1536]{1,0:T(8,128)}, f32[768,256]{1,0:T(8,128)}) custom-call(s32[5]{0:T(128)} %stack.19.refs_1_.refs_0_.meta_ref, f32[128,128]{1,0:T(8,128)} %bitcast.65, f32[1024,256]{1,0:T(8,128)} %bitcast.46, f32[16,2,64,256]{3,2,1,0:T(8,128)} %bitcast.51, f32[1024,1536]{1,0:T(8,128)} %get-tuple-element.15.refs_4_, ...), custom_call_target="tpu_custom_call" | custom-call | tf_op jit(solution)/shard_map/left_update/pallas_call | solution.py:388
  226.6 18.0 %all_to_all.92.parts_ref = f32[16,48,256]{2,1,0:T(8,128)} all-to-all(f32[16,48,256]{2,1,0:T(8,128)} %bitcast.61), channel_id=1, replica_groups=mesh['src'=8,'pair'=8,'beta'=2] {'src','beta'}, dimensions={0} | all-to-all | bytes 1572864 | tf_op jit(solution)/shard_map/all_to_all | solution.py:353
  244.6 2.1 sum_parts.5
  246.7 17.3 %all_to_all.93 = f32[16,48,256]{2,1,0:T(8,128)} all-to-all(f32[16,48,256]{2,1,0:T(8,128)} %sum_parts.5), channel_id=1, replica_groups=mesh['src'=8,'pair'=8,'beta'=2] {'src','beta'}, dimensions={0} | all-to-all | bytes 1572864 | tf_op jit(solution)/shard_map/all_to_all | solution.py:360
  264.0 4.5 %right_curve.2 = f32[128,128]{1,0:T(8,128)} custom-call(f32[768,256]{1,0:T(8,128)} %bitcast.52, f32[1024,256]{1,0:T(8,128)} %get-tuple-element.17.refs_1_.refs_3_, f32[4,4,1536]{2,1,0:T(4,128)} %get-tuple-element.14.refs_2_.refs_6_.refs_5_), custom_call_target="tpu_custom_call" | custom-call | tf_op jit(solution)/shard_map/right_curve/pallas_call | solution.py:411
  268.5 14.6 %all_to_all.94 = f32[128,1,128]{2,1,0:T(1,128)} all-to-all(f32[128,1,128]{2,1,0:T(1,128)} %bitcast.70), channel_id=1, replica_groups=mesh['src'=8,'pair'=8,'beta'=2] {'src','pair','beta'}, dimensions={0} | all-to-all | bytes 131072 | tf_op jit(solution)/shard_map/all_to_all | solution.py:364
  283.1 9.0 %right_update.1 = (f32[768,256]{1,0:T(8,128)}, f32[1024,1536]{1,0:T(8,128)}, f32[1024,256]{1,0:T(8,128)}) custom-call(f32[128,128]{1,0:T(8,128)} %bitcast.64, f32[768,256]{1,0:T(8,128)} %bitcast.53, f32[768,256]{1,0:T(8,128)} %pad_maximum_fusion.refs_3_.refs_1_.refs_5_.refs_2_, f32[1024,256]{1,0:T(8,128)} %get-tuple-element.17.refs_1_.refs_3_, ...), custom_call_target="tpu_custom_call" | custom-call | tf_op jit(solution)/shard_map/right_update/pallas_call | solution.py:437
  292.1 20.4 %all_to_all.95.parts_ref = f32[8,128,256]{2,1,0:T(8,128)} all-to-all(f32[8,128,256]{2,1,0:T(8,128)} %bitcast.58), channel_id=1, replica_groups=mesh['src'=8,'pair'=8,'beta'=2] {'pair'}, dimensions={0} | all-to-all | bytes 2097152 | tf_op jit(solution)/shard_map/all_to_all | solution.py:353
  312.6 2.3 sum_parts.6
  314.8 19.2 %all_to_all.96 = f32[8,128,256]{2,1,0:T(8,128)} all-to-all(f32[8,128,256]{2,1,0:T(8,128)} %sum_parts.6), channel_id=1, replica_groups=mesh['src'=8,'pair'=8,'beta'=2] {'pair'}, dimensions={0} | all-to-all | bytes 2097152 | tf_op jit(solution)/shard_map/all_to_all | solution.py:360
  334.1 4.3 left_curve.3
  338.4 17.5 %all_to_all.97 = f32[128,1,128]{2,1,0:T(1,128)} all-to-all(f32[128,1,128]{2,1,0:T(1,128)} %bitcast.71), channel_id=1, replica_groups=mesh['src'=8,'pair'=8,'beta'=2] {'src','pair','beta'}, dimensions={0} | all-to-all | bytes 131072 | tf_op jit(solution)/shard_map/all_to_all | solution.py:364
  355.8 8.0 %left_update.3 = (f32[1024,256]{1,0:T(8,128)}, f32[768,256]{1,0:T(8,128)}) custom-call(s32[5]{0:T(128)} %stack.19.refs_1_.refs_0_.meta_ref, f32[128,128]{1,0:T(8,128)} %bitcast.66, f32[1024,256]{1,0:T(8,128)} %bitcast.44, f32[1024,256]{1,0:T(8,128)} %get-tuple-element.17.refs_1_.refs_3_, f32[1024,1536]{1,0:T(8,128)} %get-tuple-element.21.refs_4_, ...), custom_call_target="tpu_custom_call" | custom-call | tf_op jit(solution)/shard_map/left_update/pallas_call | solution.py:388
  363.8 4.3 all-to-all-start.10
  368.1 1.4 collective-permute-start.1
  369.5 11.1 %all-to-all-done.10.parts_ref = f32[16,48,256]{2,1,0:T(8,128)S(1)} async-done(((f32[16,48,256]{2,1,0:T(8,128)}), f32[16,48,256]{2,1,0:T(8,128)S(1)}, u32[]{:S(2)}, u32[]{:S(2)}) %all-to-all-start.10) | async-done | bytes 786464 | tf_op jit(solution)/shard_map/all_to_all | solution.py:353
  380.6 0.9 copy-done.2
  381.5 2.1 sum_parts.7
  383.6 4.0 all-to-all-start.11
  387.7 0.1 iota.12
  387.7 22.6 %all-to-all-done.11 = f32[16,48,256]{2,1,0:T(8,128)S(1)} async-done(((f32[16,48,256]{2,1,0:T(8,128)}), f32[16,48,256]{2,1,0:T(8,128)S(1)}, u32[]{:S(2)}, u32[]{:S(2)}) %all-to-all-start.11) | async-done | bytes 786464 | tf_op jit(solution)/shard_map/all_to_all | solution.py:360
  410.3 0.9 copy-done
  411.2 4.5 %right_curve.3 = f32[128,128]{1,0:T(8,128)} custom-call(f32[768,256]{1,0:T(8,128)} %bitcast.54, f32[1024,256]{1,0:T(8,128)} %get-tuple-element.22.refs_1_, f32[4,4,1536]{2,1,0:T(4,128)} %get-tuple-element.14.refs_2_.refs_6_.refs_5_), custom_call_target="tpu_custom_call" | custom-call | tf_op jit(solution)/shard_map/right_curve/pallas_call | solution.py:411
  415.7 5.3 %all-to-all-start.12 = ((f32[128,1,128]{2,1,0:T(1,128)}), f32[128,1,128]{2,1,0:T(1,128)S(1)}, u32[]{:S(2)}, u32[]{:S(2)}) async-start(f32[128,1,128]{2,1,0:T(1,128)} %bitcast.68), calls=%async_computation.12 | async-start | bytes 131072 | tf_op jit(solution)/shard_map/all_to_all | solution.py:364
  421.0 0.0 collective-permute-done.1
  421.0 0.3 broadcast_in_dim.28
  421.3 0.0 copy-done.1
  421.3 0.3 broadcast_in_dim.25
  421.6 1.6 broadcast_select_fusion
  423.1 7.4 %all-to-all-done.12 = f32[128,1,128]{2,1,0:T(1,128)S(1)} async-done(((f32[128,1,128]{2,1,0:T(1,128)}), f32[128,1,128]{2,1,0:T(1,128)S(1)}, u32[]{:S(2)}, u32[]{:S(2)}) %all-to-all-start.12) | async-done | bytes 65568 | tf_op jit(solution)/shard_map/all_to_all | solution.py:364
  430.6 0.6 copy-done.4
  431.2 2.8 right_last.1
  (7 shorter events, 0.0 us)
Async XLA Ops:
  18.1 12.0 %copy-start.3 = (f32[6,1,64,256]{3,2,1,0:T(8,128)S(1)}, f32[6,1,64,256]{3,2,1,0:T(8,128)}, u32[]{:S(2)}) copy-start(f32[6,1,64,256]{3,2,1,0:T(8,128)} %param.9) | copy-start | bytes 1179652
  18.1 116.4 %all-to-all-start = ((bf16[128,4,64,128]{3,2,1,0:T(8,128)(2,1)}), bf16[128,4,64,128]{3,2,1,0:T(8,128)(2,1)}, u32[]{:S(2)}, u32[]{:S(2)}) async-start(bf16[128,4,64,128]{3,2,1,0:T(8,128)(2,1)} %bitcast.42), calls=%async_computation | async-start | bytes 16777216 | tf_op jit(solution)/shard_map/all_to_all | solution.py:307
  30.1 103.5 %collective-permute-start = (f32[384,256]{1,0:T(8,128)S(1)}, f32[384,256]{1,0:T(8,128)S(1)}, u32[]{:S(2)}, u32[]{:S(2)}) collective-permute-start(f32[384,256]{1,0:T(8,128)S(1)} %bitcast.63), channel_id=1, source_target_pairs={{0,1},{1,0},{2,3},{3,2},{4,5},{5,4},{6,7},{7,6},{8,9},{9,8},{10,11... | collective-permute-start | bytes 1179656 | tf_op jit(solution)/shard_map/ppermute | solution.py:312
  363.8 16.8 %all-to-all-start.10 = ((f32[16,48,256]{2,1,0:T(8,128)}), f32[16,48,256]{2,1,0:T(8,128)S(1)}, u32[]{:S(2)}, u32[]{:S(2)}) async-start(f32[16,48,256]{2,1,0:T(8,128)} %bitcast.60), calls=%async_computation.10 | async-start | bytes 1572864 | tf_op jit(solution)/shard_map/all_to_all | solution.py:353
  368.1 52.9 %collective-permute-start.1 = (f32[1024,256]{1,0:T(8,128)}, f32[1024,256]{1,0:T(8,128)S(1)}, u32[]{:S(2)}, u32[]{:S(2)}) collective-permute-start(f32[1024,256]{1,0:T(8,128)} %get-tuple-element.22.refs_1_), channel_id=1, source_target_pairs={{0,1},{1,0},{2,3},{3,2},{4,5},{5,4},{6,7},{7,6},{8,9},{9,8},{10,11... | collective-permute-start | bytes 3145736 | tf_op jit(solution)/shard_map/ppermute | solution.py:407
  380.6 0.9 copy-start.2
  383.6 26.7 %all-to-all-start.11 = ((f32[16,48,256]{2,1,0:T(8,128)}), f32[16,48,256]{2,1,0:T(8,128)S(1)}, u32[]{:S(2)}, u32[]{:S(2)}) async-start(f32[16,48,256]{2,1,0:T(8,128)} %sum_parts.7), calls=%async_computation.11 | async-start | bytes 1572864 | tf_op jit(solution)/shard_map/all_to_all | solution.py:360
  410.3 0.9 copy-start
  415.7 5.5 %copy-start.1 = (f32[1024,256]{1,0:T(8,128)S(1)}, f32[1024,256]{1,0:T(8,128)}, u32[]{:S(2)}) copy-start(f32[1024,256]{1,0:T(8,128)} %get-tuple-element.22.refs_1_) | copy-start | bytes 3145732
  415.7 14.9 %all-to-all-start.12 = ((f32[128,1,128]{2,1,0:T(1,128)}), f32[128,1,128]{2,1,0:T(1,128)S(1)}, u32[]{:S(2)}, u32[]{:S(2)}) async-start(f32[128,1,128]{2,1,0:T(1,128)} %bitcast.68), calls=%async_computation.12 | async-start | bytes 131072 | tf_op jit(solution)/shard_map/all_to_all | solution.py:364
  430.6 0.6 copy-start.4

commit v3 on v2

v3 whole, which is shorter than its diff:
```python
import jax
import jax.numpy as jnp
from jax import lax
from jax.experimental import pallas as pl
from jax.experimental.pallas import tpu as pltpu
from jax.sharding import PartitionSpec as P

ITERS = 2
EPSILON = 1e-06
ABSENT = 1024.0
LIMIT = 512.0
VMEM = 40 * 1024 * 1024
f32 = jnp.float32
bf16 = jnp.bfloat16


def params():
    return pltpu.CompilerParams(vmem_limit_bytes=VMEM)


def whole(shape):
    return pl.BlockSpec(shape, lambda *_: (0,) * len(shape))


def mod(x, n):
    assert n & (n - 1) == 0
    return x & (n - 1)


def div(x, n):
    assert n & (n - 1) == 0
    return x >> (n.bit_length() - 1)


def nt(a, b):
    return lax.dot_general(a, b, (((1,), (1,)), ((), ())), preferred_element_type=f32)


def nn(a, b):
    return lax.dot_general(a, b, (((1,), (0,)), ((), ())), preferred_element_type=f32)


def tn(a, b):
    return lax.dot_general(a, b, (((0,), (0,)), ((), ())), preferred_element_type=f32)


def stacked(factor, edge):
    half = factor.shape[1] // 2
    rounded = factor.astype(bf16)
    turned = jnp.concatenate([-rounded[:, half:], rounded[:, :half]], axis=1)
    pieces = []
    for t in range(factor.shape[0] // edge):
        rows = slice(t * edge, (t + 1) * edge)
        pieces += [rounded[rows], turned[rows]]
    return jnp.concatenate(pieces, axis=0)


def combined(products, edge):
    half = products.shape[1] // 2
    pieces = []
    for t in range(products.shape[0] // (2 * edge)):
        upper = products[2 * t * edge : (2 * t + 1) * edge]
        lower = products[(2 * t + 1) * edge : (2 * t + 2) * edge]
        pieces.append(jnp.concatenate(
            [upper[:, :half] + lower[:, half:], upper[:, half:] - lower[:, :half]], axis=1
        ))
    return jnp.concatenate(pieces, axis=0)


def step_of(sums):
    lane = lax.broadcasted_iota(jnp.int32, sums.shape, 1)
    numerator = jnp.sum(jnp.where(lane == 0, sums, 0.0), keepdims=True)
    denominator = jnp.sum(jnp.where(lane == 1, sums, 0.0), keepdims=True)
    return numerator / (denominator + EPSILON)


def sums_out(numerator, denominator, shape):
    lane = lax.broadcasted_iota(jnp.int32, shape, 1)
    return jnp.where(lane == 0, numerator, jnp.where(lane == 1, denominator, 0.0))


def weighted(field, weight, edge):
    blocks, columns = weight.shape
    return (field.reshape(blocks, edge, columns) * weight[:, None, :]).reshape(field.shape)


def pack_kernel(flags_ref, meta_ref, data_ref, out_ref, buf_ref, sem_ref, *, n_src, n_rcv):
    sigma = pl.program_id(0)
    steps = pl.num_programs(0)
    _, groups, _, edge, width = data_ref.shape
    pairs = width // (2 * edge)
    n_pair = n_rcv // 2
    place = mod(sigma, 2)

    def copies(step):
        held = mod(step, 2)
        return [
            pltpu.make_async_copy(
                buf_ref.at[held, q],
                out_ref.at[mod(step + q, n_src) * n_pair + q],
                sem_ref.at[held, q],
            )
            for q in range(n_pair)
        ]

    @pl.when(sigma >= 2)
    def _():
        for copy in copies(sigma - 2):
            copy.wait()

    for u in range(groups):
        for pair in range(pairs):
            re = data_ref[0, u, 0, :, pair * 2 * edge : (pair + 1) * 2 * edge]
            im = data_ref[1, u, 0, :, pair * 2 * edge : (pair + 1) * 2 * edge]
            first = jnp.concatenate([re[:, :edge], im[:, :edge]], axis=1)
            second = jnp.concatenate([re[:, edge:], im[:, edge:]], axis=1)
            for side, block in ((0, first), (1, second)):
                column = 2 * pair + side
                source = sigma + n_src * u
                seen = flags_ref[source, column] != 0
                diff = mod(column - source, n_rcv)
                q = div(diff, 2)
                turns = div(source + diff, n_rcv) + div(sigma + q, n_src)
                beta = mod(u + turns + meta_ref[1], 2)
                near = mod(sigma + diff, n_rcv) < n_rcv // 2
                slot = 2 * mod(diff, 2) + jnp.where(near, u // 2, u % 2)
                buf_ref[place, q, beta * groups + slot] = jnp.where(
                    seen, block, jnp.full_like(block, ABSENT)
                )

    for copy in copies(sigma):
        copy.start()

    @pl.when(sigma == steps - 1)
    def _():
        for copy in copies(sigma - 1) + copies(sigma):
            copy.wait()


def first_kernel(meta_ref, blocks_ref, left_ref, right_ref, target_ref, w_ref, grad_ref,
                 held_ref, sem_ref, left_b_ref, *, n_src, n_rcv, slots, edge, per_src, per_rcv):
    step = pl.program_id(0)
    steps = pl.num_programs(0)
    src, pair, beta, band = meta_ref[0], meta_ref[2], meta_ref[3], meta_ref[4]
    total = n_src * per_src
    mids = left_ref.shape[0]
    groups = per_src // n_src
    half = n_rcv // 2
    width = 2 * edge
    per_step = target_ref.shape[2] // width

    def offset_of(column):
        tau = jnp.where(column >= slots, 1, 0)
        return n_rcv * (column - slots * tau) + 2 * pair + tau - half * slots, tau

    def copies(at):
        held = mod(at, 2)
        found = []
        for side in range(per_step):
            offset, tau = offset_of(at * per_step + side)
            residue = 2 * pair + tau
            for mm in range(mids):
                mid = src + n_src * (2 * mm + beta)
                source = mod(mid - (offset >> 1), total)
                receiver = mod(source + offset, total)
                u = div(mod(source, per_src), n_src)
                near = mod(mod(source, n_src) + residue, n_rcv) < half
                slot = 2 * tau + jnp.where(near, div(u, 2), mod(u, 2))
                index = (div(source, per_src) * n_rcv + div(receiver, per_rcv)) * groups + slot
                found.append(pltpu.make_async_copy(
                    blocks_ref.at[index],
                    held_ref.at[held, side, pl.ds(mm * edge, edge)],
                    sem_ref.at[held, side, mm],
                ))
        return found

    @pl.when(step == 0)
    def _():
        for copy in copies(step):
            copy.start()
        left_b_ref[...] = left_ref[...].reshape(left_b_ref.shape).astype(bf16)
        grad_ref[...] = jnp.zeros_like(grad_ref)

    @pl.when(step + 1 < steps)
    def _():
        for copy in copies(step + 1):
            copy.start()

    stack = stacked(right_ref[...], edge)
    product = nt(left_b_ref[...], stack)
    for copy in copies(step):
        copy.wait()
    pieces = []
    for side in range(per_step):
        offset, _ = offset_of(step * per_step + side)
        inside = jnp.abs(offset) <= band
        cols = slice(side * width, (side + 1) * width)
        values = held_ref[mod(step, 2), side]
        wide = values.astype(f32)
        keep = jnp.logical_and(wide < LIMIT, inside)
        target_ref[0, :, cols] = jnp.where(keep, wide, 0.0).astype(bf16)
        for mm in range(mids):
            w_ref[0, mm : mm + 1, cols] = jnp.where(keep[mm * edge : mm * edge + 1], 1.0, 0.0)
        pieces.append(jnp.where(keep, product[:, cols] - wide, 0.0).astype(bf16))
    grad_ref[...] += nn(jnp.concatenate(pieces, axis=1), stack)


def spread_kernel(parts_ref, out_ref):
    total = jnp.sum(parts_ref[...], axis=0)
    out_ref[...] = jnp.broadcast_to(total[None], out_ref.shape)


def curve_kernel(left_ref, right_ref, w_ref, out_ref, *, edge, copies, by_left):
    left = left_ref[...]
    left_b = left.astype(bf16)
    mids = left.shape[0] // edge
    tiles, _, width = w_ref.shape
    rows = width // 2
    total = jnp.zeros((mids, width), f32)
    for tile in range(tiles):
        curve = nt(left_b, stacked(right_ref[tile * rows : (tile + 1) * rows, :], edge))
        squares = (curve * curve).reshape(mids, edge, width)
        total = total + jnp.sum(squares, axis=1) * w_ref[tile]
    grad = left if by_left else right_ref[...]
    numerator = jnp.sum(grad * grad, keepdims=True) * (1.0 / copies)
    out_ref[...] = sums_out(numerator, jnp.sum(total, keepdims=True), out_ref.shape)


def residual_of(target_ref, w_ref, lefts, stacks, steps, edge):
    residual = nt(lefts[0], stacks[0]) - target_ref[0].astype(f32)
    for left, stack, step in zip(lefts[1:], stacks[1:], steps):
        residual = residual - step * nt(left, stack)
    return weighted(residual, w_ref[0], edge).astype(bf16)


def left_update_kernel(meta_ref, *refs, edge, updates):
    taken = iter(refs)
    sums = [next(taken) for _ in range(updates)]
    target_ref, w_ref = next(taken), next(taken)
    start_ref = next(taken)
    first_grad_ref = next(taken)
    right_ref = next(taken)
    if updates == 3:
        left_ref, grad_ref = next(taken), next(taken)
        grad_r_ref, right_now_ref = next(taken), next(taken)
    left_out_ref, out_ref = next(taken), next(taken)
    held = list(taken)
    steps = [step_of(ref[...]) for ref in sums]

    @pl.when(pl.program_id(0) == 0)
    def _():
        start = start_ref[...].reshape(left_out_ref.shape)
        held[0][...] = start.astype(bf16)
        held[1][...] = first_grad_ref[...].astype(bf16)
        if updates == 1:
            new = start - steps[0] * first_grad_ref[...]
            held[2][...] = new.astype(bf16)
        else:
            held[2][...] = left_ref[...].astype(bf16)
            held[3][...] = grad_ref[...].astype(bf16)
            new = left_ref[...] - steps[2] * grad_ref[...]
            held[4][...] = new.astype(bf16)
        left_out_ref[...] = new

    stack = stacked(right_ref[...], edge)
    stacks = [stack, stack]
    lefts = [held[0][...], held[1][...]]
    if updates == 3:
        stacks += [stacked(grad_r_ref[...], edge), stacked(right_now_ref[...], edge)]
        lefts += [held[2][...], held[3][...]]
    residual = residual_of(target_ref, w_ref, lefts, stacks, steps, edge)
    out_ref[...] = combined(tn(held[-1][...], residual).T, edge)


def right_update_kernel(meta_ref, sums_ref, sums_r_ref, target_ref, w_ref, start_ref,
                        first_grad_ref, right_ref, left_ref, grad_r_ref,
                        right_out_ref, grad_ref, *held, edge):
    step = step_of(sums_ref[...])
    step_r = step_of(sums_r_ref[...])

    @pl.when(pl.program_id(0) == 0)
    def _():
        held[0][...] = start_ref[...].reshape(left_ref.shape).astype(bf16)
        held[1][...] = first_grad_ref[...].astype(bf16)
        held[2][...] = left_ref[...].astype(bf16)
        grad_ref[...] = jnp.zeros_like(grad_ref)

    right = right_ref[...] - step_r * grad_r_ref[...]
    right_out_ref[...] = right
    stack = stacked(right_ref[...], edge)
    residual = residual_of(
        target_ref, w_ref, [ref[...] for ref in held],
        [stack, stack, stacked(grad_r_ref[...], edge)], [step, step_r], edge,
    )
    grad_ref[...] += nn(residual, stacked(right, edge))


def right_last_kernel(meta_ref, sums_ref, grad_r_ref, right_ref, right_out_ref):
    right_out_ref[...] = right_ref[...] - step_of(sums_ref[...]) * grad_r_ref[...]


def per_device(data, observed, band_width, left_factor, right_factor):
    n_src = lax.axis_size("src")
    n_pair = lax.axis_size("pair")
    n_rcv = 2 * n_pair
    devices = n_src * n_rcv
    per_src, per_rcv = observed.shape
    edge = data.shape[1] // per_src
    groups = per_src // n_src
    slots = right_factor.shape[0]
    rank2 = left_factor.shape[3]
    mids = per_src // 2
    rows = mids * edge
    own_cols = slots * edge
    cols = 2 * own_cols
    width = 4 * edge
    tiles = 2 * cols // width
    everyone = ("src", "pair", "beta")
    swap = [(0, 1), (1, 0)]

    src = lax.axis_index("src")
    pair = lax.axis_index("pair")
    beta = lax.axis_index("beta")
    meta = jnp.stack([src, 2 * pair + beta, pair, beta, band_width[0]]).astype(jnp.int32)

    own_right = right_factor.reshape(own_cols, rank2)
    other_right = lax.ppermute(own_right, "beta", swap)
    packed = pl.pallas_call(
        lambda *refs: pack_kernel(*refs, n_src=n_src, n_rcv=n_rcv),
        out_shape=jax.ShapeDtypeStruct((n_src * n_pair, 2 * groups, edge, 2 * edge), bf16),
        grid_spec=pltpu.PrefetchScalarGridSpec(
            num_scalar_prefetch=2,
            grid=(n_src,),
            in_specs=[
                pl.BlockSpec((2, groups, 1, edge, data.shape[2]), lambda s, *_: (0, 0, s, 0, 0))
            ],
            out_specs=pl.BlockSpec(memory_space=pl.ANY),
            scratch_shapes=[
                pltpu.VMEM((2, n_pair, 2 * groups, edge, 2 * edge), bf16),
                pltpu.SemaphoreType.DMA((2, n_pair)),
            ],
        ),
        compiler_params=params(),
        name="pack",
    )(observed, meta, data.reshape(2, groups, n_src, edge, data.shape[2]))
    right = jnp.concatenate([
        jnp.where(beta == 0, own_right, other_right),
        jnp.where(beta == 0, other_right, own_right),
    ])
    packed, right = lax.optimization_barrier((packed, right))
    packed = packed.reshape(devices, groups, edge, 2 * edge)
    arrived = lax.all_to_all(packed, everyone, split_axis=0, concat_axis=0, tiled=True)
    arrived = arrived.reshape(devices * groups, edge, 2 * edge)

    start = left_factor.reshape(mids, 2, edge, rank2)

    start_spec = pl.BlockSpec((mids, 1, edge, rank2), lambda c, meta_ref: (0, meta_ref[3], 0, 0))
    left_spec = whole((rows, rank2))
    right_spec = pl.BlockSpec((width // 2, rank2), lambda c, *_: (c, 0))
    target_spec = pl.BlockSpec((1, rows, width), lambda c, *_: (c, 0, 0))
    w_spec = pl.BlockSpec((1, mids, width), lambda c, *_: (c, 0, 0))
    sums_spec = whole((devices, 128))
    left_shape = jax.ShapeDtypeStruct((rows, rank2), f32)
    right_shape = jax.ShapeDtypeStruct((cols, rank2), f32)
    sums_shape = jax.ShapeDtypeStruct((devices, 128), f32)
    left_scratch = pltpu.VMEM((rows, rank2), bf16)

    def call(kernel, name, out_shape, in_specs, out_specs, scratch=(), grid=(tiles,)):
        return pl.pallas_call(
            kernel,
            out_shape=out_shape,
            grid_spec=pltpu.PrefetchScalarGridSpec(
                num_scalar_prefetch=1,
                grid=grid,
                in_specs=in_specs,
                out_specs=out_specs,
                scratch_shapes=list(scratch),
            ),
            compiler_params=params(),
            name=name,
        )

    target, weight, parts = call(
        lambda *refs: first_kernel(
            *refs, n_src=n_src, n_rcv=n_rcv, slots=slots, edge=edge,
            per_src=per_src, per_rcv=per_rcv,
        ),
        "first_gradient",
        (
            jax.ShapeDtypeStruct((tiles, rows, width), bf16),
            jax.ShapeDtypeStruct((tiles, mids, width), f32),
            left_shape,
        ),
        [pl.BlockSpec(memory_space=pl.ANY), start_spec, right_spec],
        (target_spec, w_spec, left_spec),
        [
            pltpu.VMEM((2, width // (2 * edge), rows, 2 * edge), bf16),
            pltpu.SemaphoreType.DMA((2, width // (2 * edge), mids)),
            left_scratch,
        ],
    )(meta, arrived, start, right)

    def spread(parts, axis, count):
        split = parts.reshape(count, parts.shape[0] // count, rank2)
        landed = lax.all_to_all(split, axis, split_axis=0, concat_axis=0, tiled=True)
        copies = pl.pallas_call(
            spread_kernel,
            out_shape=jax.ShapeDtypeStruct(split.shape, f32),
            compiler_params=params(),
            name="sum_parts",
        )(landed)
        full = lax.all_to_all(copies, axis, split_axis=0, concat_axis=0, tiled=True)
        return full.reshape(parts.shape)

    def shared(left, right, by_left, copies):
        sums = pl.pallas_call(
            lambda *refs: curve_kernel(*refs, edge=edge, copies=copies, by_left=by_left),
            out_shape=sums_shape,
            compiler_params=params(),
            name="left_curve" if by_left else "right_curve",
        )(left, right, weight)
        return lax.all_to_all(sums, everyone, split_axis=0, concat_axis=0, tiled=True)

    lefts, grads, rights, grads_r, sums = [start], [], [right], [], []
    for iteration in range(ITERS):
        grad = spread(parts, "pair", n_pair)
        grads.append(grad)
        sums.append(shared(grad, rights[-1], True, n_pair))
        updates = 2 * iteration + 1
        more = updates == 3
        left, parts_r = call(
            lambda *refs: left_update_kernel(*refs, edge=edge, updates=updates),
            "left_update",
            (left_shape, right_shape),
            [sums_spec] * updates
            + [target_spec, w_spec, start_spec, left_spec, right_spec]
            + ([left_spec, left_spec, right_spec, right_spec] if more else []),
            (left_spec, right_spec),
            [left_scratch] * (updates + 2),
        )(
            meta, *sums, target, weight, start, grads[0], rights[0],
            *([lefts[1], grads[1], grads_r[0], rights[1]] if more else []),
        )
        lefts.append(left)
        if more:
            other_left = lax.ppermute(left, "beta", swap)
        grad_r = spread(parts_r, ("src", "beta"), 2 * n_src)
        grads_r.append(grad_r)
        sums.append(shared(left, grad_r, False, 2 * n_src))
        if more:
            own = pl.BlockSpec((own_cols, rank2), lambda c, meta_ref: (meta_ref[3], 0))
            right_out = call(
                right_last_kernel,
                "right_last",
                jax.ShapeDtypeStruct((own_cols, rank2), f32),
                [sums_spec, own, own],
                whole((own_cols, rank2)),
                grid=(1,),
            )(meta, sums[-1], grad_r, rights[-1])
        else:
            right, parts = call(
                lambda *refs: right_update_kernel(*refs, edge=edge),
                "right_update",
                (right_shape, left_shape),
                [sums_spec, sums_spec, target_spec, w_spec, start_spec, left_spec,
                 right_spec, left_spec, right_spec],
                (right_spec, left_spec),
                [left_scratch] * 3,
            )(meta, *sums, target, weight, start, grads[0], rights[0], left, grad_r)
            rights.append(right)
    own_left = lefts[-1].reshape(mids, 1, edge, rank2)
    other_left = other_left.reshape(mids, 1, edge, rank2)
    parity = lax.broadcasted_iota(jnp.int32, (mids, 2, edge, rank2), 1)
    left_out = jnp.where(parity == beta, own_left, other_left)
    return left_out.reshape(left_factor.shape), right_out.reshape(right_factor.shape)


def solution(mesh):
    n_src, n_rcv = mesh.shape["src"], mesh.shape["rcv"]
    split = jax.sharding.Mesh(
        mesh.devices.reshape(n_src, n_rcv // 2, 2), ("src", "pair", "beta")
    )
    rcv = ("pair", "beta")
    return jax.shard_map(
        per_device,
        mesh=split,
        in_specs=(
            P(None, "src", rcv),
            P("src", rcv),
            P(),
            P(None, "src", None, None),
            P(None, rcv, None, None),
        ),
        out_specs=(P(None, "src", None, None), P(None, rcv, None, None)),
        check_vma=False,
    )
```

time: 436 us -> 384 us (0.88)
  waiting for transfers between devices: 143 us -> 41.9 us
  blocking collectives: 172 us -> 259 us
  Pallas kernels: 81.1 us -> 59.4 us
  starting transfers between devices: 28.3 us -> 17.2 us
    all_to_all x0 -> x1, blocking collectives: none -> 107 us  [per_device(): lax.all_to_all(packed, everyone, split_axis=0, concat_axis=0, tiled=True)]
    ppermute x1, waiting for transfers between devices: 102 us -> 0.01 us  [per_device(): other_right = lax.ppermute(own_right, 'beta', swap)]
    pallas_call x9, Pallas kernels: 57.5 us -> 39.3 us  [the longest x2 16.5 us: per_device(): call(lambda *refs: left_update_kernel(*refs, edge=edge, updates=updates),...]
    all_to_all x1 -> x0, starting transfers between devices: 12 us -> none  [per_device(): lax.all_to_all(packed, everyone, split_axis=0, concat_axis=0, tiled=True)]
    all_to_all x3, blocking collectives: 63.2 us -> 54.8 us  [spread(): lax.all_to_all(split, axis, split_axis=0, concat_axis=0, tiled=True)]
    pallas_call x4, Pallas kernels: 8.8 us -> 1.22 us  [spread(): pl.pallas_call(spread_kernel, out_shape=jax.ShapeDtypeStruct(split.shape,...]
    all_to_all x3, blocking collectives: 53.5 us -> 46.2 us  [shared(): lax.all_to_all(sums, everyone, split_axis=0, concat_axis=0, tiled=True)]
    all_to_all x3, blocking collectives: 55.6 us -> 50.8 us  [spread(): full = lax.all_to_all(copies, axis, split_axis=0, concat_axis=0, tiled=True)]
  transfers between devices with their start and end apart: 6 -> 5, of which waited for: 4 -> 3; matrix products, arithmetic and copies ran while one was open for 1% -> 1% of each run, Pallas kernels for 2% -> 6%
where the time goes in v3:
time: 384 us
  blocking collectives  259 us (67%)
  Pallas kernels  59.4 us (15%)
  waiting for transfers between devices  41.9 us (11%)
  starting transfers between devices  17.2 us (4%)
    all_to_all x1, blocking collectives, per_device(): lax.all_to_all(packed, everyone, split_axis=0, concat_axis=0, tiled=True)  107 us
    all_to_all x3, blocking collectives, spread(): lax.all_to_all(split, axis, split_axis=0, concat_axis=0, tiled=True)  54.8 us
    all_to_all x3, blocking collectives, spread(): full = lax.all_to_all(copies, axis, split_axis=0, concat_axis=0, tiled=True)  50.8 us
    all_to_all x3, blocking collectives, shared(): lax.all_to_all(sums, everyone, split_axis=0, concat_axis=0, tiled=True)  46.2 us
    all_to_all x1, waiting for transfers between devices, spread(): full = lax.all_to_all(copies, axis, split_axis=0, concat_axis=0, tiled=True)  24.6 us
    pallas_call x1, Pallas kernels, per_device(): pl.pallas_call(lambda *refs: pack_kernel(*refs, n_src=n_src, n_rcv=n_rcv)...  18.9 us
    pallas_call x2, Pallas kernels, per_device(): call(lambda *refs: left_update_kernel(*refs, edge=edge, updates=updates),...  16.5 us
    all_to_all x1, waiting for transfers between devices, spread(): lax.all_to_all(split, axis, split_axis=0, concat_axis=0, tiled=True)  11.1 us
  transfers between devices with their start and end apart: 5, of which 3 were waited for; matrix products, arithmetic and copies ran while one was open for 1% of the time, Pallas kernels for 6%

profile of v3, /device:TPU:1, one launch (start us, length us, event | category | flops | bytes accessed | tf_op | source)
XLA Modules:
  0.0 383.6 jit_solution(15938783854556213803)
XLA Ops:
  0.6 2.1 collective-permute-start
  3.4 0.8 copy.11.refs_0_
  4.2 0.1 stack.19.refs_1_.refs_0_.meta_ref
  4.3 0.0 copy-start.1
  4.3 18.9 %pack.1 = bf16[64,8,64,128]{3,2,1,0:T(8,128)(2,1)S(1)} custom-call(s32[32,16]{1,0:T(8,128)S(1)} %copy.11.refs_0_, s32[5]{0:T(128)S(1)} %stack.19.refs_1_.refs_0_.meta_ref, bf16[2,4,8,64,1024]{4,3,2,1,0:T(8,128)(2,1)} %bitcast.75), custom_call_target="tpu_custom_call" | custom-call | tf_op jit(solution)/shard_map/pack/pallas_call | solution.py:328
  23.2 0.0 collective-permute-done
  23.2 0.0 copy-done.1
  23.2 0.1 broadcast_select_fusion.2
  23.3 0.1 pad_maximum_fusion.refs_3_.refs_1_.refs_6_.refs_7_.refs_8_
  23.3 0.0 copy-start
  23.3 107.4 %all_to_all.89 = bf16[128,4,64,128]{3,2,1,0:T(8,128)(2,1)} all-to-all(bf16[128,4,64,128]{3,2,1,0:T(8,128)(2,1)S(1)} %bitcast.42), channel_id=1, replica_groups=mesh['src'=8,'pair'=8,'beta'=2] {'src','pair','beta'}, dimensions={0} | all-to-all | bytes 16777216 | tf_op jit(solution)/shard_map/all_to_all | solution.py:352
  130.7 0.0 copy-done
  130.7 9.0 %first_gradient.1 = (bf16[6,1024,256]{2,1,0:T(8,128)(2,1)S(1)}, f32[6,16,256]{2,1,0:T(8,128)S(1)}, f32[1024,256]{1,0:T(8,128)S(1)}) custom-call(s32[5]{0:T(128)S(1)} %stack.19.refs_1_.refs_0_.meta_ref, bf16[512,64,128]{2,1,0:T(8,128)(2,1)} %bitcast.72, f32[16,2,64,256]{3,2,1,0:T(8,128)S(1)} %bitcast.43, ...), custom_call_target="tpu_custom_call" | custom-call | tf_op jit(solution)/shard_map/first_gradient/pallas_call | solution.py:383
  139.8 19.9 %all_to_all.90.parts_ref = f32[8,128,256]{2,1,0:T(8,128)S(1)} all-to-all(f32[8,128,256]{2,1,0:T(8,128)S(1)} %bitcast.62), channel_id=1, replica_groups=mesh['src'=8,'pair'=8,'beta'=2] {'pair'}, dimensions={0} | all-to-all | bytes 2097152 | tf_op jit(solution)/shard_map/all_to_all | solution.py:405
  159.7 0.1 sum_parts.4
  159.8 17.3 %all_to_all.91 = f32[8,128,256]{2,1,0:T(8,128)S(1)} all-to-all(f32[8,128,256]{2,1,0:T(8,128)S(1)} %sum_parts.4), channel_id=1, replica_groups=mesh['src'=8,'pair'=8,'beta'=2] {'pair'}, dimensions={0} | all-to-all | bytes 2097152 | tf_op jit(solution)/shard_map/all_to_all | solution.py:412
  177.1 1.2 left_curve.2
  178.3 16.1 %all_to_all.92 = f32[128,1,128]{2,1,0:T(1,128)S(1)} all-to-all(f32[128,1,128]{2,1,0:T(1,128)S(1)} %bitcast.69), channel_id=1, replica_groups=mesh['src'=8,'pair'=8,'beta'=2] {'src','pair','beta'}, dimensions={0} | all-to-all | bytes 131072 | tf_op jit(solution)/shard_map/all_to_all | solution.py:422
  194.3 6.9 %left_update.2 = (f32[1024,256]{1,0:T(8,128)S(1)}, f32[768,256]{1,0:T(8,128)S(1)}) custom-call(s32[5]{0:T(128)S(1)} %stack.19.refs_1_.refs_0_.meta_ref, f32[128,128]{1,0:T(8,128)S(1)} %bitcast.59, bf16[6,1024,256]{2,1,0:T(8,128)(2,1)S(1)} %get-tuple-element.17.refs_2_.refs_3_.refs_4_, f32[6,16,256]{2,1,0:T(8,128)S(1)} %get-tuple-element.16.refs_2_.refs_3_.refs_4_.refs_5_, ...), custom_call_target="tpu_custom_call" | custom-call | tf_op jit(solution)/shard_map/left_update/pallas_call | solution.py:431
  201.2 16.2 %all_to_all.93.parts_ref = f32[16,48,256]{2,1,0:T(8,128)S(1)} all-to-all(f32[16,48,256]{2,1,0:T(8,128)S(1)} %bitcast.64), channel_id=1, replica_groups=mesh['src'=8,'pair'=8,'beta'=2] {'src','beta'}, dimensions={0} | all-to-all | bytes 1572864 | tf_op jit(solution)/shard_map/all_to_all | solution.py:405
  217.4 0.1 sum_parts.5
  217.5 16.2 %all_to_all.94 = f32[16,48,256]{2,1,0:T(8,128)S(1)} all-to-all(f32[16,48,256]{2,1,0:T(8,128)S(1)} %sum_parts.5), channel_id=1, replica_groups=mesh['src'=8,'pair'=8,'beta'=2] {'src','beta'}, dimensions={0} | all-to-all | bytes 1572864 | tf_op jit(solution)/shard_map/all_to_all | solution.py:412
  233.7 1.2 right_curve.2
  234.9 13.9 %all_to_all.95 = f32[128,1,128]{2,1,0:T(1,128)S(1)} all-to-all(f32[128,1,128]{2,1,0:T(1,128)S(1)} %bitcast.70), channel_id=1, replica_groups=mesh['src'=8,'pair'=8,'beta'=2] {'src','pair','beta'}, dimensions={0} | all-to-all | bytes 131072 | tf_op jit(solution)/shard_map/all_to_all | solution.py:422
  248.9 7.0 %right_update.1 = (f32[768,256]{1,0:T(8,128)S(1)}, f32[1024,256]{1,0:T(8,128)S(1)}) custom-call(s32[5]{0:T(128)S(1)} %stack.19.refs_1_.refs_0_.meta_ref, f32[128,128]{1,0:T(8,128)S(1)} %bitcast.60, f32[128,128]{1,0:T(8,128)S(1)} %bitcast.65, bf16[6,1024,256]{2,1,0:T(8,128)(2,1)S(1)} %get-tuple-element.17.refs_2_.refs_3_.refs_4_, ...), custom_call_target="tpu_custom_call" | custom-call | tf_op jit(solution)/shard_map/right_update/pallas_call | solution.py:461
  255.9 18.6 %all_to_all.96.parts_ref = f32[8,128,256]{2,1,0:T(8,128)S(1)} all-to-all(f32[8,128,256]{2,1,0:T(8,128)S(1)} %bitcast.63), channel_id=1, replica_groups=mesh['src'=8,'pair'=8,'beta'=2] {'pair'}, dimensions={0} | all-to-all | bytes 2097152 | tf_op jit(solution)/shard_map/all_to_all | solution.py:405
  274.5 0.1 sum_parts.6
  274.6 17.3 %all_to_all.97 = f32[8,128,256]{2,1,0:T(8,128)S(1)} all-to-all(f32[8,128,256]{2,1,0:T(8,128)S(1)} %sum_parts.6), channel_id=1, replica_groups=mesh['src'=8,'pair'=8,'beta'=2] {'pair'}, dimensions={0} | all-to-all | bytes 2097152 | tf_op jit(solution)/shard_map/all_to_all | solution.py:412
  291.9 1.2 left_curve.3
  293.1 16.2 %all_to_all.98 = f32[128,1,128]{2,1,0:T(1,128)S(1)} all-to-all(f32[128,1,128]{2,1,0:T(1,128)S(1)} %bitcast.71), channel_id=1, replica_groups=mesh['src'=8,'pair'=8,'beta'=2] {'src','pair','beta'}, dimensions={0} | all-to-all | bytes 131072 | tf_op jit(solution)/shard_map/all_to_all | solution.py:422
  309.3 9.6 %left_update.3 = (f32[1024,256]{1,0:T(8,128)S(1)}, f32[768,256]{1,0:T(8,128)}) custom-call(s32[5]{0:T(128)S(1)} %stack.19.refs_1_.refs_0_.meta_ref, f32[128,128]{1,0:T(8,128)S(1)} %bitcast.61, f32[128,128]{1,0:T(8,128)S(1)} %bitcast.66, f32[128,128]{1,0:T(8,128)S(1)} %bitcast.67, bf16[6,1024,256]{2,1,0:T(8,128)(2,1)S(1)} %get-tuple-element.17.refs_2_.refs_3_.refs_4_, ...), custom_call_target="tpu_custom_call" | custom-call | tf_op jit(solution)/shard_map/left_update/pallas_call | solution.py:431
  318.9 4.4 %all-to-all-start.10 = ((f32[16,48,256]{2,1,0:T(8,128)}), f32[16,48,256]{2,1,0:T(8,128)S(1)}, u32[]{:S(2)}, u32[]{:S(2)}) async-start(f32[16,48,256]{2,1,0:T(8,128)} %bitcast.28), calls=%async_computation.10 | async-start | bytes 1572864 | tf_op jit(solution)/shard_map/all_to_all | solution.py:405
  323.3 1.4 collective-permute-start.1
  324.6 11.1 %all-to-all-done.10.parts_ref = f32[16,48,256]{2,1,0:T(8,128)S(1)} async-done(((f32[16,48,256]{2,1,0:T(8,128)}), f32[16,48,256]{2,1,0:T(8,128)S(1)}, u32[]{:S(2)}, u32[]{:S(2)}) %all-to-all-start.10) | async-done | bytes 786464 | tf_op jit(solution)/shard_map/all_to_all | solution.py:405
  335.8 1.0 sum_parts.7
  336.8 4.0 %all-to-all-start.11 = ((f32[16,48,256]{2,1,0:T(8,128)}), f32[16,48,256]{2,1,0:T(8,128)S(1)}, u32[]{:S(2)}, u32[]{:S(2)}) async-start(f32[16,48,256]{2,1,0:T(8,128)} %sum_parts.7), calls=%async_computation.11 | async-start | bytes 1572864 | tf_op jit(solution)/shard_map/all_to_all | solution.py:412
  340.8 0.1 iota.12
  340.9 24.6 %all-to-all-done.11 = f32[16,48,256]{2,1,0:T(8,128)S(1)} async-done(((f32[16,48,256]{2,1,0:T(8,128)}), f32[16,48,256]{2,1,0:T(8,128)S(1)}, u32[]{:S(2)}, u32[]{:S(2)}) %all-to-all-start.11) | async-done | bytes 786464 | tf_op jit(solution)/shard_map/all_to_all | solution.py:412
  365.5 1.8 right_curve.3
  367.3 5.3 %all-to-all-start.12 = ((f32[128,1,128]{2,1,0:T(1,128)}), f32[128,1,128]{2,1,0:T(1,128)S(1)}, u32[]{:S(2)}, u32[]{:S(2)}) async-start(f32[128,1,128]{2,1,0:T(1,128)} %bitcast.31), calls=%async_computation.12 | async-start | bytes 131072 | tf_op jit(solution)/shard_map/all_to_all | solution.py:422
  372.6 0.0 collective-permute-done.1
  372.6 1.5 broadcast_in_dim.28
  374.1 0.3 broadcast_in_dim.25
  374.4 1.6 broadcast_select_fusion
  376.0 6.2 %all-to-all-done.12 = f32[128,1,128]{2,1,0:T(1,128)S(1)} async-done(((f32[128,1,128]{2,1,0:T(1,128)}), f32[128,1,128]{2,1,0:T(1,128)S(1)}, u32[]{:S(2)}, u32[]{:S(2)}) %all-to-all-start.12) | async-done | bytes 65568 | tf_op jit(solution)/shard_map/all_to_all | solution.py:422
  382.1 1.5 right_last.1
  (2 shorter events, 0.0 us)
Async XLA Ops:
  0.6 22.5 %collective-permute-start = (f32[384,256]{1,0:T(8,128)}, f32[384,256]{1,0:T(8,128)S(1)}, u32[]{:S(2)}, u32[]{:S(2)}) collective-permute-start(f32[384,256]{1,0:T(8,128)} %bitcast.77), channel_id=1, source_target_pairs={{0,1},{1,0},{2,3},{3,2},{4,5},{5,4},{6,7},{7,6},{8,9},{9,8},{10,11... | collective-permute-start | bytes 1179656 | tf_op jit(solution)/shard_map/ppermute | solution.py:327
  4.3 18.9 %copy-start.1 = (f32[6,1,64,256]{3,2,1,0:T(8,128)S(1)}, f32[6,1,64,256]{3,2,1,0:T(8,128)}, u32[]{:S(2)}) copy-start(f32[6,1,64,256]{3,2,1,0:T(8,128)} %param.9) | copy-start | bytes 1179652
  23.3 107.4 %copy-start = (f32[32,1,64,256]{3,2,1,0:T(8,128)S(1)}, f32[32,1,64,256]{3,2,1,0:T(8,128)}, u32[]{:S(2)}) copy-start(f32[32,1,64,256]{3,2,1,0:T(8,128)} %param.8) | copy-start | bytes 6291460
  318.9 16.9 %all-to-all-start.10 = ((f32[16,48,256]{2,1,0:T(8,128)}), f32[16,48,256]{2,1,0:T(8,128)S(1)}, u32[]{:S(2)}, u32[]{:S(2)}) async-start(f32[16,48,256]{2,1,0:T(8,128)} %bitcast.28), calls=%async_computation.10 | async-start | bytes 1572864 | tf_op jit(solution)/shard_map/all_to_all | solution.py:405
  323.3 49.4 %collective-permute-start.1 = (f32[1024,256]{1,0:T(8,128)S(1)}, f32[1024,256]{1,0:T(8,128)}, u32[]{:S(2)}, u32[]{:S(2)}) collective-permute-start(f32[1024,256]{1,0:T(8,128)S(1)} %get-tuple-element.22.refs_0_), channel_id=1, source_target_pairs={{0,1},{1,0},{2,3},{3,2},{4,5},{5,4},{6,7},{7,6},{8,9},{9,8},{10,11... | collective-permute-start | bytes 3145736 | tf_op jit(solution)/shard_map/ppermute | solution.py:446
  336.8 28.8 %all-to-all-start.11 = ((f32[16,48,256]{2,1,0:T(8,128)}), f32[16,48,256]{2,1,0:T(8,128)S(1)}, u32[]{:S(2)}, u32[]{:S(2)}) async-start(f32[16,48,256]{2,1,0:T(8,128)} %sum_parts.7), calls=%async_computation.11 | async-start | bytes 1572864 | tf_op jit(solution)/shard_map/all_to_all | solution.py:412
  367.3 14.8 %all-to-all-start.12 = ((f32[128,1,128]{2,1,0:T(1,128)}), f32[128,1,128]{2,1,0:T(1,128)S(1)}, u32[]{:S(2)}, u32[]{:S(2)}) async-start(f32[128,1,128]{2,1,0:T(1,128)} %bitcast.31), calls=%async_computation.12 | async-start | bytes 131072 | tf_op jit(solution)/shard_map/all_to_all | solution.py:422

commit v4 on v3

v4 whole, which is shorter than its diff:
```python
import jax
import jax.numpy as jnp
from jax import lax
from jax.experimental import pallas as pl
from jax.experimental.pallas import tpu as pltpu
from jax.sharding import PartitionSpec as P

RING = 4
EPSILON = 1e-06
ABSENT = 1024.0
LIMIT = 512.0
VMEM = 24 * 1024 * 1024
f32 = jnp.float32
bf16 = jnp.bfloat16


def params():
    return pltpu.CompilerParams(vmem_limit_bytes=VMEM)


def whole(shape):
    return pl.BlockSpec(shape, lambda *_: (0,) * len(shape))


def mod(x, n):
    assert n & (n - 1) == 0
    return x & (n - 1)


def div(x, n):
    assert n & (n - 1) == 0
    return x >> (n.bit_length() - 1)


def nt(a, b):
    return lax.dot_general(a, b, (((1,), (1,)), ((), ())), preferred_element_type=f32)


def nn(a, b):
    return lax.dot_general(a, b, (((1,), (0,)), ((), ())), preferred_element_type=f32)


def tn(a, b):
    return lax.dot_general(a, b, (((0,), (0,)), ((), ())), preferred_element_type=f32)


def stacked(factor, edge):
    half = factor.shape[1] // 2
    rounded = factor.astype(bf16)
    turned = jnp.concatenate([-rounded[:, half:], rounded[:, :half]], axis=1)
    pieces = []
    for t in range(factor.shape[0] // edge):
        rows = slice(t * edge, (t + 1) * edge)
        pieces += [rounded[rows], turned[rows]]
    return jnp.concatenate(pieces, axis=0)


def combined(products, edge):
    half = products.shape[1] // 2
    pieces = []
    for t in range(products.shape[0] // (2 * edge)):
        upper = products[2 * t * edge : (2 * t + 1) * edge]
        lower = products[(2 * t + 1) * edge : (2 * t + 2) * edge]
        pieces.append(jnp.concatenate(
            [upper[:, :half] + lower[:, half:], upper[:, half:] - lower[:, :half]], axis=1
        ))
    return jnp.concatenate(pieces, axis=0)


def step_of(sums):
    lane = lax.broadcasted_iota(jnp.int32, sums.shape, 1)
    numerator = jnp.sum(jnp.where(lane == 0, sums, 0.0), keepdims=True)
    denominator = jnp.sum(jnp.where(lane == 1, sums, 0.0), keepdims=True)
    return numerator / (denominator + EPSILON)


def sums_out(numerator, denominator, shape):
    lane = lax.broadcasted_iota(jnp.int32, shape, 1)
    return jnp.where(lane == 0, numerator, jnp.where(lane == 1, denominator, 0.0))


def weighted(field, weight, edge):
    blocks, columns = weight.shape
    return (field.reshape(blocks, edge, columns) * weight[:, None, :]).reshape(field.shape)


def pack_kernel(meta_ref, flags_ref, data_ref, out_ref, *, n_src, n_rcv):
    _, groups, _, edge, width = data_ref.shape
    pairs = width // (2 * edge)
    odd = mod(meta_ref[1], 2)
    placed = (odd, 1 - odd)
    for sigma in range(n_src):
        for u in range(groups):
            for pair in range(pairs):
                re = data_ref[0, u, sigma, :, pair * 2 * edge : (pair + 1) * 2 * edge]
                im = data_ref[1, u, sigma, :, pair * 2 * edge : (pair + 1) * 2 * edge]
                first = jnp.concatenate([re[:, :edge], im[:, :edge]], axis=1)
                second = jnp.concatenate([re[:, edge:], im[:, edge:]], axis=1)
                for side, block in ((0, first), (1, second)):
                    column = 2 * pair + side
                    source = sigma + n_src * u
                    seen = flags_ref[source, column] != 0
                    diff = (column - source) % n_rcv
                    q = diff // 2
                    turns = (source + diff) // n_rcv + (sigma + q) // n_src
                    near = (sigma + diff) % n_rcv < n_rcv // 2
                    slot = 2 * (diff % 2) + (u // 2 if near else u % 2)
                    dest = (sigma + q) % n_src * n_rcv + 2 * q + placed[(u + turns) % 2]
                    out_ref[dest, slot] = jnp.where(
                        seen, block, jnp.full_like(block, ABSENT)
                    )


def first_kernel(meta_ref, blocks_ref, left_ref, right_ref,
                 target_ref, w_ref, start_ref, grad_ref, product_ref, residual_ref,
                 *, n_src, n_rcv, slots, edge, per_src, per_rcv):
    src, pair, beta, band = meta_ref[0], meta_ref[2], meta_ref[3], meta_ref[4]
    total = n_src * per_src
    mids = left_ref.shape[0]
    groups = per_src // n_src
    half = n_rcv // 2
    tiles = target_ref.shape[0]
    width = 2 * edge
    per_tile = target_ref.shape[2] // width
    start_ref[...] = left_ref[:, pl.ds(beta, 1)].reshape(start_ref.shape)
    left_b = start_ref[...].astype(bf16)
    for tile in range(tiles):
        rows = slice(tile * per_tile * edge, (tile + 1) * per_tile * edge)
        stack = stacked(right_ref[rows, :], edge)
        product_ref[...] = nt(left_b, stack)
        for side in range(per_tile):
            column = tile * per_tile + side
            tau, t = column // slots, column % slots
            residue = 2 * pair + tau
            offset = n_rcv * t + residue - half * slots
            inside = jnp.abs(offset) <= band
            cols = slice(side * width, (side + 1) * width)
            for mm in range(mids):
                mid = src + n_src * (2 * mm + beta)
                source = mod(mid - (offset >> 1), total)
                receiver = mod(source + offset, total)
                u = div(mod(source, per_src), n_src)
                near = mod(mod(source, n_src) + residue, n_rcv) < half
                slot = 2 * tau + jnp.where(near, div(u, 2), mod(u, 2))
                message = div(source, per_src) * n_rcv + div(receiver, per_rcv)
                wide = blocks_ref[message, slot].astype(f32)
                keep = jnp.logical_and(wide < LIMIT, inside)
                at = slice(mm * edge, (mm + 1) * edge)
                target_ref[tile, at, cols] = jnp.where(keep, wide, 0.0).astype(bf16)
                w_ref[tile, mm : mm + 1, cols] = jnp.where(keep[0:1], 1.0, 0.0)
                residual_ref[at, cols] = jnp.where(
                    keep, product_ref[at, cols] - wide, 0.0
                ).astype(bf16)
        grad = nn(residual_ref[...], stack)
        grad_ref[...] = grad if tile == 0 else grad_ref[...] + grad


def spread_kernel(parts_ref, out_ref):
    total = jnp.sum(parts_ref[...], axis=0)
    out_ref[...] = jnp.broadcast_to(total[None], out_ref.shape)


def curve_kernel(left_ref, right_ref, w_ref, out_ref, *, edge, copies, by_left):
    left_b = left_ref[...].astype(bf16)
    mids = left_b.shape[0] // edge
    tiles, _, width = w_ref.shape
    total = jnp.zeros((mids, width), f32)
    for tile in range(tiles):
        curve = nt(left_b, stacked(tile_rows(right_ref, tile, w_ref), edge))
        squares = (curve * curve).reshape(mids, edge, width)
        total = total + jnp.sum(squares, axis=1) * w_ref[tile]
    grad = left_ref[...] if by_left else right_ref[...]
    numerator = jnp.sum(grad * grad, keepdims=True) * (1.0 / copies)
    out_ref[...] = sums_out(numerator, jnp.sum(total, keepdims=True), out_ref.shape)


def residual_of(target, weight, lefts, stacks, steps, edge):
    residual = nt(lefts[0], stacks[0]) - target.astype(f32)
    for left, stack, step in zip(lefts[1:], stacks[1:], steps):
        residual = residual - step * nt(left, stack)
    return weighted(residual, weight, edge).astype(bf16)


def tile_rows(ref, tile, w_ref):
    rows = w_ref.shape[2] // 2
    return ref[tile * rows : (tile + 1) * rows, :]


def left_update_kernel(meta_ref, sums_ref, target_ref, w_ref, start_ref, first_grad_ref,
                       right_ref, left_out_ref, out_ref, *, edge):
    step = step_of(sums_ref[...])
    start = start_ref[...]
    grad = first_grad_ref[...]
    new = start - step * grad
    left_out_ref[...] = new
    lefts = [start.astype(bf16), grad.astype(bf16)]
    new_b = new.astype(bf16)
    rows = w_ref.shape[2] // 2
    for tile in range(w_ref.shape[0]):
        stack = stacked(tile_rows(right_ref, tile, w_ref), edge)
        residual = residual_of(
            target_ref[tile], w_ref[tile], lefts, [stack, stack], [step], edge
        )
        out_ref[tile * rows : (tile + 1) * rows, :] = combined(tn(new_b, residual).T, edge)


def left_again_kernel(meta_ref, sums_ref, sums_r_ref, sums_now_ref, target_ref, w_ref, start_ref,
                      first_grad_ref, right_ref, left_ref, grad_ref, grad_r_ref, right_now_ref,
                      *refs, edge):
    *other_refs, given_ref, left_b_ref, left_out_ref, out_ref, own_ref, other_ref, sem_ref = refs
    beta = meta_ref[3]
    fetch = pltpu.make_async_copy(given_ref.at[:, 1 - beta], other_ref, sem_ref.at[0])
    own_out = pltpu.make_async_copy(own_ref, left_out_ref.at[:, beta], sem_ref.at[1])
    other_out = pltpu.make_async_copy(other_ref, left_out_ref.at[:, 1 - beta], sem_ref.at[2])
    fetch.start()
    steps = [step_of(ref[...]) for ref in (sums_ref, sums_r_ref, sums_now_ref)]
    new = left_ref[...] - steps[2] * grad_ref[...]
    own_ref[...] = new.reshape(own_ref.shape)
    own_out.start()
    fetch.wait()
    half = len(other_refs) // 2
    mids = other_ref.shape[0] // half
    for part in range(half):
        at = slice(part * mids, (part + 1) * mids)
        first, second = other_refs[part][...], other_refs[half + part][...]
        taken = other_ref[at].reshape(first.shape) - steps[0] * first - steps[2] * second
        other_ref[at] = taken.reshape((mids,) + other_ref.shape[1:])
    other_out.start()
    new_b = new.astype(bf16)
    left_b_ref[...] = new_b
    lefts = [ref[...].astype(bf16) for ref in (start_ref, first_grad_ref, left_ref, grad_ref)]
    rows = w_ref.shape[2] // 2
    for tile in range(w_ref.shape[0]):
        stack, stack_r, stack_now = [
            stacked(tile_rows(ref, tile, w_ref), edge)
            for ref in (right_ref, grad_r_ref, right_now_ref)
        ]
        residual = residual_of(
            target_ref[tile], w_ref[tile], lefts, [stack, stack, stack_r, stack_now], steps, edge
        )
        out_ref[tile * rows : (tile + 1) * rows, :] = combined(tn(new_b, residual).T, edge)
    own_out.wait()
    other_out.wait()


def right_update_kernel(meta_ref, sums_ref, sums_r_ref, target_ref, w_ref, start_ref,
                        first_grad_ref, right_ref, left_ref, grad_r_ref,
                        right_out_ref, grad_ref, *, edge):
    step = step_of(sums_ref[...])
    step_r = step_of(sums_r_ref[...])
    right_out_ref[...] = right_ref[...] - step_r * grad_r_ref[...]
    start = start_ref[...]
    lefts = [value.astype(bf16) for value in (start, first_grad_ref[...], left_ref[...])]
    for tile in range(w_ref.shape[0]):
        stack, stack_r, stack_now = [
            stacked(tile_rows(ref, tile, w_ref), edge)
            for ref in (right_ref, grad_r_ref, right_out_ref)
        ]
        residual = residual_of(
            target_ref[tile], w_ref[tile], lefts, [stack, stack, stack_r], [step, step_r], edge
        )
        grad = nn(residual, stack_now)
        grad_ref[...] = grad if tile == 0 else grad_ref[...] + grad


def right_last_kernel(meta_ref, sums_ref, grad_r_ref, right_ref, right_out_ref):
    own = right_out_ref.shape[0]
    rows = pl.ds(pl.multiple_of(meta_ref[3] * own, own), own)
    right_out_ref[...] = right_ref[rows, :] - step_of(sums_ref[...]) * grad_r_ref[rows, :]


def per_device(data, observed, band_width, left_factor, right_factor):
    n_src = lax.axis_size("src")
    n_pair = lax.axis_size("pair")
    n_rcv = 2 * n_pair
    devices = n_src * n_rcv
    per_src, per_rcv = observed.shape
    edge = data.shape[1] // per_src
    groups = per_src // n_src
    slots = right_factor.shape[0]
    rank2 = left_factor.shape[3]
    mids = per_src // 2
    rows = mids * edge
    own_cols = slots * edge
    cols = 2 * own_cols
    width = 4 * edge
    tiles = 2 * cols // width
    everyone = ("src", "pair", "beta")
    swap = [(0, 1), (1, 0)]

    src = lax.axis_index("src")
    pair = lax.axis_index("pair")
    beta = lax.axis_index("beta")
    meta = jnp.stack([src, 2 * pair + beta, pair, beta, band_width[0]]).astype(jnp.int32)

    own_right = right_factor.reshape(own_cols, rank2)
    other_right = lax.ppermute(own_right, "beta", swap)
    packed = pl.pallas_call(
        lambda *refs: pack_kernel(*refs, n_src=n_src, n_rcv=n_rcv),
        out_shape=jax.ShapeDtypeStruct((devices, groups, edge, 2 * edge), bf16),
        in_specs=[pl.BlockSpec(memory_space=pltpu.SMEM)] * 2
        + [pl.BlockSpec(memory_space=pltpu.VMEM)],
        out_specs=pl.BlockSpec(memory_space=pltpu.VMEM),
        compiler_params=params(),
        name="pack",
    )(meta, observed, data.reshape(2, groups, n_src, edge, data.shape[2]))
    right = jnp.concatenate([
        jnp.where(beta == 0, own_right, other_right),
        jnp.where(beta == 0, other_right, own_right),
    ])
    packed, right = lax.optimization_barrier((packed, right))
    arrived = lax.all_to_all(packed, everyone, split_axis=0, concat_axis=0, tiled=True)

    left_shape = jax.ShapeDtypeStruct((rows, rank2), f32)
    right_shape = jax.ShapeDtypeStruct((cols, rank2), f32)
    sums_shape = jax.ShapeDtypeStruct((devices, 128), f32)

    def call(kernel, name, out_shape, inputs, **kw):
        return pl.pallas_call(
            kernel,
            out_shape=out_shape,
            in_specs=[pl.BlockSpec(memory_space=pltpu.SMEM)]
            + [pl.BlockSpec(memory_space=pltpu.VMEM)] * inputs,
            compiler_params=params(),
            name=name,
            **kw,
        )

    target, weight, start, parts = call(
        lambda *refs: first_kernel(
            *refs, n_src=n_src, n_rcv=n_rcv, slots=slots, edge=edge,
            per_src=per_src, per_rcv=per_rcv,
        ),
        "first_gradient",
        (
            jax.ShapeDtypeStruct((tiles, rows, width), bf16),
            jax.ShapeDtypeStruct((tiles, mids, width), f32),
            left_shape,
            left_shape,
        ),
        3,
        scratch_shapes=[pltpu.VMEM((rows, width), f32), pltpu.VMEM((rows, width), bf16)],
    )(meta, arrived, left_factor.reshape(mids, 2, edge, rank2), right)

    def spread(parts, axis, count):
        split = parts.reshape(count, parts.shape[0] // count, rank2)
        landed = lax.all_to_all(split, axis, split_axis=0, concat_axis=0, tiled=True)
        copies = pl.pallas_call(
            spread_kernel,
            out_shape=jax.ShapeDtypeStruct(split.shape, f32),
            compiler_params=params(),
            name="sum_parts",
        )(landed)
        full = lax.all_to_all(copies, axis, split_axis=0, concat_axis=0, tiled=True)
        return full.reshape(parts.shape)

    def shared(left, right, by_left, copies):
        sums = pl.pallas_call(
            lambda *refs: curve_kernel(*refs, edge=edge, copies=copies, by_left=by_left),
            out_shape=sums_shape,
            compiler_params=params(),
            name="left_curve" if by_left else "right_curve",
        )(left, right, weight)
        return lax.all_to_all(sums, everyone, split_axis=0, concat_axis=0, tiled=True)

    def from_others(grad):
        return [
            lax.ppermute(
                grad[part * rows // 2 : (part + 1) * rows // 2], ("pair", "beta"),
                [(at, at - at % RING + (at + shift) % RING) for at in range(n_rcv)],
            )
            for part, shift in enumerate((1, -1))
        ]

    right_group = ("src", "beta")
    grad = spread(parts, "pair", n_pair)
    sums = shared(grad, right, True, n_pair)
    sums, others = lax.optimization_barrier((sums, from_others(grad)))
    left_one, parts_r = call(
        lambda *refs: left_update_kernel(*refs, edge=edge),
        "left_update", (left_shape, right_shape), 6,
    )(meta, sums, target, weight, start, grad, right)
    grad_r = spread(parts_r, right_group, 2 * n_src)
    sums_r = shared(left_one, grad_r, False, 2 * n_src)
    right_one, parts = call(
        lambda *refs: right_update_kernel(*refs, edge=edge),
        "right_update", (right_shape, left_shape), 9,
    )(meta, sums, sums_r, target, weight, start, grad, right, left_one, grad_r)
    grad_two = spread(parts, "pair", n_pair)
    sums_two = shared(grad_two, right_one, True, n_pair)
    sums_two, others_two = lax.optimization_barrier((sums_two, from_others(grad_two)))
    in_vmem = pl.BlockSpec(memory_space=pltpu.VMEM)
    left_two, left_out, parts_r = pl.pallas_call(
        lambda *refs: left_again_kernel(*refs, edge=edge),
        out_shape=(
            jax.ShapeDtypeStruct((rows, rank2), bf16),
            jax.ShapeDtypeStruct((mids, 2, edge, rank2), f32),
            right_shape,
        ),
        in_specs=[pl.BlockSpec(memory_space=pltpu.SMEM)] + [in_vmem] * 16
        + [pl.BlockSpec(memory_space=pltpu.HBM)],
        out_specs=(in_vmem, pl.BlockSpec(memory_space=pltpu.HBM), in_vmem),
        scratch_shapes=[pltpu.VMEM((mids, edge, rank2), f32)] * 2
        + [pltpu.SemaphoreType.DMA((3,))],
        compiler_params=params(),
        name="left_again",
    )(
        meta, sums, sums_r, sums_two, target, weight, start, grad, right, left_one,
        grad_two, grad_r, right_one, *others, *others_two,
        left_factor.reshape(mids, 2, edge, rank2),
    )
    grad_r_two = spread(parts_r, right_group, 2 * n_src)
    sums_r_two = shared(left_two, grad_r_two, False, 2 * n_src)
    right_out = call(
        right_last_kernel, "right_last", jax.ShapeDtypeStruct((own_cols, rank2), f32), 3,
    )(meta, sums_r_two, grad_r_two, right_one)
    return left_out.reshape(left_factor.shape), right_out.reshape(right_factor.shape)


def solution(mesh):
    n_src, n_rcv = mesh.shape["src"], mesh.shape["rcv"]
    split = jax.sharding.Mesh(
        mesh.devices.reshape(n_src, n_rcv // 2, 2), ("src", "pair", "beta")
    )
    rcv = ("pair", "beta")
    return jax.shard_map(
        per_device,
        mesh=split,
        in_specs=(
            P(None, "src", rcv),
            P("src", rcv),
            P(),
            P(None, "src", None, None),
            P(None, rcv, None, None),
        ),
        out_specs=(P(None, "src", None, None), P(None, rcv, None, None)),
        check_vma=False,
    )
```

time: 384 us -> 353 us (0.919)
  blocking collectives: 259 us -> 310 us
  waiting for transfers between devices: 41.9 us -> 0.48 us
  Pallas kernels: 59.4 us -> 28.5 us
  starting transfers between devices: 17.2 us -> 7.61 us
    all_to_all x3 -> x0, waiting for transfers between devices: 41.9 us -> none  [the longest x1 24.6 us: spread(): full = lax.all_to_all(copies, axis, split_axis=0, concat_axis=0, tiled=True)]
    all_to_all x3 -> x4, blocking collectives: 46.2 us -> 63.4 us  [shared(): lax.all_to_all(sums, everyone, split_axis=0, concat_axis=0, tiled=True)]
    all_to_all x3 -> x4, blocking collectives: 54.8 us -> 71 us  [spread(): lax.all_to_all(split, axis, split_axis=0, concat_axis=0, tiled=True)]
    all_to_all x3 -> x4, blocking collectives: 50.8 us -> 67 us  [spread(): full = lax.all_to_all(copies, axis, split_axis=0, concat_axis=0, tiled=True)]
    pallas_call x1, Pallas kernels: 18.9 us -> 3.17 us  [per_device(): pl.pallas_call(lambda *refs: pack_kernel(*refs, n_src=n_src, n_rcv=n_rcv)...]
    all_to_all x3 -> x0, starting transfers between devices: 13.7 us -> none  [the longest x1 5.32 us: shared(): lax.all_to_all(sums, everyone, split_axis=0, concat_axis=0, tiled=True)]
    pallas_call x1, Pallas kernels: 9.03 us -> 3.34 us  [per_device(): call(lambda *refs: first_kernel(*refs, n_src=n_src, n_rcv=n_rcv, slots=sl...]
    pallas_call x2, Pallas kernels: 16.5 us -> 11.2 us  [the longest x1 7.34 us: per_device(): pl.pallas_call(lambda *refs: left_again_kernel(*refs, edge=edge), out_sha...]
  transfers between devices with their start and end apart: 5 -> 5, of which waited for: 3 -> 1; matrix products, arithmetic and copies ran while one was open for 1% -> 0% of each run, Pallas kernels for 6% -> 2%
where the time goes in v4:
time: 353 us
  blocking collectives  310 us (88%)
  Pallas kernels  28.5 us (8%)
  starting transfers between devices  7.61 us (2%)
  local copies, waits for them, and re-layouts  4.39 us (1%)
    all_to_all x1, blocking collectives, per_device(): lax.all_to_all(packed, everyone, split_axis=0, concat_axis=0, tiled=True)  109 us
    all_to_all x4, blocking collectives, spread(): lax.all_to_all(split, axis, split_axis=0, concat_axis=0, tiled=True)  71 us
    all_to_all x4, blocking collectives, spread(): full = lax.all_to_all(copies, axis, split_axis=0, concat_axis=0, tiled=True)  67 us
    all_to_all x4, blocking collectives, shared(): lax.all_to_all(sums, everyone, split_axis=0, concat_axis=0, tiled=True)  63.4 us
    pallas_call x1, Pallas kernels, per_device(): pl.pallas_call(lambda *refs: left_again_kernel(*refs, edge=edge), out_sha...  7.34 us
  transfers between devices with their start and end apart: 5, of which 1 were waited for; matrix products, arithmetic and copies ran while one was open for 0% of the time, Pallas kernels for 2%

profile of v4, /device:TPU:1, one launch (start us, length us, event | category | flops | bytes accessed | tf_op | source)
XLA Modules:
  0.0 352.6 jit_solution(5918701644533856022)
XLA Ops:
  0.6 2.1 collective-permute-start
  3.4 0.8 copy.10.refs_1_
  4.2 0.1 stack.19.refs_0_.meta_ref
  4.3 0.0 copy-start
  4.3 3.4 copy-done
  7.6 3.2 pack.1
  10.8 0.5 collective-permute-done
  11.3 0.0 copy-done.2
  11.3 0.1 broadcast_select_fusion.1
  11.4 0.1 pad_maximum_fusion.refs_3_.refs_1_.refs_6_.refs_7_.refs_8_
  11.4 0.0 copy-start.1
  11.4 108.6 %all_to_all.91.refs_1_ = bf16[128,4,64,128]{3,2,1,0:T(8,128)(2,1)S(1)} all-to-all(bf16[128,4,64,128]{3,2,1,0:T(8,128)(2,1)S(1)} %pack.1), channel_id=1, replica_groups=mesh['src'=8,'pair'=8,'beta'=2] {'src','pair','beta'}, dimensions={0} | all-to-all | bytes 16777216 | tf_op jit(solution)/shard_map/all_to_all | solution.py:312
  120.0 0.0 copy-done.1
  120.0 3.3 first_gradient.1
  123.4 19.9 %all_to_all.92.parts_ref = f32[8,128,256]{2,1,0:T(8,128)S(1)} all-to-all(f32[8,128,256]{2,1,0:T(8,128)S(1)} %bitcast.60), channel_id=1, replica_groups=mesh['src'=8,'pair'=8,'beta'=2] {'pair'}, dimensions={0} | all-to-all | bytes 2097152 | tf_op jit(solution)/shard_map/all_to_all | solution.py:347
  143.3 0.1 sum_parts.4
  143.4 17.3 %all_to_all.93 = f32[8,128,256]{2,1,0:T(8,128)S(1)} all-to-all(f32[8,128,256]{2,1,0:T(8,128)S(1)} %sum_parts.4), channel_id=1, replica_groups=mesh['src'=8,'pair'=8,'beta'=2] {'pair'}, dimensions={0} | all-to-all | bytes 2097152 | tf_op jit(solution)/shard_map/all_to_all | solution.py:354
  160.7 0.1 fusion.1
  160.8 0.5 collective-permute-start.1
  161.2 2.3 collective-permute-start.2
  163.5 1.2 left_curve.2
  164.7 16.4 %all_to_all.94 = f32[128,1,128]{2,1,0:T(1,128)S(1)} all-to-all(f32[128,1,128]{2,1,0:T(1,128)S(1)} %bitcast.69), channel_id=1, replica_groups=mesh['src'=8,'pair'=8,'beta'=2] {'src','pair','beta'}, dimensions={0} | all-to-all | bytes 131072 | tf_op jit(solution)/shard_map/all_to_all | solution.py:364
  181.0 0.0 collective-permute-done.1.refs_13_
  181.0 0.0 collective-permute-done.2.refs_14_
  181.1 3.9 %left_update.1 = (f32[1024,256]{1,0:T(8,128)S(1)}, f32[768,256]{1,0:T(8,128)S(1)}) custom-call(s32[5]{0:T(128)S(1)} %stack.19.refs_0_.meta_ref, f32[128,128]{1,0:T(8,128)S(1)} %bitcast.57, bf16[6,1024,256]{2,1,0:T(8,128)(2,1)S(1)} %get-tuple-element.26.refs_2_.refs_3_.refs_4_, f32[6,16,256]{2,1,0:T(8,128)S(1)} %get-tuple-element.24.refs_2_.refs_3_.refs_4_.refs_5_, ...), custom_call_target="tpu_custom_call" | custom-call | tf_op jit(solution)/shard_map/left_update/pallas_call | solution.py:379
  184.9 16.2 %all_to_all.95.parts_ref = f32[16,48,256]{2,1,0:T(8,128)S(1)} all-to-all(f32[16,48,256]{2,1,0:T(8,128)S(1)} %bitcast.63), channel_id=1, replica_groups=mesh['src'=8,'pair'=8,'beta'=2] {'src','beta'}, dimensions={0} | all-to-all | bytes 1572864 | tf_op jit(solution)/shard_map/all_to_all | solution.py:347
  201.1 0.1 sum_parts.5
  201.2 16.2 %all_to_all.96 = f32[16,48,256]{2,1,0:T(8,128)S(1)} all-to-all(f32[16,48,256]{2,1,0:T(8,128)S(1)} %sum_parts.5), channel_id=1, replica_groups=mesh['src'=8,'pair'=8,'beta'=2] {'src','beta'}, dimensions={0} | all-to-all | bytes 1572864 | tf_op jit(solution)/shard_map/all_to_all | solution.py:354
  217.4 1.2 right_curve.2
  218.6 14.6 %all_to_all.97 = f32[128,1,128]{2,1,0:T(1,128)S(1)} all-to-all(f32[128,1,128]{2,1,0:T(1,128)S(1)} %bitcast.70), channel_id=1, replica_groups=mesh['src'=8,'pair'=8,'beta'=2] {'src','pair','beta'}, dimensions={0} | all-to-all | bytes 131072 | tf_op jit(solution)/shard_map/all_to_all | solution.py:364
  233.3 4.4 %right_update.1 = (f32[768,256]{1,0:T(8,128)S(1)}, f32[1024,256]{1,0:T(8,128)S(1)}) custom-call(s32[5]{0:T(128)S(1)} %stack.19.refs_0_.meta_ref, f32[128,128]{1,0:T(8,128)S(1)} %bitcast.58, f32[128,128]{1,0:T(8,128)S(1)} %bitcast.64, bf16[6,1024,256]{2,1,0:T(8,128)(2,1)S(1)} %get-tuple-element.26.refs_2_.refs_3_.refs_4_, ...), custom_call_target="tpu_custom_call" | custom-call | tf_op jit(solution)/shard_map/right_update/pallas_call | solution.py:385
  237.6 18.7 %all_to_all.98.parts_ref = f32[8,128,256]{2,1,0:T(8,128)S(1)} all-to-all(f32[8,128,256]{2,1,0:T(8,128)S(1)} %bitcast.61), channel_id=1, replica_groups=mesh['src'=8,'pair'=8,'beta'=2] {'pair'}, dimensions={0} | all-to-all | bytes 2097152 | tf_op jit(solution)/shard_map/all_to_all | solution.py:347
  256.3 0.1 sum_parts.6
  256.4 17.3 %all_to_all.99 = f32[8,128,256]{2,1,0:T(8,128)S(1)} all-to-all(f32[8,128,256]{2,1,0:T(8,128)S(1)} %sum_parts.6), channel_id=1, replica_groups=mesh['src'=8,'pair'=8,'beta'=2] {'pair'}, dimensions={0} | all-to-all | bytes 2097152 | tf_op jit(solution)/shard_map/all_to_all | solution.py:354
  273.7 0.1 fusion
  273.7 1.1 collective-permute-start.3
  274.9 1.6 collective-permute-start.4
  276.5 1.2 left_curve.3
  277.7 16.4 %all_to_all.100 = f32[128,1,128]{2,1,0:T(1,128)S(1)} all-to-all(f32[128,1,128]{2,1,0:T(1,128)S(1)} %bitcast.71), channel_id=1, replica_groups=mesh['src'=8,'pair'=8,'beta'=2] {'src','pair','beta'}, dimensions={0} | all-to-all | bytes 131072 | tf_op jit(solution)/shard_map/all_to_all | solution.py:364
  294.0 0.0 collective-permute-done.3.refs_15_
  294.0 0.0 collective-permute-done.4.refs_16_
  294.0 7.3 %left_again.1 = (bf16[1024,256]{1,0:T(8,128)(2,1)S(1)}, f32[16,2,64,256]{3,2,1,0:T(8,128)}, f32[768,256]{1,0:T(8,128)S(1)}) custom-call(s32[5]{0:T(128)S(1)} %stack.19.refs_0_.meta_ref, f32[128,128]{1,0:T(8,128)S(1)} %bitcast.59, f32[128,128]{1,0:T(8,128)S(1)} %bitcast.65, f32[128,128]{1,0:T(8,128)S(1)} %bitcast.66, ...), custom_call_target="tpu_custom_call" | custom-call | tf_op jit(solution)/shard_map/left_again/pallas_call | solution.py:393
  301.4 16.2 %all_to_all.101.parts_ref = f32[16,48,256]{2,1,0:T(8,128)S(1)} all-to-all(f32[16,48,256]{2,1,0:T(8,128)S(1)} %bitcast.62), channel_id=1, replica_groups=mesh['src'=8,'pair'=8,'beta'=2] {'src','beta'}, dimensions={0} | all-to-all | bytes 1572864 | tf_op jit(solution)/shard_map/all_to_all | solution.py:347
  317.6 0.1 sum_parts.7
  317.7 16.2 %all_to_all.102 = f32[16,48,256]{2,1,0:T(8,128)S(1)} all-to-all(f32[16,48,256]{2,1,0:T(8,128)S(1)} %sum_parts.7), channel_id=1, replica_groups=mesh['src'=8,'pair'=8,'beta'=2] {'src','beta'}, dimensions={0} | all-to-all | bytes 1572864 | tf_op jit(solution)/shard_map/all_to_all | solution.py:354
  333.9 1.2 right_curve.3
  335.1 16.0 %all_to_all.103 = f32[128,1,128]{2,1,0:T(1,128)S(1)} all-to-all(f32[128,1,128]{2,1,0:T(1,128)S(1)} %bitcast.68), channel_id=1, replica_groups=mesh['src'=8,'pair'=8,'beta'=2] {'src','pair','beta'}, dimensions={0} | all-to-all | bytes 131072 | tf_op jit(solution)/shard_map/all_to_all | solution.py:364
  351.1 1.5 right_last.1
  (1 shorter events, 0.0 us)
Async XLA Ops:
  0.6 10.7 %collective-permute-start = (f32[384,256]{1,0:T(8,128)}, f32[384,256]{1,0:T(8,128)S(1)}, u32[]{:S(2)}, u32[]{:S(2)}) collective-permute-start(f32[384,256]{1,0:T(8,128)} %bitcast.77), channel_id=1, source_target_pairs={{0,1},{1,0},{2,3},{3,2},{4,5},{5,4},{6,7},{7,6},{8,9},{9,8},{10,11... | collective-permute-start | bytes 1179656 | tf_op jit(solution)/shard_map/ppermute | solution.py:297
  4.3 3.4 copy-start
  7.6 3.7 %copy-start.2 = (f32[6,1,64,256]{3,2,1,0:T(8,128)S(1)}, f32[6,1,64,256]{3,2,1,0:T(8,128)}, u32[]{:S(2)}) copy-start(f32[6,1,64,256]{3,2,1,0:T(8,128)} %param.9) | copy-start | bytes 1179652
  11.4 108.6 %copy-start.1 = (f32[32,1,64,256]{3,2,1,0:T(8,128)S(1)}, f32[32,1,64,256]{3,2,1,0:T(8,128)}, u32[]{:S(2)}) copy-start(f32[32,1,64,256]{3,2,1,0:T(8,128)} %param.8) | copy-start | bytes 6291460
  160.8 20.3 %collective-permute-start.1 = (f32[512,256]{1,0:T(8,128)S(1)}, f32[512,256]{1,0:T(8,128)S(1)}, u32[]{:S(2)}, u32[]{:S(2)}) collective-permute-start(f32[512,256]{1,0:T(8,128)S(1)} %bitcast.75), channel_id=1, source_target_pairs={{0,1},{1,2},{2,3},{3,0},{4,5},{5,6},{6,7},{7,4},{8,9},{9,10},{10,1... | collective-permute-start | bytes 1572872 | tf_op jit(solution)/shard_map/ppermute | solution.py:368
  161.2 19.8 %collective-permute-start.2 = (f32[512,256]{1,0:T(8,128)S(1)}, f32[512,256]{1,0:T(8,128)S(1)}, u32[]{:S(2)}, u32[]{:S(2)}) collective-permute-start(f32[512,256]{1,0:T(8,128)S(1)} %bitcast.73), channel_id=1, source_target_pairs={{0,3},{1,0},{2,1},{3,2},{4,7},{5,4},{6,5},{7,6},{8,11},{9,8},{10,9... | collective-permute-start | bytes 1572872 | tf_op jit(solution)/shard_map/ppermute | solution.py:368
  273.7 20.3 %collective-permute-start.3 = (f32[512,256]{1,0:T(8,128)S(1)}, f32[512,256]{1,0:T(8,128)S(1)}, u32[]{:S(2)}, u32[]{:S(2)}) collective-permute-start(f32[512,256]{1,0:T(8,128)S(1)} %bitcast.74), channel_id=1, source_target_pairs={{0,1},{1,2},{2,3},{3,0},{4,5},{5,6},{6,7},{7,4},{8,9},{9,10},{10,1... | collective-permute-start | bytes 1572872 | tf_op jit(solution)/shard_map/ppermute | solution.py:368
  274.9 19.2 %collective-permute-start.4 = (f32[512,256]{1,0:T(8,128)S(1)}, f32[512,256]{1,0:T(8,128)S(1)}, u32[]{:S(2)}, u32[]{:S(2)}) collective-permute-start(f32[512,256]{1,0:T(8,128)S(1)} %bitcast.72), channel_id=1, source_target_pairs={{0,3},{1,0},{2,1},{3,2},{4,7},{5,4},{6,5},{7,6},{8,11},{9,8},{10,9... | collective-permute-start | bytes 1572872 | tf_op jit(solution)/shard_map/ppermute | solution.py:368

commit v5 on v4

--- a/solution.py
+++ b/solution.py
@@ -5,8 +5,9 @@
 from jax.experimental.pallas import tpu as pltpu
 from jax.sharding import PartitionSpec as P
 
-RING = 4
 EPSILON = 1e-06
+REACH = 8
+TAIL = 8
 ABSENT = 1024.0
 LIMIT = 512.0
 VMEM = 24 * 1024 * 1024
@@ -16,10 +17,6 @@
 
 def params():
     return pltpu.CompilerParams(vmem_limit_bytes=VMEM)
-
-
-def whole(shape):
-    return pl.BlockSpec(shape, lambda *_: (0,) * len(shape))
 
 
 def mod(x, n):
@@ -82,6 +79,30 @@
 def weighted(field, weight, edge):
     blocks, columns = weight.shape
     return (field.reshape(blocks, edge, columns) * weight[:, None, :]).reshape(field.shape)
+
+
+def power(level):
+    found = jnp.full_like(level, 2.0 ** (-8 * REACH))
+    for k in range(1 - REACH, REACH + 1):
+        found = jnp.where(level >= k, 2.0 ** (8 * k), found)
+    return found
+
+
+def encode(values, out_ref):
+    count, padded, width = out_ref.shape
+    rows = padded - TAIL
+    peak = jnp.max(jnp.abs(values), keepdims=True)
+    level = jnp.full_like(peak, -REACH)
+    for k in range(1 - REACH, REACH + 1):
+        level = jnp.where(peak >= 2.0 ** (8 * k + 7), float(k), level)
+    scaled = (values * power(-level)).reshape(-1, rows, width)
+    out_ref[:, :rows] = jnp.broadcast_to(scaled, (count, rows, width))
+    out_ref[:, rows:] = jnp.broadcast_to(level[None], (count, TAIL, width))
+
+
+def decode(message_ref):
+    rows = message_ref.shape[1] - TAIL
+    return message_ref[:, :rows] * power(message_ref[:, rows : rows + 1])
 
 
 def pack_kernel(meta_ref, flags_ref, data_ref, out_ref, *, n_src, n_rcv):
@@ -112,7 +133,7 @@
 
 
 def first_kernel(meta_ref, blocks_ref, left_ref, right_ref,
-                 target_ref, w_ref, start_ref, grad_ref, product_ref, residual_ref,
+                 target_ref, w_ref, start_ref, out_ref, product_ref, residual_ref, grad_ref,
                  *, n_src, n_rcv, slots, edge, per_src, per_rcv):
     src, pair, beta, band = meta_ref[0], meta_ref[2], meta_ref[3], meta_ref[4]
     total = n_src * per_src
@@ -153,14 +174,16 @@
                 ).astype(bf16)
         grad = nn(residual_ref[...], stack)
         grad_ref[...] = grad if tile == 0 else grad_ref[...] + grad
-
-
-def spread_kernel(parts_ref, out_ref):
-    total = jnp.sum(parts_ref[...], axis=0)
-    out_ref[...] = jnp.broadcast_to(total[None], out_ref.shape)
-
-
-def curve_kernel(left_ref, right_ref, w_ref, out_ref, *, edge, copies, by_left):
+    encode(grad_ref[...], out_ref)
+
+
+def sum_kernel(parts_ref, out_ref):
+    encode(jnp.sum(decode(parts_ref), axis=0), out_ref)
+
+
+def curve_kernel(message_ref, factor_ref, w_ref, out_ref, grad_ref, *, edge, copies, by_left):
+    grad_ref[...] = decode(message_ref).reshape(grad_ref.shape)
+    left_ref, right_ref = (grad_ref, factor_ref) if by_left else (factor_ref, grad_ref)
     left_b = left_ref[...].astype(bf16)
     mids = left_b.shape[0] // edge
     tiles, _, width = w_ref.shape
@@ -169,7 +192,7 @@
         curve = nt(left_b, stacked(tile_rows(right_ref, tile, w_ref), edge))
         squares = (curve * curve).reshape(mids, edge, width)
         total = total + jnp.sum(squares, axis=1) * w_ref[tile]
-    grad = left_ref[...] if by_left else right_ref[...]
+    grad = grad_ref[...]
     numerator = jnp.sum(grad * grad, keepdims=True) * (1.0 / copies)
     out_ref[...] = sums_out(numerator, jnp.sum(total, keepdims=True), out_ref.shape)
 
@@ -187,7 +210,7 @@
 
 
 def left_update_kernel(meta_ref, sums_ref, target_ref, w_ref, start_ref, first_grad_ref,
-                       right_ref, left_out_ref, out_ref, *, edge):
+                       right_ref, left_out_ref, out_ref, parts_ref, *, edge):
     step = step_of(sums_ref[...])
     start = start_ref[...]
     grad = first_grad_ref[...]
@@ -201,13 +224,15 @@
         residual = residual_of(
             target_ref[tile], w_ref[tile], lefts, [stack, stack], [step], edge
         )
-        out_ref[tile * rows : (tile + 1) * rows, :] = combined(tn(new_b, residual).T, edge)
+        parts_ref[tile * rows : (tile + 1) * rows, :] = combined(tn(new_b, residual).T, edge)
+    encode(parts_ref[...], out_ref)
 
 
 def left_again_kernel(meta_ref, sums_ref, sums_r_ref, sums_now_ref, target_ref, w_ref, start_ref,
                       first_grad_ref, right_ref, left_ref, grad_ref, grad_r_ref, right_now_ref,
                       *refs, edge):
-    *other_refs, given_ref, left_b_ref, left_out_ref, out_ref, own_ref, other_ref, sem_ref = refs
+    (first_ref, second_ref, given_ref, left_b_ref, left_out_ref, out_ref,
+     own_ref, other_ref, parts_ref, sem_ref) = refs
     beta = meta_ref[3]
     fetch = pltpu.make_async_copy(given_ref.at[:, 1 - beta], other_ref, sem_ref.at[0])
     own_out = pltpu.make_async_copy(own_ref, left_out_ref.at[:, beta], sem_ref.at[1])
@@ -218,13 +243,10 @@
     own_ref[...] = new.reshape(own_ref.shape)
     own_out.start()
     fetch.wait()
-    half = len(other_refs) // 2
-    mids = other_ref.shape[0] // half
-    for part in range(half):
-        at = slice(part * mids, (part + 1) * mids)
-        first, second = other_refs[part][...], other_refs[half + part][...]
-        taken = other_ref[at].reshape(first.shape) - steps[0] * first - steps[2] * second
-        other_ref[at] = taken.reshape((mids,) + other_ref.shape[1:])
+    taken = other_ref[...].reshape(left_ref.shape)
+    for step, ref in ((steps[0], first_ref), (steps[2], second_ref)):
+        taken = taken - step * decode(ref).reshape(taken.shape)
+    other_ref[...] = taken.reshape(other_ref.shape)
     other_out.start()
     new_b = new.astype(bf16)
     left_b_ref[...] = new_b
@@ -238,14 +260,15 @@
         residual = residual_of(
             target_ref[tile], w_ref[tile], lefts, [stack, stack, stack_r, stack_now], steps, edge
         )
-        out_ref[tile * rows : (tile + 1) * rows, :] = combined(tn(new_b, residual).T, edge)
+        parts_ref[tile * rows : (tile + 1) * rows, :] = combined(tn(new_b, residual).T, edge)
+    encode(parts_ref[...], out_ref)
     own_out.wait()
     other_out.wait()
 
 
 def right_update_kernel(meta_ref, sums_ref, sums_r_ref, target_ref, w_ref, start_ref,
                         first_grad_ref, right_ref, left_ref, grad_r_ref,
-                        right_out_ref, grad_ref, *, edge):
+                        right_out_ref, out_ref, grad_ref, *, edge):
     step = step_of(sums_ref[...])
     step_r = step_of(sums_r_ref[...])
     right_out_ref[...] = right_ref[...] - step_r * grad_r_ref[...]
@@ -261,6 +284,7 @@
         )
         grad = nn(residual, stack_now)
         grad_ref[...] = grad if tile == 0 else grad_ref[...] + grad
+    encode(grad_ref[...], out_ref)
 
 
 def right_last_kernel(meta_ref, sums_ref, grad_r_ref, right_ref, right_out_ref):
@@ -313,6 +337,12 @@
 
     left_shape = jax.ShapeDtypeStruct((rows, rank2), f32)
     right_shape = jax.ShapeDtypeStruct((cols, rank2), f32)
+
+    def parts_shape(count, length):
+        return jax.ShapeDtypeStruct((count, length // count + TAIL, rank2), f32)
+
+    left_parts = parts_shape(n_pair, rows)
+    right_parts = parts_shape(2 * n_src, cols)
     sums_shape = jax.ShapeDtypeStruct((devices, 128), f32)
 
     def call(kernel, name, out_shape, inputs, **kw):
@@ -336,81 +366,81 @@
             jax.ShapeDtypeStruct((tiles, rows, width), bf16),
             jax.ShapeDtypeStruct((tiles, mids, width), f32),
             left_shape,
-            left_shape,
+            left_parts,
         ),
         3,
-        scratch_shapes=[pltpu.VMEM((rows, width), f32), pltpu.VMEM((rows, width), bf16)],
+        scratch_shapes=[
+            pltpu.VMEM((rows, width), f32), pltpu.VMEM((rows, width), bf16),
+            pltpu.VMEM((rows, rank2), f32),
+        ],
     )(meta, arrived, left_factor.reshape(mids, 2, edge, rank2), right)
 
-    def spread(parts, axis, count):
-        split = parts.reshape(count, parts.shape[0] // count, rank2)
-        landed = lax.all_to_all(split, axis, split_axis=0, concat_axis=0, tiled=True)
-        copies = pl.pallas_call(
-            spread_kernel,
-            out_shape=jax.ShapeDtypeStruct(split.shape, f32),
+    def send(parts, axis):
+        return lax.all_to_all(
+            parts.astype(jnp.float16), axis, split_axis=0, concat_axis=0, tiled=True
+        )
+
+    def spread(parts, axis):
+        summed = pl.pallas_call(
+            sum_kernel,
+            out_shape=jax.ShapeDtypeStruct(parts.shape, f32),
             compiler_params=params(),
             name="sum_parts",
-        )(landed)
-        full = lax.all_to_all(copies, axis, split_axis=0, concat_axis=0, tiled=True)
-        return full.reshape(parts.shape)
-
-    def shared(left, right, by_left, copies):
-        sums = pl.pallas_call(
+        )(send(parts, axis).astype(f32))
+        return send(summed, axis)
+
+    def shared(message, factor, by_left, copies):
+        sums, grad = pl.pallas_call(
             lambda *refs: curve_kernel(*refs, edge=edge, copies=copies, by_left=by_left),
-            out_shape=sums_shape,
+            out_shape=(sums_shape, left_shape if by_left else right_shape),
             compiler_params=params(),
             name="left_curve" if by_left else "right_curve",
-        )(left, right, weight)
-        return lax.all_to_all(sums, everyone, split_axis=0, concat_axis=0, tiled=True)
-
-    def from_others(grad):
-        return [
-            lax.ppermute(
-                grad[part * rows // 2 : (part + 1) * rows // 2], ("pair", "beta"),
-                [(at, at - at % RING + (at + shift) % RING) for at in range(n_rcv)],
-            )
-            for part, shift in enumerate((1, -1))
-        ]
+        )(message.astype(f32), factor, weight)
+        sums = lax.all_to_all(sums, everyone, split_axis=0, concat_axis=0, tiled=True)
+        return sums, grad
+
+    def shared_left(parts, factor, *before):
+        message = spread(parts, "pair")
+        other = lax.ppermute(message, "beta", swap)
+        sums, grad = shared(message, factor, True, n_pair)
+        sums, *others = lax.optimization_barrier((sums, *before, other))
+        return sums, grad, *others
 
     right_group = ("src", "beta")
-    grad = spread(parts, "pair", n_pair)
-    sums = shared(grad, right, True, n_pair)
-    sums, others = lax.optimization_barrier((sums, from_others(grad)))
+    sums, grad, other = shared_left(parts, right)
     left_one, parts_r = call(
         lambda *refs: left_update_kernel(*refs, edge=edge),
-        "left_update", (left_shape, right_shape), 6,
+        "left_update", (left_shape, right_parts), 6,
+        scratch_shapes=[pltpu.VMEM((cols, rank2), f32)],
     )(meta, sums, target, weight, start, grad, right)
-    grad_r = spread(parts_r, right_group, 2 * n_src)
-    sums_r = shared(left_one, grad_r, False, 2 * n_src)
+    sums_r, grad_r = shared(spread(parts_r, right_group), left_one, False, 2 * n_src)
     right_one, parts = call(
         lambda *refs: right_update_kernel(*refs, edge=edge),
-        "right_update", (right_shape, left_shape), 9,
+        "right_update", (right_shape, left_parts), 9,
+        scratch_shapes=[pltpu.VMEM((rows, rank2), f32)],
     )(meta, sums, sums_r, target, weight, start, grad, right, left_one, grad_r)
-    grad_two = spread(parts, "pair", n_pair)
-    sums_two = shared(grad_two, right_one, True, n_pair)
-    sums_two, others_two = lax.optimization_barrier((sums_two, from_others(grad_two)))
+    sums_two, grad_two, other, other_two = shared_left(parts, right_one, other)
     in_vmem = pl.BlockSpec(memory_space=pltpu.VMEM)
     left_two, left_out, parts_r = pl.pallas_call(
         lambda *refs: left_again_kernel(*refs, edge=edge),
         out_shape=(
             jax.ShapeDtypeStruct((rows, rank2), bf16),
             jax.ShapeDtypeStruct((mids, 2, edge, rank2), f32),
-            right_shape,
+            right_parts,
         ),
-        in_specs=[pl.BlockSpec(memory_space=pltpu.SMEM)] + [in_vmem] * 16
+        in_specs=[pl.BlockSpec(memory_space=pltpu.SMEM)] + [in_vmem] * 14
         + [pl.BlockSpec(memory_space=pltpu.HBM)],
         out_specs=(in_vmem, pl.BlockSpec(memory_space=pltpu.HBM), in_vmem),
         scratch_shapes=[pltpu.VMEM((mids, edge, rank2), f32)] * 2
-        + [pltpu.SemaphoreType.DMA((3,))],
+        + [pltpu.VMEM((cols, rank2), f32), pltpu.SemaphoreType.DMA((3,))],
         compiler_params=params(),
         name="left_again",
     )(
         meta, sums, sums_r, sums_two, target, weight, start, grad, right, left_one,
-        grad_two, grad_r, right_one, *others, *others_two,
+        grad_two, grad_r, right_one, other.astype(f32), other_two.astype(f32),
         left_factor.reshape(mids, 2, edge, rank2),
     )
-    grad_r_two = spread(parts_r, right_group, 2 * n_src)
-    sums_r_two = shared(left_two, grad_r_two, False, 2 * n_src)
+    sums_r_two, grad_r_two = shared(spread(parts_r, right_group), left_two, False, 2 * n_src)
     right_out = call(
         right_last_kernel, "right_last", jax.ShapeDtypeStruct((own_cols, rank2), f32), 3,
     )(meta, sums_r_two, grad_r_two, right_one)

time: 353 us -> 319 us (0.904)
  blocking collectives: 310 us -> 276 us
  starting transfers between devices: 7.61 us -> 3.96 us
    all_to_all x8, blocking collectives: 138 us -> 103 us  [send(): lax.all_to_all(parts.astype(jnp.float16), axis, split_axis=0, concat_axis...]
    ppermute x4 -> x2, starting transfers between devices: 5.49 us -> 1.84 us  [shared_left(): other = lax.ppermute(message, 'beta', swap)]
  transfers between devices with their start and end apart: 5 -> 3, of which waited for: 1 -> 1; matrix products, arithmetic and copies ran while one was open for 0% -> 0% of each run, Pallas kernels for 2% -> 2%
where the time goes in v5:
time: 319 us
  blocking collectives  276 us (87%)
  Pallas kernels  30.7 us (10%)
  local copies, waits for them, and re-layouts  4.25 us (1%)
  starting transfers between devices  3.96 us (1%)
    all_to_all x1, blocking collectives, per_device(): lax.all_to_all(packed, everyone, split_axis=0, concat_axis=0, tiled=True)  109 us
    all_to_all x8, blocking collectives, send(): lax.all_to_all(parts.astype(jnp.float16), axis, split_axis=0, concat_axis...  103 us
    all_to_all x4, blocking collectives, shared(): lax.all_to_all(sums, everyone, split_axis=0, concat_axis=0, tiled=True)  64.9 us
    pallas_call x1, Pallas kernels, per_device(): pl.pallas_call(lambda *refs: left_again_kernel(*refs, edge=edge), out_sha...  7.8 us
  transfers between devices with their start and end apart: 3, of which 1 were waited for; matrix products, arithmetic and copies ran while one was open for 0% of the time, Pallas kernels for 2%

profile of v5, /device:TPU:1, one launch (start us, length us, event | category | flops | bytes accessed | tf_op | source)
XLA Modules:
  0.0 318.6 jit_solution(8703425568787732879)
XLA Ops:
  0.6 2.1 collective-permute-start
  3.4 0.8 copy.10.refs_1_
  4.2 0.1 stack.19.refs_0_.meta_ref
  4.3 3.4 %copy-done = bf16[2,2048,1024]{2,1,0:T(8,128)(2,1)S(1)} copy-done((bf16[2,2048,1024]{2,1,0:T(8,128)(2,1)S(1)}, bf16[2,2048,1024]{2,1,0:T(8,128)(2,1)}, u32[]{:S(2)}) %copy-start) | copy-done | bytes 8388632
  7.6 3.2 pack.1
  10.8 0.5 collective-permute-done
  11.4 108.6 %all_to_all.91.refs_1_ = bf16[128,4,64,128]{3,2,1,0:T(8,128)(2,1)S(1)} all-to-all(bf16[128,4,64,128]{3,2,1,0:T(8,128)(2,1)S(1)} %pack.1), channel_id=1, replica_groups=mesh['src'=8,'pair'=8,'beta'=2] {'src','pair','beta'}, dimensions={0} | all-to-all | bytes 16777216 | tf_op jit(solution)/shard_map/all_to_all | solution.py:336
  120.0 3.6 %first_gradient.1 = (bf16[6,1024,256]{2,1,0:T(8,128)(2,1)S(1)}, f32[6,16,256]{2,1,0:T(8,128)S(1)}, f32[1024,256]{1,0:T(8,128)S(1)}, f32[8,136,256]{2,1,0:T(8,128)S(1)}) custom-call(s32[5]{0:T(128)S(1)} %stack.19.refs_0_.meta_ref, bf16[128,4,64,128]{3,2,1,0:T(8,128)(2,1)S(1)} %all_to_all.91.refs_1_, f32[16,2,64,256]{3,2,1,0:T(8,128)S(1)} %bitcast.32, ...), custom_call_target="tpu_custom_call" | custom-call | tf_op jit(solution)/shard_map/first_gradient/pallas_call | solution.py:359
  123.6 0.1 convert_element_type.54
  123.7 14.5 %all_to_all.92 = f16[8,136,256]{2,1,0:T(8,128)(2,1)S(1)} all-to-all(f16[8,136,256]{2,1,0:T(8,128)(2,1)S(1)} %convert_element_type.54), channel_id=1, replica_groups=mesh['src'=8,'pair'=8,'beta'=2] {'pair'}, dimensions={0} | all-to-all | bytes 1114112 | tf_op jit(solution)/shard_map/all_to_all | solution.py:379
  138.2 0.1 convert_element_type.55.parts_ref
  138.3 0.3 sum_parts.4
  138.6 0.1 convert_element_type.56
  138.7 13.0 %all_to_all.93 = f16[8,136,256]{2,1,0:T(8,128)(2,1)S(1)} all-to-all(f16[8,136,256]{2,1,0:T(8,128)(2,1)S(1)} %convert_element_type.56), channel_id=1, replica_groups=mesh['src'=8,'pair'=8,'beta'=2] {'pair'}, dimensions={0} | all-to-all | bytes 1114112 | tf_op jit(solution)/shard_map/all_to_all | solution.py:379
  151.7 0.1 convert_element_type.57.refs_0_
  151.8 1.2 left_curve.2
  153.0 16.7 %all_to_all.94 = f32[128,1,128]{2,1,0:T(1,128)S(1)} all-to-all(f32[128,1,128]{2,1,0:T(1,128)S(1)} %bitcast.42), channel_id=1, replica_groups=mesh['src'=8,'pair'=8,'beta'=2] {'src','pair','beta'}, dimensions={0} | all-to-all | bytes 131072 | tf_op jit(solution)/shard_map/all_to_all | solution.py:399
  169.7 4.1 %left_update.1 = (f32[1024,256]{1,0:T(8,128)S(1)}, f32[16,56,256]{2,1,0:T(8,128)S(1)}) custom-call(s32[5]{0:T(128)S(1)} %stack.19.refs_0_.meta_ref, f32[128,128]{1,0:T(8,128)S(1)} %bitcast.34, bf16[6,1024,256]{2,1,0:T(8,128)(2,1)S(1)} %get-tuple-element.34.refs_2_.refs_3_.refs_4_, f32[6,16,256]{2,1,0:T(8,128)S(1)} %get-tuple-element.31.refs_2_.refs_3_.refs_4_.refs_5_, ...), custom_call_target="tpu_custom_call" | custom-call | tf_op jit(solution)/shard_map/left_update/pallas_call | solution.py:411
  173.8 0.1 convert_element_type.58
  173.9 12.4 %all_to_all.95 = f16[16,56,256]{2,1,0:T(8,128)(2,1)S(1)} all-to-all(f16[16,56,256]{2,1,0:T(8,128)(2,1)S(1)} %convert_element_type.58), channel_id=1, replica_groups=mesh['src'=8,'pair'=8,'beta'=2] {'src','beta'}, dimensions={0} | all-to-all | bytes 917504 | tf_op jit(solution)/shard_map/all_to_all | solution.py:379
  186.3 0.1 convert_element_type.59.parts_ref
  186.3 0.3 sum_parts.5
  186.7 0.1 convert_element_type.60
  186.8 12.5 %all_to_all.96 = f16[16,56,256]{2,1,0:T(8,128)(2,1)S(1)} all-to-all(f16[16,56,256]{2,1,0:T(8,128)(2,1)S(1)} %convert_element_type.60), channel_id=1, replica_groups=mesh['src'=8,'pair'=8,'beta'=2] {'src','beta'}, dimensions={0} | all-to-all | bytes 917504 | tf_op jit(solution)/shard_map/all_to_all | solution.py:379
  199.4 1.2 right_curve.2
  200.5 16.0 %all_to_all.97 = f32[128,1,128]{2,1,0:T(1,128)S(1)} all-to-all(f32[128,1,128]{2,1,0:T(1,128)S(1)} %bitcast.43), channel_id=1, replica_groups=mesh['src'=8,'pair'=8,'beta'=2] {'src','pair','beta'}, dimensions={0} | all-to-all | bytes 131072 | tf_op jit(solution)/shard_map/all_to_all | solution.py:399
  216.5 4.6 %right_update.1 = (f32[768,256]{1,0:T(8,128)S(1)}, f32[8,136,256]{2,1,0:T(8,128)S(1)}) custom-call(s32[5]{0:T(128)S(1)} %stack.19.refs_0_.meta_ref, f32[128,128]{1,0:T(8,128)S(1)} %bitcast.35, f32[128,128]{1,0:T(8,128)S(1)} %bitcast.37, bf16[6,1024,256]{2,1,0:T(8,128)(2,1)S(1)} %get-tuple-element.34.refs_2_.refs_3_.refs_4_, ...), custom_call_target="tpu_custom_call" | custom-call | tf_op jit(solution)/shard_map/right_update/pallas_call | solution.py:417
  221.1 0.1 convert_element_type.62
  221.2 13.4 %all_to_all.98 = f16[8,136,256]{2,1,0:T(8,128)(2,1)S(1)} all-to-all(f16[8,136,256]{2,1,0:T(8,128)(2,1)S(1)} %convert_element_type.62), channel_id=1, replica_groups=mesh['src'=8,'pair'=8,'beta'=2] {'pair'}, dimensions={0} | all-to-all | bytes 1114112 | tf_op jit(solution)/shard_map/all_to_all | solution.py:379
  234.6 0.1 convert_element_type.63.parts_ref
  234.7 0.3 sum_parts.6
  235.0 0.1 convert_element_type.64
  235.1 11.9 %all_to_all.99 = f16[8,136,256]{2,1,0:T(8,128)(2,1)S(1)} all-to-all(f16[8,136,256]{2,1,0:T(8,128)(2,1)S(1)} %convert_element_type.64), channel_id=1, replica_groups=mesh['src'=8,'pair'=8,'beta'=2] {'pair'}, dimensions={0} | all-to-all | bytes 1114112 | tf_op jit(solution)/shard_map/all_to_all | solution.py:379
  247.0 1.8 collective-permute-start.2
  248.9 0.1 convert_element_type.65.refs_0_
  248.9 1.2 left_curve.3
  250.1 15.9 %all_to_all.100 = f32[128,1,128]{2,1,0:T(1,128)S(1)} all-to-all(f32[128,1,128]{2,1,0:T(1,128)S(1)} %bitcast.44), channel_id=1, replica_groups=mesh['src'=8,'pair'=8,'beta'=2] {'src','pair','beta'}, dimensions={0} | all-to-all | bytes 131072 | tf_op jit(solution)/shard_map/all_to_all | solution.py:399
  266.1 0.1 convert_element_type.66.refs_13_
  266.2 0.1 convert_element_type.67.refs_14_
  266.2 7.8 %left_again.1 = (bf16[1024,256]{1,0:T(8,128)(2,1)S(1)}, f32[16,2,64,256]{3,2,1,0:T(8,128)}, f32[16,56,256]{2,1,0:T(8,128)S(1)}) custom-call(s32[5]{0:T(128)S(1)} %stack.19.refs_0_.meta_ref, f32[128,128]{1,0:T(8,128)S(1)} %bitcast.36, f32[128,128]{1,0:T(8,128)S(1)} %bitcast.38, f32[128,128]{1,0:T(8,128)S(1)} %bitcast.39, ...), custom_call_target="tpu_custom_call" | custom-call | tf_op jit(solution)/shard_map/left_again/pallas_call | solution.py:424
  274.1 0.1 convert_element_type.68
  274.1 12.4 %all_to_all.101 = f16[16,56,256]{2,1,0:T(8,128)(2,1)S(1)} all-to-all(f16[16,56,256]{2,1,0:T(8,128)(2,1)S(1)} %convert_element_type.68), channel_id=1, replica_groups=mesh['src'=8,'pair'=8,'beta'=2] {'src','beta'}, dimensions={0} | all-to-all | bytes 917504 | tf_op jit(solution)/shard_map/all_to_all | solution.py:379
  286.6 0.3 sum_parts.7
  286.9 0.1 convert_element_type.70
  287.0 12.5 %all_to_all.102 = f16[16,56,256]{2,1,0:T(8,128)(2,1)S(1)} all-to-all(f16[16,56,256]{2,1,0:T(8,128)(2,1)S(1)} %convert_element_type.70), channel_id=1, replica_groups=mesh['src'=8,'pair'=8,'beta'=2] {'src','beta'}, dimensions={0} | all-to-all | bytes 917504 | tf_op jit(solution)/shard_map/all_to_all | solution.py:379
  299.6 1.2 right_curve.3
  300.8 16.3 %all_to_all.103 = f32[128,1,128]{2,1,0:T(1,128)S(1)} all-to-all(f32[128,1,128]{2,1,0:T(1,128)S(1)} %bitcast.41), channel_id=1, replica_groups=mesh['src'=8,'pair'=8,'beta'=2] {'src','pair','beta'}, dimensions={0} | all-to-all | bytes 131072 | tf_op jit(solution)/shard_map/all_to_all | solution.py:399
  317.1 1.5 right_last.1
  (13 shorter events, 0.3 us)
Async XLA Ops:
  0.6 10.7 %collective-permute-start = (f32[384,256]{1,0:T(8,128)}, f32[384,256]{1,0:T(8,128)S(1)}, u32[]{:S(2)}, u32[]{:S(2)}) collective-permute-start(f32[384,256]{1,0:T(8,128)} %bitcast.46), channel_id=1, source_target_pairs={{0,1},{1,0},{2,3},{3,2},{4,5},{5,4},{6,7},{7,6},{8,9},{9,8},{10,11... | collective-permute-start | bytes 1179656 | tf_op jit(solution)/shard_map/ppermute | solution.py:321
  4.3 3.4 %copy-start = (bf16[2,2048,1024]{2,1,0:T(8,128)(2,1)S(1)}, bf16[2,2048,1024]{2,1,0:T(8,128)(2,1)}, u32[]{:S(2)}) copy-start(bf16[2,2048,1024]{2,1,0:T(8,128)(2,1)} %param.5) | copy-start | bytes 25165828
  7.6 3.7 %copy-start.2 = (f32[6,1,64,256]{3,2,1,0:T(8,128)S(1)}, f32[6,1,64,256]{3,2,1,0:T(8,128)}, u32[]{:S(2)}) copy-start(f32[6,1,64,256]{3,2,1,0:T(8,128)} %param.9) | copy-start | bytes 1179652
  11.4 108.6 %copy-start.1 = (f32[32,1,64,256]{3,2,1,0:T(8,128)S(1)}, f32[32,1,64,256]{3,2,1,0:T(8,128)}, u32[]{:S(2)}) copy-start(f32[32,1,64,256]{3,2,1,0:T(8,128)} %param.8) | copy-start | bytes 6291460
  151.7 18.0 %collective-permute-start.1 = (f16[8,136,256]{2,1,0:T(8,128)(2,1)S(1)}, f16[8,136,256]{2,1,0:T(8,128)(2,1)S(1)}, u32[]{:S(2)}, u32[]{:S(2)}) collective-permute-start(f16[8,136,256]{2,1,0:T(8,128)(2,1)S(1)} %all_to_all.93), channel_id=1, source_target_pairs={{0,1},{1,0},{2,3},{3,2},{4,5},{5,4},{6,7},{7,6},{8,9},{9,8},{10,11... | collective-permute-start | bytes 1671176 | tf_op jit(solution)/shard_map/ppermute | solution.py:404
  247.0 19.1 %collective-permute-start.2 = (f16[8,136,256]{2,1,0:T(8,128)(2,1)S(1)}, f16[8,136,256]{2,1,0:T(8,128)(2,1)S(1)}, u32[]{:S(2)}, u32[]{:S(2)}) collective-permute-start(f16[8,136,256]{2,1,0:T(8,128)(2,1)S(1)} %all_to_all.99), channel_id=1, source_target_pairs={{0,1},{1,0},{2,3},{3,2},{4,5},{5,4},{6,7},{7,6},{8,9},{9,8},{10,11... | collective-permute-start | bytes 1671176 | tf_op jit(solution)/shard_map/ppermute | solution.py:404

commit v6 on v5

--- a/solution.py
+++ b/solution.py
@@ -88,14 +88,23 @@
     return found
 
 
-def encode(values, out_ref):
+def steady(values):
+    near = values.astype(bf16).astype(f32)
+    spread = values * (2.0 ** 13 + 1.0)
+    rounded = spread - (spread - values)
+    same = rounded.astype(bf16).astype(f32) == near
+    return jnp.where(same, values, near + 0.8 * (values - near))
+
+
+def encode(values, out_ref, last=False):
     count, padded, width = out_ref.shape
     rows = padded - TAIL
     peak = jnp.max(jnp.abs(values), keepdims=True)
     level = jnp.full_like(peak, -REACH)
     for k in range(1 - REACH, REACH + 1):
         level = jnp.where(peak >= 2.0 ** (8 * k + 7), float(k), level)
-    scaled = (values * power(-level)).reshape(-1, rows, width)
+    scaled = values * power(-level)
+    scaled = (steady(scaled) if last else scaled).reshape(-1, rows, width)
     out_ref[:, :rows] = jnp.broadcast_to(scaled, (count, rows, width))
     out_ref[:, rows:] = jnp.broadcast_to(level[None], (count, TAIL, width))
 
@@ -178,7 +187,7 @@
 
 
 def sum_kernel(parts_ref, out_ref):
-    encode(jnp.sum(decode(parts_ref), axis=0), out_ref)
+    encode(jnp.sum(decode(parts_ref), axis=0), out_ref, last=True)
 
 
 def curve_kernel(message_ref, factor_ref, w_ref, out_ref, grad_ref, *, edge, copies, by_left):
@@ -242,12 +251,6 @@
     new = left_ref[...] - steps[2] * grad_ref[...]
     own_ref[...] = new.reshape(own_ref.shape)
     own_out.start()
-    fetch.wait()
-    taken = other_ref[...].reshape(left_ref.shape)
-    for step, ref in ((steps[0], first_ref), (steps[2], second_ref)):
-        taken = taken - step * decode(ref).reshape(taken.shape)
-    other_ref[...] = taken.reshape(other_ref.shape)
-    other_out.start()
     new_b = new.astype(bf16)
     left_b_ref[...] = new_b
     lefts = [ref[...].astype(bf16) for ref in (start_ref, first_grad_ref, left_ref, grad_ref)]
@@ -257,6 +260,13 @@
             stacked(tile_rows(ref, tile, w_ref), edge)
             for ref in (right_ref, grad_r_ref, right_now_ref)
         ]
+        if tile == 1:
+            fetch.wait()
+            taken = other_ref[...].reshape(left_ref.shape)
+            for step, ref in ((steps[0], first_ref), (steps[2], second_ref)):
+                taken = taken - step * decode(ref).reshape(taken.shape)
+            other_ref[...] = taken.reshape(other_ref.shape)
+            other_out.start()
         residual = residual_of(
             target_ref[tile], w_ref[tile], lefts, [stack, stack, stack_r, stack_now], steps, edge
         )

time: 319 us -> 319 us (level)
  no operation moved by 1% of the time
where the time goes in v6:
time: 319 us
  blocking collectives  277 us (87%)
  Pallas kernels  30.9 us (10%)
  local copies, waits for them, and re-layouts  4.25 us (1%)
    all_to_all x1, blocking collectives, per_device(): lax.all_to_all(packed, everyone, split_axis=0, concat_axis=0, tiled=True)  109 us
    all_to_all x8, blocking collectives, send(): lax.all_to_all(parts.astype(jnp.float16), axis, split_axis=0, concat_axis...  103 us
    all_to_all x4, blocking collectives, shared(): lax.all_to_all(sums, everyone, split_axis=0, concat_axis=0, tiled=True)  65.9 us
    pallas_call x1, Pallas kernels, per_device(): pl.pallas_call(lambda *refs: left_again_kernel(*refs, edge=edge), out_sha...  7.82 us
  transfers between devices with their start and end apart: 3, of which 1 were waited for; matrix products, arithmetic and copies ran while one was open for 0% of the time, Pallas kernels for 2%

profile of v6, /device:TPU:1, one launch (start us, length us, event | category | flops | bytes accessed | tf_op | source)
XLA Modules:
  0.0 318.8 jit_solution(16627792860613526997)
XLA Ops:
  0.6 2.1 collective-permute-start
  3.4 0.8 copy.10.refs_1_
  4.2 0.1 stack.19.refs_0_.meta_ref
  4.3 3.4 %copy-done = bf16[2,2048,1024]{2,1,0:T(8,128)(2,1)S(1)} copy-done((bf16[2,2048,1024]{2,1,0:T(8,128)(2,1)S(1)}, bf16[2,2048,1024]{2,1,0:T(8,128)(2,1)}, u32[]{:S(2)}) %copy-start) | copy-done | bytes 8388632
  7.6 3.2 pack.1
  10.8 0.5 collective-permute-done
  11.4 108.6 %all_to_all.91.refs_1_ = bf16[128,4,64,128]{3,2,1,0:T(8,128)(2,1)S(1)} all-to-all(bf16[128,4,64,128]{3,2,1,0:T(8,128)(2,1)S(1)} %pack.1), channel_id=1, replica_groups=mesh['src'=8,'pair'=8,'beta'=2] {'src','pair','beta'}, dimensions={0} | all-to-all | bytes 16777216 | tf_op jit(solution)/shard_map/all_to_all | solution.py:346
  120.0 3.6 %first_gradient.1 = (bf16[6,1024,256]{2,1,0:T(8,128)(2,1)S(1)}, f32[6,16,256]{2,1,0:T(8,128)S(1)}, f32[1024,256]{1,0:T(8,128)S(1)}, f32[8,136,256]{2,1,0:T(8,128)S(1)}) custom-call(s32[5]{0:T(128)S(1)} %stack.19.refs_0_.meta_ref, bf16[128,4,64,128]{3,2,1,0:T(8,128)(2,1)S(1)} %all_to_all.91.refs_1_, f32[16,2,64,256]{3,2,1,0:T(8,128)S(1)} %bitcast.32, ...), custom_call_target="tpu_custom_call" | custom-call | tf_op jit(solution)/shard_map/first_gradient/pallas_call | solution.py:369
  123.6 0.1 convert_element_type.54
  123.7 14.5 %all_to_all.92 = f16[8,136,256]{2,1,0:T(8,128)(2,1)S(1)} all-to-all(f16[8,136,256]{2,1,0:T(8,128)(2,1)S(1)} %convert_element_type.54), channel_id=1, replica_groups=mesh['src'=8,'pair'=8,'beta'=2] {'pair'}, dimensions={0} | all-to-all | bytes 1114112 | tf_op jit(solution)/shard_map/all_to_all | solution.py:389
  138.2 0.1 convert_element_type.55.parts_ref
  138.3 0.4 sum_parts.4
  138.7 0.1 convert_element_type.56
  138.8 13.0 %all_to_all.93 = f16[8,136,256]{2,1,0:T(8,128)(2,1)S(1)} all-to-all(f16[8,136,256]{2,1,0:T(8,128)(2,1)S(1)} %convert_element_type.56), channel_id=1, replica_groups=mesh['src'=8,'pair'=8,'beta'=2] {'pair'}, dimensions={0} | all-to-all | bytes 1114112 | tf_op jit(solution)/shard_map/all_to_all | solution.py:389
  151.8 0.1 convert_element_type.57.refs_0_
  151.8 1.2 left_curve.2
  153.0 16.7 %all_to_all.94 = f32[128,1,128]{2,1,0:T(1,128)S(1)} all-to-all(f32[128,1,128]{2,1,0:T(1,128)S(1)} %bitcast.42), channel_id=1, replica_groups=mesh['src'=8,'pair'=8,'beta'=2] {'src','pair','beta'}, dimensions={0} | all-to-all | bytes 131072 | tf_op jit(solution)/shard_map/all_to_all | solution.py:409
  169.7 4.1 %left_update.1 = (f32[1024,256]{1,0:T(8,128)S(1)}, f32[16,56,256]{2,1,0:T(8,128)S(1)}) custom-call(s32[5]{0:T(128)S(1)} %stack.19.refs_0_.meta_ref, f32[128,128]{1,0:T(8,128)S(1)} %bitcast.34, bf16[6,1024,256]{2,1,0:T(8,128)(2,1)S(1)} %get-tuple-element.34.refs_2_.refs_3_.refs_4_, f32[6,16,256]{2,1,0:T(8,128)S(1)} %get-tuple-element.31.refs_2_.refs_3_.refs_4_.refs_5_, ...), custom_call_target="tpu_custom_call" | custom-call | tf_op jit(solution)/shard_map/left_update/pallas_call | solution.py:421
  173.8 0.1 convert_element_type.58
  173.9 12.4 %all_to_all.95 = f16[16,56,256]{2,1,0:T(8,128)(2,1)S(1)} all-to-all(f16[16,56,256]{2,1,0:T(8,128)(2,1)S(1)} %convert_element_type.58), channel_id=1, replica_groups=mesh['src'=8,'pair'=8,'beta'=2] {'src','beta'}, dimensions={0} | all-to-all | bytes 917504 | tf_op jit(solution)/shard_map/all_to_all | solution.py:389
  186.3 0.1 convert_element_type.59.parts_ref
  186.4 0.3 sum_parts.5
  186.8 0.1 convert_element_type.60
  186.8 12.5 %all_to_all.96 = f16[16,56,256]{2,1,0:T(8,128)(2,1)S(1)} all-to-all(f16[16,56,256]{2,1,0:T(8,128)(2,1)S(1)} %convert_element_type.60), channel_id=1, replica_groups=mesh['src'=8,'pair'=8,'beta'=2] {'src','beta'}, dimensions={0} | all-to-all | bytes 917504 | tf_op jit(solution)/shard_map/all_to_all | solution.py:389
  199.4 1.2 right_curve.2
  200.6 16.0 %all_to_all.97 = f32[128,1,128]{2,1,0:T(1,128)S(1)} all-to-all(f32[128,1,128]{2,1,0:T(1,128)S(1)} %bitcast.43), channel_id=1, replica_groups=mesh['src'=8,'pair'=8,'beta'=2] {'src','pair','beta'}, dimensions={0} | all-to-all | bytes 131072 | tf_op jit(solution)/shard_map/all_to_all | solution.py:409
  216.6 4.6 %right_update.1 = (f32[768,256]{1,0:T(8,128)S(1)}, f32[8,136,256]{2,1,0:T(8,128)S(1)}) custom-call(s32[5]{0:T(128)S(1)} %stack.19.refs_0_.meta_ref, f32[128,128]{1,0:T(8,128)S(1)} %bitcast.35, f32[128,128]{1,0:T(8,128)S(1)} %bitcast.37, bf16[6,1024,256]{2,1,0:T(8,128)(2,1)S(1)} %get-tuple-element.34.refs_2_.refs_3_.refs_4_, ...), custom_call_target="tpu_custom_call" | custom-call | tf_op jit(solution)/shard_map/right_update/pallas_call | solution.py:427
  221.2 0.1 convert_element_type.62
  221.3 13.4 %all_to_all.98 = f16[8,136,256]{2,1,0:T(8,128)(2,1)S(1)} all-to-all(f16[8,136,256]{2,1,0:T(8,128)(2,1)S(1)} %convert_element_type.62), channel_id=1, replica_groups=mesh['src'=8,'pair'=8,'beta'=2] {'pair'}, dimensions={0} | all-to-all | bytes 1114112 | tf_op jit(solution)/shard_map/all_to_all | solution.py:389
  234.6 0.1 convert_element_type.63.parts_ref
  234.7 0.4 sum_parts.6
  235.1 0.1 convert_element_type.64
  235.2 11.9 %all_to_all.99 = f16[8,136,256]{2,1,0:T(8,128)(2,1)S(1)} all-to-all(f16[8,136,256]{2,1,0:T(8,128)(2,1)S(1)} %convert_element_type.64), channel_id=1, replica_groups=mesh['src'=8,'pair'=8,'beta'=2] {'pair'}, dimensions={0} | all-to-all | bytes 1114112 | tf_op jit(solution)/shard_map/all_to_all | solution.py:389
  247.1 0.9 collective-permute-start.2
  248.0 0.1 convert_element_type.65.refs_0_
  248.1 1.2 left_curve.3
  249.2 16.9 %all_to_all.100 = f32[128,1,128]{2,1,0:T(1,128)S(1)} all-to-all(f32[128,1,128]{2,1,0:T(1,128)S(1)} %bitcast.44), channel_id=1, replica_groups=mesh['src'=8,'pair'=8,'beta'=2] {'src','pair','beta'}, dimensions={0} | all-to-all | bytes 131072 | tf_op jit(solution)/shard_map/all_to_all | solution.py:409
  266.1 0.1 convert_element_type.66.refs_13_
  266.2 0.1 convert_element_type.67.refs_14_
  266.3 7.8 %left_again.1 = (bf16[1024,256]{1,0:T(8,128)(2,1)S(1)}, f32[16,2,64,256]{3,2,1,0:T(8,128)}, f32[16,56,256]{2,1,0:T(8,128)S(1)}) custom-call(s32[5]{0:T(128)S(1)} %stack.19.refs_0_.meta_ref, f32[128,128]{1,0:T(8,128)S(1)} %bitcast.36, f32[128,128]{1,0:T(8,128)S(1)} %bitcast.38, f32[128,128]{1,0:T(8,128)S(1)} %bitcast.39, ...), custom_call_target="tpu_custom_call" | custom-call | tf_op jit(solution)/shard_map/left_again/pallas_call | solution.py:434
  274.1 0.1 convert_element_type.68
  274.2 12.4 %all_to_all.101 = f16[16,56,256]{2,1,0:T(8,128)(2,1)S(1)} all-to-all(f16[16,56,256]{2,1,0:T(8,128)(2,1)S(1)} %convert_element_type.68), channel_id=1, replica_groups=mesh['src'=8,'pair'=8,'beta'=2] {'src','beta'}, dimensions={0} | all-to-all | bytes 917504 | tf_op jit(solution)/shard_map/all_to_all | solution.py:389
  286.7 0.3 sum_parts.7
  287.1 0.1 convert_element_type.70
  287.1 12.5 %all_to_all.102 = f16[16,56,256]{2,1,0:T(8,128)(2,1)S(1)} all-to-all(f16[16,56,256]{2,1,0:T(8,128)(2,1)S(1)} %convert_element_type.70), channel_id=1, replica_groups=mesh['src'=8,'pair'=8,'beta'=2] {'src','beta'}, dimensions={0} | all-to-all | bytes 917504 | tf_op jit(solution)/shard_map/all_to_all | solution.py:389
  299.7 1.2 right_curve.3
  300.9 16.4 %all_to_all.103 = f32[128,1,128]{2,1,0:T(1,128)S(1)} all-to-all(f32[128,1,128]{2,1,0:T(1,128)S(1)} %bitcast.41), channel_id=1, replica_groups=mesh['src'=8,'pair'=8,'beta'=2] {'src','pair','beta'}, dimensions={0} | all-to-all | bytes 131072 | tf_op jit(solution)/shard_map/all_to_all | solution.py:409
  317.3 1.5 right_last.1
  (13 shorter events, 0.3 us)
Async XLA Ops:
  0.6 10.7 %collective-permute-start = (f32[384,256]{1,0:T(8,128)}, f32[384,256]{1,0:T(8,128)S(1)}, u32[]{:S(2)}, u32[]{:S(2)}) collective-permute-start(f32[384,256]{1,0:T(8,128)} %bitcast.46), channel_id=1, source_target_pairs={{0,1},{1,0},{2,3},{3,2},{4,5},{5,4},{6,7},{7,6},{8,9},{9,8},{10,11... | collective-permute-start | bytes 1179656 | tf_op jit(solution)/shard_map/ppermute | solution.py:331
  4.3 3.4 %copy-start = (bf16[2,2048,1024]{2,1,0:T(8,128)(2,1)S(1)}, bf16[2,2048,1024]{2,1,0:T(8,128)(2,1)}, u32[]{:S(2)}) copy-start(bf16[2,2048,1024]{2,1,0:T(8,128)(2,1)} %param.5) | copy-start | bytes 25165828
  7.6 3.7 %copy-start.2 = (f32[6,1,64,256]{3,2,1,0:T(8,128)S(1)}, f32[6,1,64,256]{3,2,1,0:T(8,128)}, u32[]{:S(2)}) copy-start(f32[6,1,64,256]{3,2,1,0:T(8,128)} %param.9) | copy-start | bytes 1179652
  11.4 108.6 %copy-start.1 = (f32[32,1,64,256]{3,2,1,0:T(8,128)S(1)}, f32[32,1,64,256]{3,2,1,0:T(8,128)}, u32[]{:S(2)}) copy-start(f32[32,1,64,256]{3,2,1,0:T(8,128)} %param.8) | copy-start | bytes 6291460
  151.8 18.0 %collective-permute-start.1 = (f16[8,136,256]{2,1,0:T(8,128)(2,1)S(1)}, f16[8,136,256]{2,1,0:T(8,128)(2,1)S(1)}, u32[]{:S(2)}, u32[]{:S(2)}) collective-permute-start(f16[8,136,256]{2,1,0:T(8,128)(2,1)S(1)} %all_to_all.93), channel_id=1, source_target_pairs={{0,1},{1,0},{2,3},{3,2},{4,5},{5,4},{6,7},{7,6},{8,9},{9,8},{10,11... | collective-permute-start | bytes 1671176 | tf_op jit(solution)/shard_map/ppermute | solution.py:414
  247.1 19.0 %collective-permute-start.2 = (f16[8,136,256]{2,1,0:T(8,128)(2,1)S(1)}, f16[8,136,256]{2,1,0:T(8,128)(2,1)S(1)}, u32[]{:S(2)}, u32[]{:S(2)}) collective-permute-start(f16[8,136,256]{2,1,0:T(8,128)(2,1)S(1)} %all_to_all.99), channel_id=1, source_target_pairs={{0,1},{1,0},{2,3},{3,2},{4,5},{5,4},{6,7},{7,6},{8,9},{9,8},{10,11... | collective-permute-start | bytes 1671176 | tf_op jit(solution)/shard_map/ppermute | solution.py:414

commit v7 on v6

--- a/solution.py
+++ b/solution.py
@@ -7,6 +7,7 @@
 
 EPSILON = 1e-06
 REACH = 8
+SLOTS = 8
 TAIL = 8
 ABSENT = 1024.0
 LIMIT = 512.0
@@ -114,16 +115,31 @@
     return message_ref[:, :rows] * power(message_ref[:, rows : rows + 1])
 
 
-def pack_kernel(meta_ref, flags_ref, data_ref, out_ref, *, n_src, n_rcv):
+def place(own, other, beta, out_ref):
+    rows = own.shape[0]
+    out_ref[pl.ds(pl.multiple_of(beta * rows, rows), rows), :] = own
+    out_ref[pl.ds(pl.multiple_of((1 - beta) * rows, rows), rows), :] = other
+
+
+def pack_kernel(meta_ref, flags_ref, data_ref, out_ref, buf_ref, sem_ref, *, n_src, n_rcv):
     _, groups, _, edge, width = data_ref.shape
+    copies = [
+        pltpu.make_async_copy(
+            data_ref.at[:, :, sigma], buf_ref.at[sigma % SLOTS], sem_ref.at[sigma % SLOTS]
+        )
+        for sigma in range(n_src)
+    ]
+    for copy in copies[:SLOTS]:
+        copy.start()
     pairs = width // (2 * edge)
     odd = mod(meta_ref[1], 2)
     placed = (odd, 1 - odd)
     for sigma in range(n_src):
+        copies[sigma].wait()
         for u in range(groups):
             for pair in range(pairs):
-                re = data_ref[0, u, sigma, :, pair * 2 * edge : (pair + 1) * 2 * edge]
-                im = data_ref[1, u, sigma, :, pair * 2 * edge : (pair + 1) * 2 * edge]
+                re = buf_ref[sigma % SLOTS, 0, u, :, pair * 2 * edge : (pair + 1) * 2 * edge]
+                im = buf_ref[sigma % SLOTS, 1, u, :, pair * 2 * edge : (pair + 1) * 2 * edge]
                 first = jnp.concatenate([re[:, :edge], im[:, :edge]], axis=1)
                 second = jnp.concatenate([re[:, edge:], im[:, edge:]], axis=1)
                 for side, block in ((0, first), (1, second)):
@@ -139,10 +155,12 @@
                     out_ref[dest, slot] = jnp.where(
                         seen, block, jnp.full_like(block, ABSENT)
                     )
-
-
-def first_kernel(meta_ref, blocks_ref, left_ref, right_ref,
-                 target_ref, w_ref, start_ref, out_ref, product_ref, residual_ref, grad_ref,
+        if sigma + SLOTS < n_src:
+            copies[sigma + SLOTS].start()
+
+
+def first_kernel(meta_ref, blocks_ref, left_ref, own_ref, other_ref,
+                 target_ref, w_ref, start_ref, right_ref, out_ref, product_ref, residual_ref, grad_ref,
                  *, n_src, n_rcv, slots, edge, per_src, per_rcv):
     src, pair, beta, band = meta_ref[0], meta_ref[2], meta_ref[3], meta_ref[4]
     total = n_src * per_src
@@ -153,6 +171,7 @@
     width = 2 * edge
     per_tile = target_ref.shape[2] // width
     start_ref[...] = left_ref[:, pl.ds(beta, 1)].reshape(start_ref.shape)
+    place(own_ref[...], other_ref[...], beta, right_ref)
     left_b = start_ref[...].astype(bf16)
     for tile in range(tiles):
         rows = slice(tile * per_tile * edge, (tile + 1) * per_tile * edge)
@@ -277,11 +296,12 @@
 
 
 def right_update_kernel(meta_ref, sums_ref, sums_r_ref, target_ref, w_ref, start_ref,
-                        first_grad_ref, right_ref, left_ref, grad_r_ref,
+                        first_grad_ref, right_ref, left_ref, grad_r_ref, own_ref, other_ref,
                         right_out_ref, out_ref, grad_ref, *, edge):
     step = step_of(sums_ref[...])
     step_r = step_of(sums_r_ref[...])
-    right_out_ref[...] = right_ref[...] - step_r * grad_r_ref[...]
+    place(own_ref[...], other_ref[...], meta_ref[3], right_out_ref)
+    right_out_ref[...] = right_out_ref[...] - step_r * grad_r_ref[...]
     start = start_ref[...]
     lefts = [value.astype(bf16) for value in (start, first_grad_ref[...], left_ref[...])]
     for tile in range(w_ref.shape[0]):
@@ -328,21 +348,24 @@
     meta = jnp.stack([src, 2 * pair + beta, pair, beta, band_width[0]]).astype(jnp.int32)
 
     own_right = right_factor.reshape(own_cols, rank2)
-    other_right = lax.ppermute(own_right, "beta", swap)
+    own_short = own_right.astype(bf16)
+    other_short = lax.ppermute(own_short, "beta", swap)
     packed = pl.pallas_call(
         lambda *refs: pack_kernel(*refs, n_src=n_src, n_rcv=n_rcv),
         out_shape=jax.ShapeDtypeStruct((devices, groups, edge, 2 * edge), bf16),
         in_specs=[pl.BlockSpec(memory_space=pltpu.SMEM)] * 2
-        + [pl.BlockSpec(memory_space=pltpu.VMEM)],
+        + [pl.BlockSpec(memory_space=pltpu.HBM)],
         out_specs=pl.BlockSpec(memory_space=pltpu.VMEM),
+        scratch_shapes=[
+            pltpu.VMEM((SLOTS, 2, groups, edge, data.shape[2]), bf16),
+            pltpu.SemaphoreType.DMA((SLOTS,)),
+        ],
         compiler_params=params(),
         name="pack",
-    )(meta, observed, data.reshape(2, groups, n_src, edge, data.shape[2]))
-    right = jnp.concatenate([
-        jnp.where(beta == 0, own_right, other_right),
-        jnp.where(beta == 0, other_right, own_right),
-    ])
-    packed, right = lax.optimization_barrier((packed, right))
+    )(meta, observed, pltpu.with_memory_space_constraint(
+        data.reshape(2, groups, n_src, edge, data.shape[2]), pltpu.HBM
+    ))
+    packed, other_short = lax.optimization_barrier((packed, other_short))
     arrived = lax.all_to_all(packed, everyone, split_axis=0, concat_axis=0, tiled=True)
 
     left_shape = jax.ShapeDtypeStruct((rows, rank2), f32)
@@ -366,7 +389,7 @@
             **kw,
         )
 
-    target, weight, start, parts = call(
+    target, weight, start, right, parts = call(
         lambda *refs: first_kernel(
             *refs, n_src=n_src, n_rcv=n_rcv, slots=slots, edge=edge,
             per_src=per_src, per_rcv=per_rcv,
@@ -376,14 +399,15 @@
             jax.ShapeDtypeStruct((tiles, rows, width), bf16),
             jax.ShapeDtypeStruct((tiles, mids, width), f32),
             left_shape,
+            jax.ShapeDtypeStruct((cols, rank2), bf16),
             left_parts,
         ),
-        3,
+        4,
         scratch_shapes=[
             pltpu.VMEM((rows, width), f32), pltpu.VMEM((rows, width), bf16),
             pltpu.VMEM((rows, rank2), f32),
         ],
-    )(meta, arrived, left_factor.reshape(mids, 2, edge, rank2), right)
+    )(meta, arrived, left_factor.reshape(mids, 2, edge, rank2), own_short, other_short)
 
     def send(parts, axis):
         return lax.all_to_all(
@@ -423,12 +447,19 @@
         "left_update", (left_shape, right_parts), 6,
         scratch_shapes=[pltpu.VMEM((cols, rank2), f32)],
     )(meta, sums, target, weight, start, grad, right)
-    sums_r, grad_r = shared(spread(parts_r, right_group), left_one, False, 2 * n_src)
+    message = spread(parts_r, right_group)
+    message, own_right = lax.optimization_barrier((message, own_right))
+    other_right = lax.ppermute(own_right, "beta", swap)
+    sums_r, grad_r = shared(message, left_one, False, 2 * n_src)
+    sums_r, other_right = lax.optimization_barrier((sums_r, other_right))
     right_one, parts = call(
         lambda *refs: right_update_kernel(*refs, edge=edge),
-        "right_update", (right_shape, left_parts), 9,
+        "right_update", (right_shape, left_parts), 11,
         scratch_shapes=[pltpu.VMEM((rows, rank2), f32)],
-    )(meta, sums, sums_r, target, weight, start, grad, right, left_one, grad_r)
+    )(
+        meta, sums, sums_r, target, weight, start, grad, right, left_one, grad_r,
+        own_right, other_right,
+    )
     sums_two, grad_two, other, other_two = shared_left(parts, right_one, other)
     in_vmem = pl.BlockSpec(memory_space=pltpu.VMEM)
     left_two, left_out, parts_r = pl.pallas_call(

time: 319 us -> 318 us (level)
  local copies, waits for them, and re-layouts: 4.25 us -> 0.87 us
    unnamed x7 -> x5, local copies, waits for them, and re-layouts: 4.16 us -> 0.79 us
  transfers between devices with their start and end apart: 3 -> 4, of which waited for: 1 -> 0; matrix products, arithmetic and copies ran while one was open for 0% -> 0% of each run, Pallas kernels for 2% -> 3%
where the time goes in v7:
time: 318 us; the launch traced here: 317 us
  blocking collectives  275 us (86%)
  Pallas kernels  32.7 us (10%)
  starting transfers between devices  5.16 us (2%)
    all_to_all x1, blocking collectives, per_device(): lax.all_to_all(packed, everyone, split_axis=0, concat_axis=0, tiled=True)  107 us
    all_to_all x8, blocking collectives, send(): lax.all_to_all(parts.astype(jnp.float16), axis, split_axis=0, concat_axis...  103 us
    all_to_all x4, blocking collectives, shared(): lax.all_to_all(sums, everyone, split_axis=0, concat_axis=0, tiled=True)  64.6 us
    pallas_call x1, Pallas kernels, per_device(): pl.pallas_call(lambda *refs: left_again_kernel(*refs, edge=edge), out_sha...  7.85 us
  transfers between devices with their start and end apart: 4, of which 0 were waited for; matrix products, arithmetic and copies ran while one was open for 0% of the time, Pallas kernels for 3%

profile of v7, /device:TPU:1, one launch (start us, length us, event | category | flops | bytes accessed | tf_op | source)
XLA Modules:
  0.0 317.3 jit_solution(9779817256992265389)
XLA Ops:
  0.6 1.0 bitcast_convert_fusion.refs_3_
  1.7 2.1 collective-permute-start
  4.4 0.8 copy.10.refs_1_
  5.2 0.1 stack.19.refs_0_.meta_ref
  5.3 4.9 %pack.1 = bf16[128,4,64,128]{3,2,1,0:T(8,128)(2,1)S(1)} custom-call(s32[5]{0:T(128)S(1)} %stack.19.refs_0_.meta_ref, s32[32,16]{1,0:T(8,128)S(1)} %copy.10.refs_1_, bf16[2,4,8,64,1024]{4,3,2,1,0:T(8,128)(2,1)} %bitcast.45), custom_call_target="tpu_custom_call" | custom-call | tf_op jit(solution)/shard_map/pack/pallas_call | solution.py:353
  10.2 107.3 %all_to_all.92.refs_1_ = bf16[128,4,64,128]{3,2,1,0:T(8,128)(2,1)S(1)} all-to-all(bf16[128,4,64,128]{3,2,1,0:T(8,128)(2,1)S(1)} %pack.1), channel_id=1, replica_groups=mesh['src'=8,'pair'=8,'beta'=2] {'src','pair','beta'}, dimensions={0} | all-to-all | bytes 16777216 | tf_op jit(solution)/shard_map/all_to_all | solution.py:369
  117.5 3.6 %first_gradient.1 = (bf16[6,1024,256]{2,1,0:T(8,128)(2,1)S(1)}, f32[6,16,256]{2,1,0:T(8,128)S(1)}, f32[1024,256]{1,0:T(8,128)S(1)}, bf16[768,256]{1,0:T(8,128)(2,1)S(1)}, f32[8,136,256]{2,1,0:T(8,128)S(1)}) custom-call(s32[5]{0:T(128)S(1)} %stack.19.refs_0_.meta_ref, bf16[128,4,64,128]{3,2,1,0:T(8,128)(2,1)S(1)} %all_to_all.92.refs_1_, ...), custom_call_target="tpu_custom_call" | custom-call | tf_op jit(solution)/shard_map/first_gradient/pallas_call | solution.py:392
  121.1 0.1 convert_element_type.58
  121.2 14.5 %all_to_all.93 = f16[8,136,256]{2,1,0:T(8,128)(2,1)S(1)} all-to-all(f16[8,136,256]{2,1,0:T(8,128)(2,1)S(1)} %convert_element_type.58), channel_id=1, replica_groups=mesh['src'=8,'pair'=8,'beta'=2] {'pair'}, dimensions={0} | all-to-all | bytes 1114112 | tf_op jit(solution)/shard_map/all_to_all | solution.py:413
  135.7 0.1 convert_element_type.59.parts_ref
  135.7 0.4 sum_parts.4
  136.1 0.1 convert_element_type.60
  136.2 13.0 %all_to_all.94 = f16[8,136,256]{2,1,0:T(8,128)(2,1)S(1)} all-to-all(f16[8,136,256]{2,1,0:T(8,128)(2,1)S(1)} %convert_element_type.60), channel_id=1, replica_groups=mesh['src'=8,'pair'=8,'beta'=2] {'pair'}, dimensions={0} | all-to-all | bytes 1114112 | tf_op jit(solution)/shard_map/all_to_all | solution.py:413
  149.2 0.1 convert_element_type.61.refs_0_
  149.3 1.2 left_curve.2
  150.5 16.7 %all_to_all.95 = f32[128,1,128]{2,1,0:T(1,128)S(1)} all-to-all(f32[128,1,128]{2,1,0:T(1,128)S(1)} %bitcast.42), channel_id=1, replica_groups=mesh['src'=8,'pair'=8,'beta'=2] {'src','pair','beta'}, dimensions={0} | all-to-all | bytes 131072 | tf_op jit(solution)/shard_map/all_to_all | solution.py:433
  167.2 4.1 %left_update.1 = (f32[1024,256]{1,0:T(8,128)S(1)}, f32[16,56,256]{2,1,0:T(8,128)S(1)}) custom-call(s32[5]{0:T(128)S(1)} %stack.19.refs_0_.meta_ref, f32[128,128]{1,0:T(8,128)S(1)} %bitcast.34, bf16[6,1024,256]{2,1,0:T(8,128)(2,1)S(1)} %get-tuple-element.40.refs_2_.refs_3_.refs_4_, f32[6,16,256]{2,1,0:T(8,128)S(1)} %get-tuple-element.37.refs_2_.refs_3_.refs_4_.refs_5_, ...), custom_call_target="tpu_custom_call" | custom-call | tf_op jit(solution)/shard_map/left_update/pallas_call | solution.py:445
  171.3 0.1 convert_element_type.62
  171.4 12.4 %all_to_all.96 = f16[16,56,256]{2,1,0:T(8,128)(2,1)S(1)} all-to-all(f16[16,56,256]{2,1,0:T(8,128)(2,1)S(1)} %convert_element_type.62), channel_id=1, replica_groups=mesh['src'=8,'pair'=8,'beta'=2] {'src','beta'}, dimensions={0} | all-to-all | bytes 917504 | tf_op jit(solution)/shard_map/all_to_all | solution.py:413
  183.9 0.3 sum_parts.5
  184.2 0.1 convert_element_type.64
  184.3 12.7 %all_to_all.97 = f16[16,56,256]{2,1,0:T(8,128)(2,1)S(1)} all-to-all(f16[16,56,256]{2,1,0:T(8,128)(2,1)S(1)} %convert_element_type.64), channel_id=1, replica_groups=mesh['src'=8,'pair'=8,'beta'=2] {'src','beta'}, dimensions={0} | all-to-all | bytes 917504 | tf_op jit(solution)/shard_map/all_to_all | solution.py:413
  197.0 1.2 collective-permute-start.2
  198.2 1.2 right_curve.2
  199.4 15.7 %all_to_all.98 = f32[128,1,128]{2,1,0:T(1,128)S(1)} all-to-all(f32[128,1,128]{2,1,0:T(1,128)S(1)} %bitcast.43), channel_id=1, replica_groups=mesh['src'=8,'pair'=8,'beta'=2] {'src','pair','beta'}, dimensions={0} | all-to-all | bytes 131072 | tf_op jit(solution)/shard_map/all_to_all | solution.py:433
  215.1 4.6 %right_update.1 = (f32[768,256]{1,0:T(8,128)S(1)}, f32[8,136,256]{2,1,0:T(8,128)S(1)}) custom-call(s32[5]{0:T(128)S(1)} %stack.19.refs_0_.meta_ref, f32[128,128]{1,0:T(8,128)S(1)} %bitcast.35, f32[128,128]{1,0:T(8,128)S(1)} %bitcast.37, bf16[6,1024,256]{2,1,0:T(8,128)(2,1)S(1)} %get-tuple-element.40.refs_2_.refs_3_.refs_4_, ...), custom_call_target="tpu_custom_call" | custom-call | tf_op jit(solution)/shard_map/right_update/pallas_call | solution.py:455
  219.7 0.1 convert_element_type.66
  219.8 13.4 %all_to_all.99 = f16[8,136,256]{2,1,0:T(8,128)(2,1)S(1)} all-to-all(f16[8,136,256]{2,1,0:T(8,128)(2,1)S(1)} %convert_element_type.66), channel_id=1, replica_groups=mesh['src'=8,'pair'=8,'beta'=2] {'pair'}, dimensions={0} | all-to-all | bytes 1114112 | tf_op jit(solution)/shard_map/all_to_all | solution.py:413
  233.1 0.1 convert_element_type.67.parts_ref
  233.2 0.4 sum_parts.6
  233.6 0.1 convert_element_type.68
  233.7 11.9 %all_to_all.100 = f16[8,136,256]{2,1,0:T(8,128)(2,1)S(1)} all-to-all(f16[8,136,256]{2,1,0:T(8,128)(2,1)S(1)} %convert_element_type.68), channel_id=1, replica_groups=mesh['src'=8,'pair'=8,'beta'=2] {'pair'}, dimensions={0} | all-to-all | bytes 1114112 | tf_op jit(solution)/shard_map/all_to_all | solution.py:413
  245.6 1.9 collective-permute-start.3
  247.5 0.1 convert_element_type.69.refs_0_
  247.6 1.2 left_curve.3
  248.8 15.9 %all_to_all.101 = f32[128,1,128]{2,1,0:T(1,128)S(1)} all-to-all(f32[128,1,128]{2,1,0:T(1,128)S(1)} %bitcast.44), channel_id=1, replica_groups=mesh['src'=8,'pair'=8,'beta'=2] {'src','pair','beta'}, dimensions={0} | all-to-all | bytes 131072 | tf_op jit(solution)/shard_map/all_to_all | solution.py:433
  264.6 0.1 convert_element_type.70.refs_13_
  264.7 0.1 convert_element_type.71.refs_14_
  264.8 7.9 %left_again.1 = (bf16[1024,256]{1,0:T(8,128)(2,1)S(1)}, f32[16,2,64,256]{3,2,1,0:T(8,128)}, f32[16,56,256]{2,1,0:T(8,128)S(1)}) custom-call(s32[5]{0:T(128)S(1)} %stack.19.refs_0_.meta_ref, f32[128,128]{1,0:T(8,128)S(1)} %bitcast.36, f32[128,128]{1,0:T(8,128)S(1)} %bitcast.38, f32[128,128]{1,0:T(8,128)S(1)} %bitcast.39, ...), custom_call_target="tpu_custom_call" | custom-call | tf_op jit(solution)/shard_map/left_again/pallas_call | solution.py:465
  272.7 0.1 convert_element_type.72
  272.8 12.4 %all_to_all.102 = f16[16,56,256]{2,1,0:T(8,128)(2,1)S(1)} all-to-all(f16[16,56,256]{2,1,0:T(8,128)(2,1)S(1)} %convert_element_type.72), channel_id=1, replica_groups=mesh['src'=8,'pair'=8,'beta'=2] {'src','beta'}, dimensions={0} | all-to-all | bytes 917504 | tf_op jit(solution)/shard_map/all_to_all | solution.py:413
  285.2 0.1 convert_element_type.73.parts_ref
  285.2 0.3 sum_parts.7
  285.6 0.1 convert_element_type.74
  285.7 12.5 %all_to_all.103 = f16[16,56,256]{2,1,0:T(8,128)(2,1)S(1)} all-to-all(f16[16,56,256]{2,1,0:T(8,128)(2,1)S(1)} %convert_element_type.74), channel_id=1, replica_groups=mesh['src'=8,'pair'=8,'beta'=2] {'src','beta'}, dimensions={0} | all-to-all | bytes 917504 | tf_op jit(solution)/shard_map/all_to_all | solution.py:413
  298.3 1.2 right_curve.3
  299.5 16.4 %all_to_all.104 = f32[128,1,128]{2,1,0:T(1,128)S(1)} all-to-all(f32[128,1,128]{2,1,0:T(1,128)S(1)} %bitcast.41), channel_id=1, replica_groups=mesh['src'=8,'pair'=8,'beta'=2] {'src','pair','beta'}, dimensions={0} | all-to-all | bytes 131072 | tf_op jit(solution)/shard_map/all_to_all | solution.py:433
  315.8 1.5 right_last.1
  (12 shorter events, 0.2 us)
Async XLA Ops:
  1.7 8.5 %collective-permute-start = (bf16[384,256]{1,0:T(8,128)(2,1)S(1)}, bf16[384,256]{1,0:T(8,128)(2,1)S(1)}, u32[]{:S(2)}, u32[]{:S(2)}) collective-permute-start(bf16[384,256]{1,0:T(8,128)(2,1)S(1)} %bitcast_convert_fusion.refs_3_), channel_id=1, source_target_pairs={{0,1},{1,0},{2,3},{3,2},{4,5},{5,4},{6,7},{7,6},{8,9},{9,8},{10,11... | collective-permute-start | bytes 589832 | tf_op jit(solution)/shard_map/ppermute | solution.py:352
  10.2 107.3 %copy-start = (f32[32,1,64,256]{3,2,1,0:T(8,128)S(1)}, f32[32,1,64,256]{3,2,1,0:T(8,128)}, u32[]{:S(2)}) copy-start(f32[32,1,64,256]{3,2,1,0:T(8,128)} %param.8) | copy-start | bytes 6291460
  149.2 18.0 %collective-permute-start.1 = (f16[8,136,256]{2,1,0:T(8,128)(2,1)S(1)}, f16[8,136,256]{2,1,0:T(8,128)(2,1)S(1)}, u32[]{:S(2)}, u32[]{:S(2)}) collective-permute-start(f16[8,136,256]{2,1,0:T(8,128)(2,1)S(1)} %all_to_all.94), channel_id=1, source_target_pairs={{0,1},{1,0},{2,3},{3,2},{4,5},{5,4},{6,7},{7,6},{8,9},{9,8},{10,11... | collective-permute-start | bytes 1671176 | tf_op jit(solution)/shard_map/ppermute | solution.py:438
  184.2 12.8 %copy-start.1 = (f32[6,1,64,256]{3,2,1,0:T(8,128)S(1)}, f32[6,1,64,256]{3,2,1,0:T(8,128)}, u32[]{:S(2)}) copy-start(f32[6,1,64,256]{3,2,1,0:T(8,128)} %param.9) | copy-start | bytes 1179652
  197.0 18.1 %collective-permute-start.2 = (f32[384,256]{1,0:T(8,128)S(1)}, f32[384,256]{1,0:T(8,128)S(1)}, u32[]{:S(2)}, u32[]{:S(2)}) collective-permute-start(f32[384,256]{1,0:T(8,128)S(1)} %bitcast.32), channel_id=1, source_target_pairs={{0,1},{1,0},{2,3},{3,2},{4,5},{5,4},{6,7},{7,6},{8,9},{9,8},{10,11... | collective-permute-start | bytes 1179656 | tf_op jit(solution)/shard_map/ppermute | solution.py:452
  245.6 19.0 %collective-permute-start.3 = (f16[8,136,256]{2,1,0:T(8,128)(2,1)S(1)}, f16[8,136,256]{2,1,0:T(8,128)(2,1)S(1)}, u32[]{:S(2)}, u32[]{:S(2)}) collective-permute-start(f16[8,136,256]{2,1,0:T(8,128)(2,1)S(1)} %all_to_all.100), channel_id=1, source_target_pairs={{0,1},{1,0},{2,3},{3,2},{4,5},{5,4},{6,7},{7,6},{8,9},{9,8},{10,11... | collective-permute-start | bytes 1671176 | tf_op jit(solution)/shard_map/ppermute | solution.py:438
